TPU v7x, 32 devices: a whole 2x2x4 slice. The times are simulated.
32 devices in a mesh: fsdp: 8 (over z, y), ctx: 4 (over x, core).
Axes of the slice: x: 2, y: 2, z: 4, core: 2. Of those that a mesh axis runs over, the one named last changes fastest.
Arguments:
- hidden: bfloat16 [8, 1024, 8192], P('fsdp', 'ctx'), may hold values from -400 to 400
- norm_gain: bfloat16 [8192], replicated, may hold values from 0.099609375 to 1.8984375
- w_query: bfloat16 [8192, 1024], P('fsdp'), may hold values from -0.109375 to 0.109375
- w_key: bfloat16 [8192, 128], P('fsdp'), may hold values from -0.109375 to 0.109375
- w_value: bfloat16 [8192, 128], P('fsdp'), may hold values from -0.0625 to 0.0625
- bias_query: bfloat16 [1024], replicated, may hold values from -24 to 24
- bias_key: bfloat16 [128], replicated, may hold values from -9 to 9
- bias_value: bfloat16 [128], replicated, may hold values from -3 to 3
Outputs:
- attended: bfloat16 [8, 1024, 1024], P('fsdp', 'ctx')
All inputs are finite; a program needn't handle non-finite values.
Results may differ from a plain program's by a relative error of at most 0.012.
Values may be sent and summed in bfloat16 or wider, within the bound.
No kernel may reach another device: no remote copies, remote signals or barrier semaphores. Data moves between devices by JAX's collectives and lax.ppermute only.
A program may use at most 128 MiB of HBM per device.

v0:
```python
import math

import jax
import jax.numpy as jnp
from jax import lax
from jax.sharding import PartitionSpec as P

epsilon = 1e-06
rotary_base = 1000000.0
masked_score = -1e30


def shifted(value, axis, steps):
    count = lax.axis_size(axis)
    first, last = (max(0, -steps), min(count, count - steps))
    return lax.ppermute(value, axis, [(source, source + steps) for source in range(first, last)])


def rotary_tables(positions, head_width):
    half_width = head_width // 2
    frequency = jnp.exp(
        -(jnp.arange(half_width, dtype=jnp.float32) * (2.0 / head_width)) * math.log(rotary_base)
    )
    angles = positions.astype(jnp.float32)[:, None] * frequency[None, :]
    return (jnp.cos(angles)[:, None, :], jnp.sin(angles)[:, None, :])


def rotate(tensor, cosine, sine_table):
    half_width = tensor.shape[-1] // 2
    lower_half = tensor[..., :half_width]
    upper_half = tensor[..., half_width:]
    return jnp.concatenate(
        [
            lower_half * cosine - upper_half * sine_table,
            upper_half * cosine + lower_half * sine_table,
        ],
        axis=-1,
    )


def normalize(inputs, norm_gain):
    floats = inputs.astype(jnp.float32)
    scaled = floats * lax.rsqrt(jnp.mean(floats * floats, axis=-1, keepdims=True) + epsilon)
    return (scaled * norm_gain.astype(jnp.float32)).astype(jnp.bfloat16)


def contract_rows(operand, pieces):
    return tuple((jnp.dot(operand, piece, preferred_element_type=jnp.float32) for piece in pieces))


def attend(work_queries, score_scale, running, key_value, visible):
    row_peak, row_total, weighted = running
    scores = (
        jnp.einsum("qhd,kd->hqk", work_queries, key_value[0], preferred_element_type=jnp.float32)
        * score_scale
    )
    scores = jnp.where(visible, scores, masked_score)
    new_peak = jnp.maximum(row_peak, jnp.max(scores, axis=-1))
    factor = jnp.exp(row_peak - new_peak)
    expsum = jnp.exp(scores - new_peak[..., None])
    row_total = row_total * factor + jnp.sum(expsum, axis=-1)
    weights = expsum.astype(jnp.bfloat16)
    weighted = weighted * factor[..., None] + jnp.einsum(
        "hqk,kd->hqd", weights, key_value[1], preferred_element_type=jnp.float32
    )
    return (new_peak, row_total, weighted)


def shards(hidden, norm_gain, w_query, w_key, w_value, bias_query, bias_key, bias_value):
    local_rows = hidden.shape[1]
    head_width = w_key.shape[1]
    query_width = w_query.shape[1]
    query_heads = query_width // head_width
    normed = normalize(hidden[0], norm_gain)
    sums = contract_rows(
        normed,
        (
            lax.all_gather(w_query, "fsdp", axis=0, tiled=True),
            lax.all_gather(w_key, "fsdp", axis=0, tiled=True),
            lax.all_gather(w_value, "fsdp", axis=0, tiled=True),
        ),
    )
    query_sums, key_sums, value_sums = sums
    slab_index = lax.axis_index("ctx")
    slab_count = lax.axis_size("ctx")
    positions = slab_index * local_rows + jnp.arange(local_rows, dtype=jnp.int32)
    cosine, sine_table = rotary_tables(positions, head_width)
    queries = rotate(
        (query_sums + bias_query.astype(jnp.float32)).reshape(local_rows, query_heads, head_width),
        cosine,
        sine_table,
    ).astype(jnp.bfloat16)
    keys = rotate((key_sums + bias_key.astype(jnp.float32))[:, None, :], cosine, sine_table)[
        :, 0, :
    ].astype(jnp.bfloat16)
    values = (value_sums + bias_value.astype(jnp.float32)).astype(jnp.bfloat16)
    score_scale = head_width ** (-0.5)
    start_state = (
        jnp.full((query_heads, local_rows), masked_score, jnp.float32),
        jnp.zeros((query_heads, local_rows), jnp.float32),
        jnp.zeros((query_heads, local_rows, head_width), jnp.float32),
    )
    key_value = jnp.stack([keys, values])
    column_ids = jnp.arange(local_rows, dtype=jnp.int32)
    causal = column_ids[None, :] <= column_ids[:, None]
    running = attend(queries, score_scale, start_state, key_value, causal[None])

    def forward_step(step_number, state):
        held_running, blocks = state
        blocks = shifted(blocks, "ctx", 1)
        visible = step_number <= slab_index
        held_running = attend(queries, score_scale, held_running, blocks, visible)
        return (held_running, blocks)

    running, key_value = lax.fori_loop(1, slab_count, forward_step, (running, key_value))
    row_peak, row_total, weighted = running
    attended = (
        (weighted / row_total[..., None])
        .transpose(1, 0, 2)
        .reshape(local_rows, query_width)
        .astype(jnp.bfloat16)
    )
    return attended[None]


def solution(mesh):
    in_specs = (
        P("fsdp", "ctx", None),
        P(),
        P("fsdp", None),
        P("fsdp", None),
        P("fsdp", None),
        P(),
        P(),
        P(),
    )
    out_specs = P("fsdp", "ctx", None)
    return jax.shard_map(shards, mesh=mesh, in_specs=in_specs, out_specs=out_specs, check_vma=False)
```

profile of v0, /device:TPU:11, one launch (start us, length us, event | category | flops | bytes accessed | tf_op | source)
XLA Modules:
  0.0 379.1 jit_solution(6353027936937991859)
XLA Ops:
  6.5 0.0 copy-start
  6.5 0.0 copy-start.1
  6.5 0.0 all-gather.4.cloned.1.call-start
  6.6 0.7 all-gather.4.cloned.1.call-update
  7.3 0.0 all-gather.8.cloned.1.call-start
  7.3 0.7 all-gather.8.cloned.1.call-update
  8.0 0.0 all-gather.6.cloned.1.call-start
  8.1 0.7 all-gather.6.cloned.1.call-update
  8.8 0.0 copy-done
  8.8 0.0 copy-done.1
  8.8 0.0 copy-done.2
  8.8 0.0 copy-done.3
  8.9 3.1 fusion.11
  12.0 0.5 multiply_cosine_fusion
  12.6 46.5 %all-gather.4.cloned.1.call-done = bf16[8192,128]{1,0:T(8,128)(2,1)} async-done(((bf16[1024,128]{1,0:T(8,128)(2,1)}), bf16[8192,128]{1,0:T(8,128)(2,1)}) %all-gather.4.cloned.1.call-update) | async-done | bytes 2097168 | tf_op jit(solution)/shard_map/all_gather | solution.py:79
  59.1 4.6 %fusion.17 = f32[256,1,128]{0,2,1:T(8,128)S(1)} fusion(bf16[8192,128]{1,0:T(8,128)(2,1)} %all-gather.4.cloned.1.call-done, f32[128]{0:T(128)S(1)} %convert_element_type.78, bf16[1,256,8192]{2,1,0:T(8,128)(2,1)} %param.10, f32[8192]{0:T(1024)S(1)} %convert_element_type.76, f32[256]{0:T(256)S(1)} %add_rsqrt_fusion), kind=kOutput, calls=%fused_computation.32 | convolution fusion | flops 545292288 | bytes 6456832 | tf_op jit(solution)/shard_map/dot_general | solution.py:48
  63.7 0.3 fusion.26
  64.1 45.0 %all-gather.8.cloned.1.call-done = bf16[8192,128]{1,0:T(8,128)(2,1)} async-done(((bf16[1024,128]{1,0:T(8,128)(2,1)}), bf16[8192,128]{1,0:T(8,128)(2,1)}) %all-gather.8.cloned.1.call-update) | async-done | bytes 2097168 | tf_op jit(solution)/shard_map/all_gather | solution.py:80
  109.0 4.6 %fusion.18 = bf16[256,128]{0,1:T(8,128)(2,1)S(1)} fusion(bf16[8192,128]{1,0:T(8,128)(2,1)} %all-gather.8.cloned.1.call-done, f32[128]{0:T(128)S(1)} %convert_element_type.84, bf16[1,256,8192]{2,1,0:T(8,128)(2,1)} %param.10, f32[8192]{0:T(1024)S(1)} %convert_element_type.76, f32[256]{0:T(256)S(1)} %add_rsqrt_fusion), kind=kOutput, calls=%fused_computation.33 | convolution fusion | flops 545325056 | bytes 6391296 | tf_op jit(solution)/shard_map/dot_general | solution.py:48
  113.7 0.1 copy.16
  113.8 222.1 %all-gather.6.cloned.1.call-done = bf16[8192,1024]{1,0:T(8,128)(2,1)} async-done(((bf16[1024,1024]{1,0:T(8,128)(2,1)}), bf16[8192,1024]{1,0:T(8,128)(2,1)}) %all-gather.6.cloned.1.call-update) | async-done | bytes 16777232 | tf_op jit(solution)/shard_map/all_gather | solution.py:78
  335.9 9.6 %fusion.16 = f32[32,8,8,128]{3,1,2,0:T(8,128)S(1)} fusion(bf16[8192,1024]{1,0:T(8,128)(2,1)} %all-gather.6.cloned.1.call-done, f32[1024]{0:T(1024)S(1)} %convert_element_type.82, bf16[1,256,8192]{2,1,0:T(8,128)(2,1)} %param.10, f32[8192]{0:T(1024)S(1)} %convert_element_type.76, f32[256]{0:T(256)S(1)} %add_rsqrt_fusion), kind=kOutput, calls=%fused_computation.28 | convolution fusion | flops 4303618048 | bytes 22057984 | tf_op jit(solution)/shard_map/dot_general | solution.py:48
  345.5 0.2 copy.27
  345.7 0.3 fusion.36
  346.0 0.4 subtract_convert_fusion
  346.4 0.3 pad_maximum_fusion
  346.7 0.5 fusion.37
  347.2 0.3 fusion.15
  347.6 0.8 convolution_add_fusion.2
  348.4 22.5 %while.19 = (s32[]{:T(128)}, f32[8,256]{1,0:T(8,128)S(1)}, f32[8,256]{1,0:T(8,128)S(1)}, f32[8,256,128]{2,1,0:T(8,128)S(1)}, bf16[2,256,128]{2,1,0:T(8,128)(2,1)...) while((s32[]{:T(128)}, f32[8,256]{1,0:T(8,128)S(1)}, f32[8,256]{1,0:T(8,128)S(1)}, ...), condition=%wide.region_6.7_spmd, body=%wide.region_3.6_spmd.sunk | while | flops 274731008 | bytes 9961609 | solution.py:115
  348.4 1.3 collective-permute-start
  349.7 2.5 collective-permute-done
  352.2 0.4 bitcast_reduce_fusion.2
  352.7 0.4 fusion.48
  353.1 1.0 convolution_add_fusion.6
  354.2 1.3 collective-permute-start
  355.5 5.0 %collective-permute-done = bf16[2,256,128]{2,1,0:T(8,128)(2,1)S(1)} collective-permute-done((bf16[2,256,128]{2,1,0:T(8,128)(2,1)S(1)}, bf16[2,256,128]{2,1,0:T(8,128)(2,1)S(1)}, u32[]{:S(2)}, u32[]{:S(2)}) %collective-permute-start) | collective-permute-done | bytes 131104 | tf_op jit(solution)/shard_map/while/body/eval_jaxpr/ppermute | solution.py:16
  360.5 0.4 bitcast_reduce_fusion.2
  361.0 0.4 fusion.48
  361.5 1.0 convolution_add_fusion.6
  362.5 1.3 collective-permute-start
  363.8 5.0 %collective-permute-done = bf16[2,256,128]{2,1,0:T(8,128)(2,1)S(1)} collective-permute-done((bf16[2,256,128]{2,1,0:T(8,128)(2,1)S(1)}, bf16[2,256,128]{2,1,0:T(8,128)(2,1)S(1)}, u32[]{:S(2)}, u32[]{:S(2)}) %collective-permute-start) | collective-permute-done | bytes 131104 | tf_op jit(solution)/shard_map/while/body/eval_jaxpr/ppermute | solution.py:16
  368.8 0.4 bitcast_reduce_fusion.2
  369.3 0.4 fusion.48
  369.8 1.0 convolution_add_fusion.6
  370.8 0.3 fusion.21
  371.2 0.3 copy.17
  371.5 1.0 convert_element_type.89
  (26 shorter events, 0.2 us)
Async XLA Ops:
  6.5 2.2 copy-start
  6.5 2.2 copy-start.1
  6.5 2.3 copy-start.2
  6.5 2.3 copy-start.3
  6.5 52.6 %all-gather.4.cloned.1.call-start = ((), (), s32[]{:S(2)}) async-start(), calls=%async_computation | async-start | bytes 2359296 | tf_op jit(solution)/shard_map/all_gather | solution.py:79
  7.3 101.8 %all-gather.8.cloned.1.call-start = ((), (), s32[]{:S(2)}) async-start(), calls=%async_computation.2 | async-start | bytes 2359296 | tf_op jit(solution)/shard_map/all_gather | solution.py:80
  8.0 327.9 %all-gather.6.cloned.1.call-start = ((), (), s32[]{:S(2)}) async-start(), calls=%async_computation.1 | async-start | bytes 18874368 | tf_op jit(solution)/shard_map/all_gather | solution.py:78
  348.4 3.8 %collective-permute-start = (bf16[2,256,128]{2,1,0:T(8,128)(2,1)S(1)}, bf16[2,256,128]{2,1,0:T(8,128)(2,1)S(1)}, u32[]{:S(2)}, u32[]{:S(2)}) collective-permute-start(bf16[2,256,128]{2,1,0:T(8,128)(2,1)S(1)} %get-tuple-element.232), channel_id=1, source_target_pairs={{0,1},{1,2},{2,3},{4,5},{5,6},{6,7},{8,9},{9,10},{10,11},{12,13},{... | collective-permute-start | bytes 393224 | tf_op jit(solution)/shard_map/while/body/eval_jaxpr/ppermute | solution.py:16
  354.2 6.3 %collective-permute-start = (bf16[2,256,128]{2,1,0:T(8,128)(2,1)S(1)}, bf16[2,256,128]{2,1,0:T(8,128)(2,1)S(1)}, u32[]{:S(2)}, u32[]{:S(2)}) collective-permute-start(bf16[2,256,128]{2,1,0:T(8,128)(2,1)S(1)} %get-tuple-element.232), channel_id=1, source_target_pairs={{0,1},{1,2},{2,3},{4,5},{5,6},{6,7},{8,9},{9,10},{10,11},{12,13},{... | collective-permute-start | bytes 393224 | tf_op jit(solution)/shard_map/while/body/eval_jaxpr/ppermute | solution.py:16
  362.5 6.3 %collective-permute-start = (bf16[2,256,128]{2,1,0:T(8,128)(2,1)S(1)}, bf16[2,256,128]{2,1,0:T(8,128)(2,1)S(1)}, u32[]{:S(2)}, u32[]{:S(2)}) collective-permute-start(bf16[2,256,128]{2,1,0:T(8,128)(2,1)S(1)} %get-tuple-element.232), channel_id=1, source_target_pairs={{0,1},{1,2},{2,3},{4,5},{5,6},{6,7},{8,9},{9,10},{10,11},{12,13},{... | collective-permute-start | bytes 393224 | tf_op jit(solution)/shard_map/while/body/eval_jaxpr/ppermute | solution.py:16
Sparse Core Ops, SparseCore 0:
  9.5 49.5 all-gather.3
  61.2 47.7 all-gather.7
  111.2 224.6 all-gather.5
where the time goes:
time: 384 us; the launch traced here: 379 us
  waiting for transfers between devices  328 us (85%)
  matrix products  24.5 us (6%)
  between operations  13.3 us (3%)
  other arithmetic  6.76 us (2%)
  starting transfers between devices  3.99 us (1%)
    all_gather x1, waiting for transfers between devices, shards(): lax.all_gather(w_query, 'fsdp', axis=0, tiled=True)  222 us
    all_gather x1, waiting for transfers between devices, shards(): lax.all_gather(w_key, 'fsdp', axis=0, tiled=True)  46.5 us
    all_gather x1, waiting for transfers between devices, shards(): lax.all_gather(w_value, 'fsdp', axis=0, tiled=True)  45 us
    dot_general x3, matrix products, contract_rows(): jnp.dot(operand, piece, preferred_element_type=jnp.float32)  18.8 us
    ppermute x3, waiting for transfers between devices, shifted(): lax.ppermute(value, axis, [(source, source + steps) for source in range(f...  12.5 us
  transfers between devices with their start and end apart: 6, of which 6 were waited for; matrix products, arithmetic and copies ran while one was open for 4% of the time, Pallas kernels for 0%

commit v1 on v0

--- a/solution.py
+++ b/solution.py
@@ -3,7 +3,7 @@
 import jax
 import jax.numpy as jnp
 from jax import lax
-from jax.sharding import PartitionSpec as P
+from jax.sharding import Mesh, PartitionSpec as P
 
 epsilon = 1e-06
 rotary_base = 1000000.0
@@ -38,16 +38,6 @@
     )
 
 
-def normalize(inputs, norm_gain):
-    floats = inputs.astype(jnp.float32)
-    scaled = floats * lax.rsqrt(jnp.mean(floats * floats, axis=-1, keepdims=True) + epsilon)
-    return (scaled * norm_gain.astype(jnp.float32)).astype(jnp.bfloat16)
-
-
-def contract_rows(operand, pieces):
-    return tuple((jnp.dot(operand, piece, preferred_element_type=jnp.float32) for piece in pieces))
-
-
 def attend(work_queries, score_scale, running, key_value, visible):
     row_peak, row_total, weighted = running
     scores = (
@@ -66,21 +56,56 @@
     return (new_peak, row_total, weighted)
 
 
+def row_scale(inputs):
+    floats = inputs.astype(jnp.float32)
+    return lax.rsqrt(jnp.mean(floats * floats, axis=-1, keepdims=True) + epsilon)
+
+
+def scaled_rows(inputs, scale, gain):
+    return (inputs.astype(jnp.float32) * scale * gain.astype(jnp.float32)).astype(jnp.bfloat16)
+
+
+def project(hidden, norm_gain, w_query, w_key, w_value):
+    local_rows, width = hidden.shape
+    lines, slabs = (lax.axis_size("line"), lax.axis_size("ctx"))
+    depth = w_query.shape[0]
+    side = lax.axis_index("pair")
+    swap = [(0, 1), (1, 0)]
+    split = hidden.reshape(local_rows, lines, 2, depth)
+    half_width = lines * depth
+
+    def half(array, which):
+        return lax.dynamic_index_in_dim(array, which, array.ndim - 2, keepdims=False)
+
+    sent = half(split, 1 - side).reshape(local_rows, half_width)
+    kept = half(split, side).reshape(local_rows, half_width)
+    gain = half(norm_gain.reshape(lines, 2, depth), side).reshape(half_width)
+    came = lax.ppermute(sent, "pair", swap)
+    scale = row_scale(hidden)
+    came_scale = lax.ppermute(scale, "pair", swap)
+    piece = depth // slabs
+    start = lax.axis_index("ctx") * piece
+    packed = jnp.concatenate(
+        [lax.dynamic_slice_in_dim(w, start, piece, 0) for w in (w_query, w_key, w_value)], axis=1
+    )
+    weights = lax.all_gather(packed, ("line", "ctx"), axis=0, tiled=True)
+    rows = jnp.concatenate(
+        [scaled_rows(kept, scale, gain), scaled_rows(came, came_scale, gain)], axis=0
+    )
+    sums = jnp.dot(rows, weights, preferred_element_type=jnp.float32)
+    back = lax.ppermute(sums[local_rows:].astype(jnp.bfloat16), "pair", swap)
+    return sums[:local_rows] + back.astype(jnp.float32)
+
+
 def shards(hidden, norm_gain, w_query, w_key, w_value, bias_query, bias_key, bias_value):
     local_rows = hidden.shape[1]
     head_width = w_key.shape[1]
     query_width = w_query.shape[1]
     query_heads = query_width // head_width
-    normed = normalize(hidden[0], norm_gain)
-    sums = contract_rows(
-        normed,
-        (
-            lax.all_gather(w_query, "fsdp", axis=0, tiled=True),
-            lax.all_gather(w_key, "fsdp", axis=0, tiled=True),
-            lax.all_gather(w_value, "fsdp", axis=0, tiled=True),
-        ),
-    )
-    query_sums, key_sums, value_sums = sums
+    sums = project(hidden[0], norm_gain, w_query, w_key, w_value)
+    query_sums = sums[:, :query_width]
+    key_sums = sums[:, query_width : query_width + head_width]
+    value_sums = sums[:, query_width + head_width :]
     slab_index = lax.axis_index("ctx")
     slab_count = lax.axis_size("ctx")
     positions = slab_index * local_rows + jnp.arange(local_rows, dtype=jnp.int32)
@@ -124,15 +149,18 @@
 
 
 def solution(mesh):
+    groups, slabs = (mesh.shape["fsdp"], mesh.shape["ctx"])
+    pairs = Mesh(mesh.devices.reshape(groups // 2, 2, slabs), ("line", "pair", "ctx"))
+    both = ("line", "pair")
     in_specs = (
-        P("fsdp", "ctx", None),
+        P(both, "ctx", None),
         P(),
-        P("fsdp", None),
-        P("fsdp", None),
-        P("fsdp", None),
+        P(both, None),
+        P(both, None),
+        P(both, None),
         P(),
         P(),
         P(),
     )
-    out_specs = P("fsdp", "ctx", None)
-    return jax.shard_map(shards, mesh=mesh, in_specs=in_specs, out_specs=out_specs, check_vma=False)
+    out_specs = P(both, "ctx", None)
+    return jax.shard_map(shards, mesh=pairs, in_specs=in_specs, out_specs=out_specs, check_vma=False)

time: 384 us -> 168 us (0.44)
  the two profiles are of different devices: /device:TPU:11 before, /device:TPU:1 now
where the time goes in v1:
time: 168 us; the launch traced here: 167 us
  waiting for transfers between devices  92.3 us (55%)
  matrix products  19.4 us (12%)
  local copies, waits for them, and re-layouts  16.4 us (10%)
  starting transfers between devices  15.2 us (9%)
  between operations  13.6 us (8%)
  other arithmetic  10.1 us (6%)
    ppermute x1, waiting for transfers between devices, project(): came_scale = lax.ppermute(scale, 'pair', swap)  44.6 us
    all_gather x1, waiting for transfers between devices, project(): weights = lax.all_gather(packed, ('line', 'ctx'), axis=0, tiled=True)  27.7 us
    ppermute x1, waiting for transfers between devices, project(): back = lax.ppermute(sums[local_rows:].astype(jnp.bfloat16), 'pair', swap)  14.3 us
    ppermute x3, starting transfers between devices, shifted(): lax.ppermute(value, axis, [(source, source + steps) for source in range(f...  11.8 us
    dot_general x1, matrix products, project(): sums = jnp.dot(rows, weights, preferred_element_type=jnp.float32)  10.6 us
    unnamed x16, local copies, waits for them, and re-layouts  8.96 us
    ppermute x3, waiting for transfers between devices, shifted(): lax.ppermute(value, axis, [(source, source + steps) for source in range(f...  5.76 us
    dot_general x4, matrix products, attend(): jnp.einsum('qhd,kd->hqk', work_queries, key_value[0], preferred_element_t...  4.99 us
  transfers between devices with their start and end apart: 7, of which 6 were waited for; matrix products, arithmetic and copies ran while one was open for 10% of the time, Pallas kernels for 0%

profile of v1, /device:TPU:1, one launch (start us, length us, event | category | flops | bytes accessed | tf_op | source)
XLA Modules:
  0.0 167.4 jit_solution(3614708173990688279)
XLA Ops:
  6.5 1.6 copy-done
  8.2 0.9 constant_dynamic-slice_fusion
  9.1 0.9 pad_maximum_fusion
  10.0 0.0 all-gather.2.cloned.1.call-update
  10.0 6.4 %copy.20 = bf16[1,256,8192]{1,2,0:T(8,128)(2,1)} copy(bf16[1,256,8192]{2,1,0:T(8,128)(2,1)} %param.10) | data formatting | bytes 8388608 | tf_op args[0]
  16.3 4.7 %constant_dynamic-slice_fusion.4 = (bf16[256,4,1,1024]{0,3,2,1:T(8,128)(2,1)}, bf16[256,4,1,1024]{0,3,2,1:T(8,128)(2,1)}) fusion(bf16[256,4,2,1024]{0,3,2,1:T(8,128)(2,1)} %bitcast.65, s32[]{:T(128)S(6)} %select_n.37, s32[]{:T(128)S(6)} %select_n.38), kind=kLoop, calls=%fused_computation.70 | loop fusion | bytes 8388616 | tf_op jit(solution)/shard_map/jit(dynamic_index_in_dim)/dynamic_slice | solution.py:78
  21.0 2.1 %collective-permute-start.1 = (bf16[256,4096]{0,1:T(8,128)(2,1)}, bf16[256,4096]{0,1:T(8,128)(2,1)}, u32[]{:S(2)}, u32[]{:S(2)}) collective-permute-start(bf16[256,4096]{0,1:T(8,128)(2,1)} %bitcast.8), channel_id=1, source_target_pairs={{0,4},{4,0},{1,5},{5,1},{2,6},{6,2},{3,7},{7,3},{8,12},{12,8},{9,1... | collective-permute-start | bytes 6291464 | tf_op jit(solution)/shard_map/ppermute | solution.py:83
  23.1 0.9 multiply_reduce_fusion
  24.0 0.1 collective-permute-start.2
  24.2 44.6 %collective-permute-done.2 = f32[256,1]{0,1:T(1,128)S(1)} collective-permute-done((f32[256,1]{0,1:T(1,128)S(1)}, f32[256,1]{0,1:T(1,128)S(1)}, u32[]{:S(2)}, u32[]{:S(2)}) %collective-permute-start.2) | collective-permute-done | bytes 1056 | tf_op jit(solution)/shard_map/ppermute | solution.py:85
  68.8 4.0 %fusion.16 = (bf16[256,4096]{0,1:T(8,128)(2,1)}, bf16[256,4096]{0,1:T(8,128)(2,1)}) fusion(bf16[256,4,1,1024]{0,3,2,1:T(8,128)(2,1)} %get-tuple-element.150, f32[4096]{0:T(1024)S(1)} %bitcast.67, f32[256]{0:T(256)S(1)} %add_rsqrt_fusion, f32[256]{0:T(256)S(1)} %bitcast.69, bf16[256,4096]{0,1:T(8,128)(2,1)} %collective-permute-done.1), kind=kLoop, calls=%fused_computation.25 | loop fusion | flops 8388608 | bytes 8407040 | tf_op jit(solution)/shard_map/convert_element_type | solution.py:65
  72.8 27.7 %all-gather.2.cloned.1.call-done = bf16[4096,1280]{1,0:T(8,128)(2,1)} async-done(((bf16[256,1280]{1,0:T(8,128)(2,1)}), bf16[4096,1280]{1,0:T(8,128)(2,1)}) %all-gather.2.cloned.1.call-update) | async-done | bytes 10485776 | tf_op jit(solution)/shard_map/all_gather | solution.py:91
  100.5 10.6 %fusion.11 = f32[512,1280]{1,0:T(8,128)S(1)} fusion(bf16[4096,1280]{1,0:T(8,128)(2,1)} %all-gather.2.cloned.1.call-done, bf16[256,4096]{0,1:T(8,128)(2,1)} %get-tuple-element.161, bf16[256,4096]{0,1:T(8,128)(2,1)} %get-tuple-element.160), kind=kOutput, calls=%fused_computation.19 | convolution fusion | flops 5377097728 | bytes 17301504 | tf_op jit(solution)/shard_map/dot_general | solution.py:95
  111.2 0.1 slice.86
  111.2 1.3 collective-permute-start.3
  112.6 0.5 multiply_cosine_fusion
  113.1 14.3 %collective-permute-done.3 = bf16[256,1280]{1,0:T(8,128)(2,1)S(1)} collective-permute-done((bf16[256,1280]{1,0:T(8,128)(2,1)S(1)}, bf16[256,1280]{1,0:T(8,128)(2,1)S(1)}, u32[]{:S(2)}, u32[]{:S(2)}) %collective-permute-start.3) | collective-permute-done | bytes 655392 | tf_op jit(solution)/shard_map/ppermute | solution.py:96
  127.4 0.1 slice_add_fusion
  127.6 0.6 fusion.27
  128.1 0.1 fusion.20
  128.3 0.2 copy.29
  128.5 0.3 fusion.37
  128.8 0.1 fusion.39
  128.9 0.4 subtract_convert_fusion
  129.3 0.3 pad_maximum_fusion.1
  129.6 0.8 copy-done.1
  130.4 0.5 fusion.38
  131.0 0.3 fusion.18
  131.3 0.7 convolution_add_fusion.1
  132.0 26.8 %while.19 = (s32[]{:T(128)}, f32[8,256]{1,0:T(8,128)S(1)}, f32[8,256]{1,0:T(8,128)S(1)}, f32[8,256,128]{2,1,0:T(8,128)S(1)}, bf16[2,256,128]{2,1,0:T(8,128)(2,1)...) while((s32[]{:T(128)}, f32[8,256]{1,0:T(8,128)S(1)}, f32[8,256]{1,0:T(8,128)S(1)}, ...), condition=%wide.region_6.7_spmd, body=%wide.region_3.6_spmd.sunk | while | flops 274731008 | bytes 9961609 | solution.py:140
  132.0 3.1 %collective-permute-start = (bf16[2,256,128]{2,1,0:T(8,128)(2,1)S(1)}, bf16[2,256,128]{2,1,0:T(8,128)(2,1)S(1)}, u32[]{:S(2)}, u32[]{:S(2)}) collective-permute-start(bf16[2,256,128]{2,1,0:T(8,128)(2,1)S(1)} %get-tuple-element.233), channel_id=1, source_target_pairs={{0,1},{1,2},{2,3},{4,5},{5,6},{6,7},{8,9},{9,10},{10,11},{12,13},{... | collective-permute-start | bytes 393224 | tf_op jit(solution)/shard_map/while/body/eval_jaxpr/ppermute | solution.py:16
  135.1 1.9 %collective-permute-done = bf16[2,256,128]{2,1,0:T(8,128)(2,1)S(1)} collective-permute-done((bf16[2,256,128]{2,1,0:T(8,128)(2,1)S(1)}, bf16[2,256,128]{2,1,0:T(8,128)(2,1)S(1)}, u32[]{:S(2)}, u32[]{:S(2)}) %collective-permute-start) | collective-permute-done | bytes 131104 | tf_op jit(solution)/shard_map/while/body/eval_jaxpr/ppermute | solution.py:16
  137.1 1.5 bitcast_reduce_fusion.2
  138.6 0.4 fusion.48
  139.1 1.0 convolution_add_fusion.3
  140.1 4.3 %collective-permute-start = (bf16[2,256,128]{2,1,0:T(8,128)(2,1)S(1)}, bf16[2,256,128]{2,1,0:T(8,128)(2,1)S(1)}, u32[]{:S(2)}, u32[]{:S(2)}) collective-permute-start(bf16[2,256,128]{2,1,0:T(8,128)(2,1)S(1)} %get-tuple-element.233), channel_id=1, source_target_pairs={{0,1},{1,2},{2,3},{4,5},{5,6},{6,7},{8,9},{9,10},{10,11},{12,13},{... | collective-permute-start | bytes 393224 | tf_op jit(solution)/shard_map/while/body/eval_jaxpr/ppermute | solution.py:16
  144.5 1.9 %collective-permute-done = bf16[2,256,128]{2,1,0:T(8,128)(2,1)S(1)} collective-permute-done((bf16[2,256,128]{2,1,0:T(8,128)(2,1)S(1)}, bf16[2,256,128]{2,1,0:T(8,128)(2,1)S(1)}, u32[]{:S(2)}, u32[]{:S(2)}) %collective-permute-start) | collective-permute-done | bytes 131104 | tf_op jit(solution)/shard_map/while/body/eval_jaxpr/ppermute | solution.py:16
  146.4 1.5 bitcast_reduce_fusion.2
  147.9 0.4 fusion.48
  148.4 1.0 convolution_add_fusion.3
  149.5 4.4 %collective-permute-start = (bf16[2,256,128]{2,1,0:T(8,128)(2,1)S(1)}, bf16[2,256,128]{2,1,0:T(8,128)(2,1)S(1)}, u32[]{:S(2)}, u32[]{:S(2)}) collective-permute-start(bf16[2,256,128]{2,1,0:T(8,128)(2,1)S(1)} %get-tuple-element.233), channel_id=1, source_target_pairs={{0,1},{1,2},{2,3},{4,5},{5,6},{6,7},{8,9},{9,10},{10,11},{12,13},{... | collective-permute-start | bytes 393224 | tf_op jit(solution)/shard_map/while/body/eval_jaxpr/ppermute | solution.py:16
  153.8 1.9 %collective-permute-done = bf16[2,256,128]{2,1,0:T(8,128)(2,1)S(1)} collective-permute-done((bf16[2,256,128]{2,1,0:T(8,128)(2,1)S(1)}, bf16[2,256,128]{2,1,0:T(8,128)(2,1)S(1)}, u32[]{:S(2)}, u32[]{:S(2)}) %collective-permute-start) | collective-permute-done | bytes 131104 | tf_op jit(solution)/shard_map/while/body/eval_jaxpr/ppermute | solution.py:16
  155.8 1.5 bitcast_reduce_fusion.2
  157.3 0.4 fusion.48
  157.8 1.0 convolution_add_fusion.3
  158.8 0.3 fusion.22
  159.2 0.3 copy.24
  159.5 1.0 convert_element_type.116
  (40 shorter events, 0.3 us)
Async XLA Ops:
  6.5 1.6 copy-start
  6.5 94.0 %all-gather.2.cloned.1.call-start = ((), (), s32[]{:S(2)}) async-start(), calls=%async_computation | async-start | bytes 11141120 | tf_op jit(solution)/shard_map/all_gather | solution.py:91
  16.3 6.8 %copy-start.2 = (bf16[1,256,8192]{2,1,0:T(8,128)(2,1)S(1)}, bf16[1,256,8192]{2,1,0:T(8,128)(2,1)}, u32[]{:S(2)}) copy-start(bf16[1,256,8192]{2,1,0:T(8,128)(2,1)} %param.10) | copy-start | bytes 12582916
  21.0 3.1 %copy-start.3 = (bf16[8192]{0:T(1024)(128)(2,1)S(1)}, bf16[8192]{0:T(1024)(128)(2,1)}, u32[]{:S(2)}) copy-start(bf16[8192]{0:T(1024)(128)(2,1)} %param.11) | copy-start | bytes 49156
  21.0 47.7 %collective-permute-start.1 = (bf16[256,4096]{0,1:T(8,128)(2,1)}, bf16[256,4096]{0,1:T(8,128)(2,1)}, u32[]{:S(2)}, u32[]{:S(2)}) collective-permute-start(bf16[256,4096]{0,1:T(8,128)(2,1)} %bitcast.8), channel_id=1, source_target_pairs={{0,4},{4,0},{1,5},{5,1},{2,6},{6,2},{3,7},{7,3},{8,12},{12,8},{9,1... | collective-permute-start | bytes 6291464 | tf_op jit(solution)/shard_map/ppermute | solution.py:83
  24.0 44.7 %collective-permute-start.2 = (f32[256,1]{0,1:T(1,128)S(1)}, f32[256,1]{0,1:T(1,128)S(1)}, u32[]{:S(2)}, u32[]{:S(2)}) collective-permute-start(f32[256,1]{0,1:T(1,128)S(1)} %bitcast.68), channel_id=1, source_target_pairs={{0,4},{4,0},{1,5},{5,1},{2,6},{6,2},{3,7},{7,3},{8,12},{12,8},{9,1... | collective-permute-start | bytes 3080 | tf_op jit(solution)/shard_map/ppermute | solution.py:85
  100.5 12.0 %copy-start.5 = (bf16[128]{0:T(256)(128)(2,1)S(1)}, bf16[128]{0:T(256)(128)(2,1)}, u32[]{:S(2)}) copy-start(bf16[128]{0:T(256)(128)(2,1)} %param.17) | copy-start | bytes 772
  100.5 12.0 %copy-start.6 = (bf16[128]{0:T(256)(128)(2,1)S(1)}, bf16[128]{0:T(256)(128)(2,1)}, u32[]{:S(2)}) copy-start(bf16[128]{0:T(256)(128)(2,1)} %param.16) | copy-start | bytes 772
  100.5 12.0 %copy-start.4 = (bf16[1024]{0:T(1024)(128)(2,1)S(1)}, bf16[1024]{0:T(1024)(128)(2,1)}, u32[]{:S(2)}) copy-start(bf16[1024]{0:T(1024)(128)(2,1)} %param.15) | copy-start | bytes 6148
  111.2 16.1 %collective-permute-start.3 = (bf16[256,1280]{1,0:T(8,128)(2,1)S(1)}, bf16[256,1280]{1,0:T(8,128)(2,1)S(1)}, u32[]{:S(2)}, u32[]{:S(2)}) collective-permute-start(bf16[256,1280]{1,0:T(8,128)(2,1)S(1)} %slice.86), channel_id=1, source_target_pairs={{0,4},{4,0},{1,5},{5,1},{2,6},{6,2},{3,7},{7,3},{8,12},{12,8},{9,1... | collective-permute-start | bytes 1966088 | tf_op jit(solution)/shard_map/ppermute | solution.py:96
  129.6 0.8 copy-start.1
  132.0 5.1 %collective-permute-start = (bf16[2,256,128]{2,1,0:T(8,128)(2,1)S(1)}, bf16[2,256,128]{2,1,0:T(8,128)(2,1)S(1)}, u32[]{:S(2)}, u32[]{:S(2)}) collective-permute-start(bf16[2,256,128]{2,1,0:T(8,128)(2,1)S(1)} %get-tuple-element.233), channel_id=1, source_target_pairs={{0,1},{1,2},{2,3},{4,5},{5,6},{6,7},{8,9},{9,10},{10,11},{12,13},{... | collective-permute-start | bytes 393224 | tf_op jit(solution)/shard_map/while/body/eval_jaxpr/ppermute | solution.py:16
  140.1 6.3 %collective-permute-start = (bf16[2,256,128]{2,1,0:T(8,128)(2,1)S(1)}, bf16[2,256,128]{2,1,0:T(8,128)(2,1)S(1)}, u32[]{:S(2)}, u32[]{:S(2)}) collective-permute-start(bf16[2,256,128]{2,1,0:T(8,128)(2,1)S(1)} %get-tuple-element.233), channel_id=1, source_target_pairs={{0,1},{1,2},{2,3},{4,5},{5,6},{6,7},{8,9},{9,10},{10,11},{12,13},{... | collective-permute-start | bytes 393224 | tf_op jit(solution)/shard_map/while/body/eval_jaxpr/ppermute | solution.py:16
  149.5 6.3 %collective-permute-start = (bf16[2,256,128]{2,1,0:T(8,128)(2,1)S(1)}, bf16[2,256,128]{2,1,0:T(8,128)(2,1)S(1)}, u32[]{:S(2)}, u32[]{:S(2)}) collective-permute-start(bf16[2,256,128]{2,1,0:T(8,128)(2,1)S(1)} %get-tuple-element.233), channel_id=1, source_target_pairs={{0,1},{1,2},{2,3},{4,5},{5,6},{6,7},{8,9},{9,10},{10,11},{12,13},{... | collective-permute-start | bytes 393224 | tf_op jit(solution)/shard_map/while/body/eval_jaxpr/ppermute | solution.py:16
Sparse Core Ops, SparseCore 0:
  10.1 90.3 all-gather.1

commit v2 on v1

--- a/solution.py
+++ b/solution.py
@@ -1,8 +1,11 @@
+import functools
 import math
 
 import jax
 import jax.numpy as jnp
 from jax import lax
+from jax.experimental import pallas as pl
+from jax.experimental.pallas import tpu as pltpu
 from jax.sharding import Mesh, PartitionSpec as P
 
 epsilon = 1e-06
@@ -97,7 +100,297 @@
     return sums[:local_rows] + back.astype(jnp.float32)
 
 
+def normed_rows(block, scale, gain):
+    return (block.astype(jnp.float32) * scale * gain).astype(jnp.bfloat16)
+
+
+def slots_body(local, count, piece, order_ref, hidden, came, scale, came_scale, gain, *refs):
+    weights = refs[: (3 if local else 0) + 4 * (count - local)]
+    refs = refs[len(weights) :]
+    if local:
+        sums, held, guest, wide, stacked, sems = refs
+    else:
+        before, sums, back_kv, back_q, held, guest, wide, stacked, total, sems = refs
+    rows, depth = held.shape[1:]
+    copies = []
+    pending = list(weights)
+    slab = order_ref[count]
+    for slot in range(count):
+        column = pl.multiple_of(order_ref[slot] * depth, depth)
+        now = [
+            (hidden.at[:, pl.ds(column, depth)], held.at[slot]),
+            (came.at[:, pl.ds(slot * depth, depth)], guest.at[slot]),
+        ]
+        if slot < local:
+            at = 0
+            for _ in range(3):
+                weight = pending.pop(0)
+                now.append((weight, wide.at[slot, :, pl.ds(at, weight.shape[1])]))
+                at += weight.shape[1]
+        else:
+            for flip in (0, 2, 1, 3):
+                row = pl.multiple_of(jnp.bitwise_xor(slab, flip) * piece, piece)
+                now.append((pending.pop(0), wide.at[slot, pl.ds(row, piece), :]))
+        copies.append(now)
+    flights = []
+    number = 0
+    for now in copies:
+        flight = []
+        for source, target in now:
+            flight.append(pltpu.make_async_copy(source, target, sems.at[number]))
+            number += 1
+        flights.append(flight)
+    for flight in flights:
+        for copy in flight:
+            copy.start()
+    if not local:
+        fetch = pltpu.make_async_copy(before, total, sems.at[number])
+        fetch.start()
+    else:
+        total = sums
+    width = total.shape[1]
+    step = 256
+    tiles = list(range(0, width, step))
+    for slot in range(count):
+        for copy in flights[slot]:
+            copy.wait()
+        column = pl.multiple_of(order_ref[slot] * depth, depth)
+        row_gain = gain[:, pl.ds(column, depth)].astype(jnp.float32)
+        stacked[:rows] = normed_rows(held[slot], scale[...], row_gain)
+        stacked[rows:] = normed_rows(guest[slot], came_scale[...], row_gain)
+        if slot == 0 and not local:
+            fetch.wait()
+        for at in reversed(tiles):
+            cols = pl.ds(at, step)
+            product = jnp.dot(
+                stacked[...], wide[slot, :, cols], preferred_element_type=jnp.float32
+            )
+            if slot > 0 or not local:
+                product = product + total[:, cols]
+            if local or slot < count - 1:
+                total[:, cols] = product
+            else:
+                sums[:, cols] = product[:rows]
+                guests = product[rows:].astype(jnp.bfloat16)
+                if at == tiles[-1]:
+                    back_kv[...] = guests
+                else:
+                    back_q[:, cols] = guests
+
+
+def add_slots(local, order, hidden, came, scale, came_scale, gain, weights, before=None):
+    rows = hidden.shape[0]
+    count = order.shape[0] - 1
+    depth = came.shape[1] // count
+    piece = depth // 4
+    width = weights[-1].shape[1] if not local else sum(w.shape[1] for w in weights[:3])
+    anywhere = pl.BlockSpec(memory_space=pl.ANY)
+    inside = pl.BlockSpec(memory_space=pltpu.VMEM)
+    scratch = [
+        pltpu.VMEM((count, rows, depth), jnp.bfloat16),
+        pltpu.VMEM((count, rows, depth), jnp.bfloat16),
+        pltpu.VMEM((count, depth, width), jnp.bfloat16),
+        pltpu.VMEM((2 * rows, depth), jnp.bfloat16),
+    ]
+    copies = 2 * count + len(weights) + 1
+    args = [order, hidden, came, scale, came_scale, gain, *weights]
+    in_specs = [pl.BlockSpec(memory_space=pltpu.SMEM), anywhere, anywhere, inside, inside, inside]
+    in_specs += [anywhere] * len(weights)
+    if local:
+        out_shape = jax.ShapeDtypeStruct((2 * rows, width), jnp.float32)
+        out_specs = inside
+    else:
+        args.append(before)
+        in_specs.append(anywhere)
+        out_shape = (
+            jax.ShapeDtypeStruct((rows, width), jnp.float32),
+            jax.ShapeDtypeStruct((rows, 256), jnp.bfloat16),
+            jax.ShapeDtypeStruct((rows, width - 256), jnp.bfloat16),
+        )
+        out_specs = (inside, inside, inside)
+        scratch.append(pltpu.VMEM((2 * rows, width), jnp.float32))
+    scratch.append(pltpu.SemaphoreType.DMA((copies,)))
+    flops = 4 * rows * depth * count * width
+    moved = 2 * (depth * width * count + 2 * rows * depth * count) + 8 * rows * width
+    return pl.pallas_call(
+        functools.partial(slots_body, local, count, piece),
+        out_shape=out_shape,
+        in_specs=in_specs,
+        out_specs=out_specs,
+        scratch_shapes=scratch,
+        cost_estimate=pl.CostEstimate(flops=flops, bytes_accessed=moved, transcendentals=0),
+        compiler_params=pltpu.CompilerParams(vmem_limit_bytes=40 * 2**20),
+        name="slots_first" if local else "slots_last",
+    )(*args)
+
+
+def turned(tensor, cosine, sine_table):
+    half = tensor.shape[-1] // 2
+    return tensor * cosine + pltpu.roll(tensor, half, 1) * sine_table
+
+
+def key_value_body(sums, back, bias, cosine, sine_table, out):
+    head = out.shape[1] // 2
+    total = sums[...] + back[...].astype(jnp.float32) + bias[...].astype(jnp.float32)
+    out[:, :head] = turned(total[:, :head], cosine[...], sine_table[...]).astype(jnp.bfloat16)
+    out[:, head:] = total[:, head:].astype(jnp.bfloat16)
+
+
+def attention_body(scale, slab_ref, sums, back, bias, cosine, sine_table, *refs):
+    blocks, (out, keys, values) = (refs[:4], refs[4:])
+    rows, width = out.shape
+    head = cosine.shape[1]
+    slab = slab_ref[0]
+    for flip, block in zip((0, 1, 2, 3), blocks):
+        row = pl.multiple_of(jnp.bitwise_xor(slab, flip) * rows, rows)
+        keys[pl.ds(row, rows), :] = block[:, :head]
+        values[pl.ds(row, rows), :] = block[:, head:]
+    total_keys = keys.shape[0]
+    row_ids = slab * rows + lax.broadcasted_iota(jnp.int32, (rows, total_keys), 0)
+    visible = lax.broadcasted_iota(jnp.int32, (rows, total_keys), 1) <= row_ids
+    for at in range(0, width, head):
+        cols = pl.ds(at, head)
+        query = sums[:, cols] + back[:, cols].astype(jnp.float32) + bias[:, cols].astype(jnp.float32)
+        query = turned(query, cosine[...], sine_table[...]).astype(jnp.bfloat16)
+        scores = lax.dot_general(
+            query, keys[...], (((1,), (1,)), ((), ())), preferred_element_type=jnp.float32
+        )
+        scores = jnp.where(visible, scores * scale, masked_score)
+        exps = jnp.exp(scores - jnp.max(scores, axis=1, keepdims=True))
+        length = jnp.sum(exps, axis=1, keepdims=True)
+        mixed = jnp.dot(exps.astype(jnp.bfloat16), values[...], preferred_element_type=jnp.float32)
+        out[:, cols] = (mixed / length).astype(jnp.bfloat16)
+
+
+def planned(hidden, norm_gain, w_query, w_key, w_value, bias_query, bias_key, bias_value):
+    tokens = hidden[0]
+    rows = tokens.shape[0]
+    depth, query_width = w_query.shape
+    head = w_key.shape[1]
+    line, side, slab = (lax.axis_index("line"), lax.axis_index("pair"), lax.axis_index("ctx"))
+    inner = (line == 1) | (line == 2)
+    swap = [(0, 1), (1, 0)]
+    ends = [(0, 1), (1, 0), (2, 3), (3, 2)]
+    middle = [(1, 2), (2, 1)]
+    outward = [(1, 0), (2, 3)]
+    across = [(i, i ^ 2) for i in range(4)]
+    beside = [(i, i ^ 1) for i in range(4)]
+    third = jnp.where(inner, line ^ 3, line ^ 2)
+    fourth = jnp.where(inner, line ^ 2, line ^ 3)
+    lines = [line, line ^ 1, third, fourth]
+
+    def column_block(which, parity):
+        return lax.dynamic_slice_in_dim(tokens, (2 * which + parity) * depth, depth, 1)
+
+    sent_first = jnp.concatenate([column_block(which, 1 - side) for which in lines[:3]], axis=1)
+    sent_last = column_block(lines[3], 1 - side)
+    came_first = lax.ppermute(sent_first, "pair", swap)
+    came_last = lax.ppermute(sent_last, "pair", swap)
+    scale = row_scale(tokens)
+    came_scale = lax.ppermute(scale.reshape(rows), "pair", swap).reshape(rows, 1)
+
+    piece = depth // 4
+    start = slab * piece
+    mine = jnp.concatenate(
+        [lax.dynamic_slice_in_dim(w, start, piece, 0) for w in (w_query, w_key, w_value)], axis=1
+    )
+    second_piece = lax.ppermute(mine, "line", ends)
+    third_in = lax.ppermute(mine, "line", middle)
+    third_out = lax.ppermute(third_in, "line", outward)
+    fourth_in = lax.ppermute(second_piece, "line", middle)
+    fourth_out = lax.ppermute(fourth_in, "line", outward)
+    third_piece = jnp.where(inner, third_in, third_out)
+    fourth_piece = jnp.where(inner, fourth_in, fourth_out)
+
+    def spread(part):
+        far = lax.ppermute(part, "ctx", across)
+        return [part, far, lax.ppermute(part, "ctx", beside), lax.ppermute(far, "ctx", beside)]
+
+    second, third_all, fourth_all = [spread(p) for p in (second_piece, third_piece, fourth_piece)]
+    gain = norm_gain.reshape(1, -1)
+    order_first = jnp.stack([2 * which + side for which in lines[:3]] + [slab]).astype(jnp.int32)
+    order_last = jnp.stack([2 * lines[3] + side, slab]).astype(jnp.int32)
+    before = add_slots(
+        1,
+        order_first,
+        tokens,
+        came_first,
+        scale,
+        came_scale,
+        gain,
+        [w_query, w_key, w_value, *second, *third_all],
+    )
+    sums, back_kv, back_q = add_slots(
+        0, order_last, tokens, came_last, scale, came_scale, gain, fourth_all, before
+    )
+    back_kv = lax.ppermute(back_kv, "pair", swap)
+    back_q = lax.ppermute(back_q, "pair", swap)
+
+    positions = slab * rows + jnp.arange(rows, dtype=jnp.int32)
+    cosine, sine_table = rotary_tables(positions, head)
+    cosine = jnp.concatenate([cosine, cosine], axis=-1).reshape(rows, head)
+    sine_table = jnp.concatenate([-sine_table, sine_table], axis=-1).reshape(rows, head)
+    key_value = pl.pallas_call(
+        key_value_body,
+        out_shape=jax.ShapeDtypeStruct((rows, 2 * head), jnp.bfloat16),
+        grid=(1,),
+        in_specs=[
+            pl.BlockSpec((rows, 2 * head), lambda i: (0, query_width // (2 * head))),
+            pl.BlockSpec((rows, 2 * head), lambda i: (0, 0)),
+            pl.BlockSpec((1, 2 * head), lambda i: (0, 0)),
+            pl.BlockSpec((rows, head), lambda i: (0, 0)),
+            pl.BlockSpec((rows, head), lambda i: (0, 0)),
+        ],
+        out_specs=pl.BlockSpec((rows, 2 * head), lambda i: (0, 0)),
+        name="key_value",
+    )(sums, back_kv, jnp.concatenate([bias_key, bias_value]).reshape(1, -1), cosine, sine_table)
+    kv_across = lax.ppermute(key_value, "ctx", [(0, 2), (1, 3)])
+    kv_beside = lax.ppermute(key_value, "ctx", beside)
+    kv_corner = lax.ppermute(kv_across, "ctx", [(2, 3), (3, 2)])
+    kv_spec = pl.BlockSpec((rows, 2 * head), lambda i: (0, 0))
+    attended = pl.pallas_call(
+        functools.partial(attention_body, head ** (-0.5)),
+        out_shape=jax.ShapeDtypeStruct((rows, query_width), jnp.bfloat16),
+        grid=(1,),
+        in_specs=[
+            pl.BlockSpec(memory_space=pltpu.SMEM),
+            pl.BlockSpec((rows, query_width), lambda i: (0, 0)),
+            pl.BlockSpec((rows, query_width), lambda i: (0, 0)),
+            pl.BlockSpec((1, query_width), lambda i: (0, 0)),
+            pl.BlockSpec((rows, head), lambda i: (0, 0)),
+            pl.BlockSpec((rows, head), lambda i: (0, 0)),
+            kv_spec,
+            kv_spec,
+            kv_spec,
+            kv_spec,
+        ],
+        out_specs=pl.BlockSpec((rows, query_width), lambda i: (0, 0)),
+        scratch_shapes=[
+            pltpu.VMEM((4 * rows, head), jnp.bfloat16),
+            pltpu.VMEM((4 * rows, head), jnp.bfloat16),
+        ],
+        compiler_params=pltpu.CompilerParams(vmem_limit_bytes=40 * 2**20),
+        name="attention",
+    )(
+        slab.reshape(1).astype(jnp.int32),
+        sums,
+        back_q,
+        bias_query.reshape(1, -1),
+        cosine,
+        sine_table,
+        key_value,
+        kv_beside,
+        kv_across,
+        kv_corner,
+    )
+    return attended[None]
+
+
 def shards(hidden, norm_gain, w_query, w_key, w_value, bias_query, bias_key, bias_value):
+    if lax.axis_size("line") == 4 and lax.axis_size("ctx") == 4:
+        return planned(
+            hidden, norm_gain, w_query, w_key, w_value, bias_query, bias_key, bias_value
+        )
     local_rows = hidden.shape[1]
     head_width = w_key.shape[1]
     query_width = w_query.shape[1]

time: 168 us -> 146 us (0.87)
  the two profiles are of different devices: /device:TPU:1 before, /device:TPU:11 now
where the time goes in v2:
time: 146 us; the launch traced here: 145 us
  waiting for transfers between devices  65.7 us (45%)
  starting transfers between devices  37.3 us (26%)
  Pallas kernels  19.8 us (14%)
  local copies, waits for them, and re-layouts  17.5 us (12%)
  other arithmetic  4.42 us (3%)
    pallas_call x2, Pallas kernels, add_slots(): pl.pallas_call(functools.partial(slots_body, local, count, piece), out_sh...  12.8 us
    ppermute x1, waiting for transfers between devices, planned(): back_kv = lax.ppermute(back_kv, 'pair', swap)  12.7 us
    ppermute x1, waiting for transfers between devices, planned(): third_in = lax.ppermute(mine, 'line', middle)  11.6 us
    ppermute x3, waiting for transfers between devices, spread(): far = lax.ppermute(part, 'ctx', across)  11 us
    ppermute x3, starting transfers between devices, spread(): lax.ppermute(far, 'ctx', beside)  10.4 us
    ppermute x1, waiting for transfers between devices, planned(): fourth_in = lax.ppermute(second_piece, 'line', middle)  10.2 us
    unnamed x40, local copies, waits for them, and re-layouts  10 us
    ppermute x1, waiting for transfers between devices, planned(): lax.ppermute(scale.reshape(rows), 'pair', swap).reshape(rows, 1)  8.64 us
  transfers between devices with their start and end apart: 22, of which 9 were waited for; matrix products, arithmetic and copies ran while one was open for 7% of the time, Pallas kernels for 7%

profile of v2, /device:TPU:11, one launch (start us, length us, event | category | flops | bytes accessed | tf_op | source)
XLA Modules:
  0.0 145.1 jit_solution(17135379297118938351)
XLA Ops:
  0.0 1.1 constant_dynamic-slice_fusion.2
  1.1 0.9 constant_dynamic-slice_fusion
  2.0 3.2 %collective-permute-start.12 = (bf16[256,1280]{1,0:T(8,128)(2,1)S(1)}, bf16[256,1280]{1,0:T(8,128)(2,1)S(1)}, u32[]{:S(2)}, u32[]{:S(2)}) collective-permute-start(bf16[256,1280]{1,0:T(8,128)(2,1)S(1)} %pad_maximum_fusion.1), channel_id=1, source_target_pairs={{8,16},{16,8},{9,17},{17,9},{10,18},{18,10},{11,19},{19,11},{12,20... | collective-permute-start | bytes 1966088 | tf_op jit(solution)/shard_map/ppermute | solution.py:298
  5.4 2.7 %dynamic-slice_bitcast_fusion.2 = (bf16[256,1024]{1,0:T(8,128)(2,1)S(1)}, bf16[256,1024]{1,0:T(8,128)(2,1)}, bf16[256,1024]{1,0:T(8,128)(2,1)S(1)}, bf16[256,1024]{1,0:T(8,128)(2,1)S(1)}) fusion(bf16[1,256,8192]{2,1,0:T(8,128)(2,1)} %param.8, s32[]{:T(128)S(6)} %select_n.42, s32[]{:T(128)S(6)} %select_n.37, s32[]{:T(128)S(6)} %select_n.44, s32[]{:T(128)S(6)} %select_n.43), kind=kLoop, calls=%fused_computation.7 | loop fusion | bytes 4194320 | tf_op jit(solution)/shard_map/dynamic_slice | solution.py:283
  8.0 11.6 %collective-permute-done.12 = bf16[256,1280]{1,0:T(8,128)(2,1)S(1)} collective-permute-done((bf16[256,1280]{1,0:T(8,128)(2,1)S(1)}, bf16[256,1280]{1,0:T(8,128)(2,1)S(1)}, u32[]{:S(2)}, u32[]{:S(2)}) %collective-permute-start.12) | collective-permute-done | bytes 655392 | tf_op jit(solution)/shard_map/ppermute | solution.py:298
  19.6 1.3 collective-permute-start.13
  21.0 3.2 %collective-permute-start.3 = (bf16[256,1280]{1,0:T(8,128)(2,1)}, bf16[256,1280]{1,0:T(8,128)(2,1)S(1)}, u32[]{:S(2)}, u32[]{:S(2)}) collective-permute-start(bf16[256,1280]{1,0:T(8,128)(2,1)} %collective-permute-done.2.refs_3_), channel_id=1, source_target_pairs={{8,16},{16,8},{9,17},{17,9},{10,18},{18,10},{11,19},{19,11},{12,20... | collective-permute-start | bytes 1966088 | tf_op jit(solution)/shard_map/ppermute | solution.py:300
  24.2 1.3 pad_maximum_fusion
  25.5 1.2 collective-permute-start.8
  26.7 0.9 multiply_reduce_fusion
  27.6 10.2 %collective-permute-done.3 = bf16[256,1280]{1,0:T(8,128)(2,1)S(1)} collective-permute-done((bf16[256,1280]{1,0:T(8,128)(2,1)}, bf16[256,1280]{1,0:T(8,128)(2,1)S(1)}, u32[]{:S(2)}, u32[]{:S(2)}) %collective-permute-start.3) | collective-permute-done | bytes 655392 | tf_op jit(solution)/shard_map/ppermute | solution.py:300
  37.8 1.3 collective-permute-start.4
  39.2 1.3 collective-permute-start.1
  40.7 3.0 %collective-permute-start.10 = (bf16[256,1280]{1,0:T(8,128)(2,1)}, bf16[256,1280]{1,0:T(8,128)(2,1)S(1)}, u32[]{:S(2)}, u32[]{:S(2)}) collective-permute-start(bf16[256,1280]{1,0:T(8,128)(2,1)} %collective-permute-done.2.refs_3_), channel_id=1, source_target_pairs={{0,1},{1,0},{2,3},{3,2},{4,5},{5,4},{6,7},{7,6},{8,9},{9,8},{10,11... | collective-permute-start | bytes 1966088 | tf_op jit(solution)/shard_map/ppermute | solution.py:307
  43.8 7.2 %collective-permute-done.4 = bf16[256,1280]{1,0:T(8,128)(2,1)S(1)} collective-permute-done((bf16[256,1280]{1,0:T(8,128)(2,1)S(1)}, bf16[256,1280]{1,0:T(8,128)(2,1)S(1)}, u32[]{:S(2)}, u32[]{:S(2)}) %collective-permute-start.4) | collective-permute-done | bytes 655392 | tf_op jit(solution)/shard_map/ppermute | solution.py:301
  51.3 8.6 %collective-permute-done.1 = f32[256]{0:T(256)S(1)} collective-permute-done((f32[256]{0:T(256)S(1)}, f32[256]{0:T(256)S(1)}, u32[]{:S(2)}, u32[]{:S(2)}) %collective-permute-start.1) | collective-permute-done | bytes 1056 | tf_op jit(solution)/shard_map/ppermute | solution.py:290
  60.2 2.9 %collective-permute-start.15 = (bf16[256,1280]{1,0:T(8,128)(2,1)S(1)}, bf16[256,1280]{1,0:T(8,128)(2,1)}, u32[]{:S(2)}, u32[]{:S(2)}) collective-permute-start(bf16[256,1280]{1,0:T(8,128)(2,1)S(1)} %broadcast_select_fusion.refs_7_), channel_id=1, source_target_pairs={{0,1},{1,0},{2,3},{3,2},{4,5},{5,4},{6,7},{7,6},{8,9},{9,8},{10,11... | collective-permute-start | bytes 1966088 | tf_op jit(solution)/shard_map/ppermute | solution.py:307
  63.1 0.9 copy-done.9
  64.1 4.3 %collective-permute-done.14.refs_8_ = bf16[256,1280]{1,0:T(8,128)(2,1)} collective-permute-done((bf16[256,1280]{1,0:T(8,128)(2,1)S(1)}, bf16[256,1280]{1,0:T(8,128)(2,1)}, u32[]{:S(2)}, u32[]{:S(2)}) %collective-permute-start.14) | collective-permute-done | bytes 655392 | tf_op jit(solution)/shard_map/ppermute | solution.py:306
  68.4 6.8 %collective-permute-start.16 = (bf16[256,1280]{1,0:T(8,128)(2,1)}, bf16[256,1280]{1,0:T(8,128)(2,1)}, u32[]{:S(2)}, u32[]{:S(2)}) collective-permute-start(bf16[256,1280]{1,0:T(8,128)(2,1)} %collective-permute-done.14.refs_8_), channel_id=1, source_target_pairs={{0,1},{1,0},{2,3},{3,2},{4,5},{5,4},{6,7},{7,6},{8,9},{9,8},{10,11... | collective-permute-start | bytes 1966088 | tf_op jit(solution)/shard_map/ppermute | solution.py:307
  75.7 6.7 %collective-permute-done.5.refs_1_ = bf16[256,1280]{1,0:T(8,128)(2,1)} collective-permute-done((bf16[256,1280]{1,0:T(8,128)(2,1)S(1)}, bf16[256,1280]{1,0:T(8,128)(2,1)}, u32[]{:S(2)}, u32[]{:S(2)}) %collective-permute-start.5) | collective-permute-done | bytes 655392 | tf_op jit(solution)/shard_map/ppermute | solution.py:306
  82.4 3.6 %collective-permute-start.7 = (bf16[256,1280]{1,0:T(8,128)(2,1)}, bf16[256,1280]{1,0:T(8,128)(2,1)}, u32[]{:S(2)}, u32[]{:S(2)}) collective-permute-start(bf16[256,1280]{1,0:T(8,128)(2,1)} %collective-permute-done.5.refs_1_), channel_id=1, source_target_pairs={{0,1},{1,0},{2,3},{3,2},{4,5},{5,4},{6,7},{7,6},{8,9},{9,8},{10,11... | collective-permute-start | bytes 1966088 | tf_op jit(solution)/shard_map/ppermute | solution.py:307
  86.6 1.4 reshape.182.gain
  87.9 0.8 copy.12.came_scale
  88.7 0.9 copy-done.5
  89.6 1.1 copy-done.10
  90.7 0.9 copy-done.12
  91.7 0.9 copy-done.13
  92.6 0.8 copy-done.14
  93.4 7.8 %slots_first.1.refs_4_ = f32[512,1280]{1,0:T(8,128)S(1)} custom-call(s32[4]{0:T(128)S(1)} %pad_add_fusion.1.order_ref, bf16[256,8192]{1,0:T(8,128)(2,1)} %bitcast.22, bf16[256,3072]{1,0:T(8,128)(2,1)} %collective-permute-done.8.came, f32[256,1]{1,0:T(8,128)S(1)} %copy.11.scale, f32[256,1]{1,0:T(8,128)S(1)} %copy-done.5, bf16[1,8192]{1,0:T(2,128)(2,1)S(1)} %copy-done.14, ...), custom_call_target="tpu_custom_call" | custom-call | flops 4026531840 | bytes 13631488 | tf_op jit(solution)/shard_map/slots_first/pallas_call | solution.py:215
  101.3 5.0 %slots_last.1 = (f32[256,1280]{1,0:T(8,128)S(1)}, bf16[256,256]{1,0:T(8,128)(2,1)S(1)}, bf16[256,1024]{1,0:T(8,128)(2,1)}) custom-call(s32[2]{0:T(128)S(1)} %pad_add_fusion.order_ref, bf16[256,8192]{1,0:T(8,128)(2,1)S(1)} %bitcast.23, bf16[256,1024]{1,0:T(8,128)(2,1)} %collective-permute-done.came, f32[256,1]{1,0:T(8,128)S(1)} %copy.11.scale, ...), custom_call_target="tpu_custom_call" | custom-call | flops 1342177280 | bytes 6291456 | tf_op jit(solution)/shard_map/slots_last/pallas_call | solution.py:215
  106.3 1.1 copy-done.2
  107.3 1.2 collective-permute-start.17
  108.6 0.5 fusion
  109.4 0.6 reshape.186.bias
  110.0 0.8 maximum_bitcast_fusion
  110.8 12.7 %collective-permute-done.18.back = bf16[256,256]{1,0:T(8,128)(2,1)S(1)} collective-permute-done((bf16[256,256]{1,0:T(8,128)(2,1)S(1)}, bf16[256,256]{1,0:T(8,128)(2,1)S(1)}, u32[]{:S(2)}, u32[]{:S(2)}) %collective-permute-start.18) | collective-permute-done | bytes 131104 | tf_op jit(solution)/shard_map/ppermute | solution.py:326
  123.6 0.7 copy-done.15
  124.2 1.9 %key_value.1.refs_0_ = bf16[256,256]{1,0:T(8,128)(2,1)} custom-call(f32[256,1280]{1,0:T(8,128)} %copy-done.2, bf16[256,256]{1,0:T(8,128)(2,1)} %copy-done.15, bf16[1,256]{1,0:T(2,128)(2,1)} %reshape.186.bias, f32[256,128]{1,0:T(8,128)} %get-tuple-element.20.cosine, f32[256,128]{1,0:T(8,128)} %get-tuple-element.21.sine_table), custom_call_target="tpu_custom_call" | custom-call | tf_op jit(solution)/shard_map/key_value/pallas_call | solution.py:333
  126.1 1.3 collective-permute-start.20
  127.4 1.2 collective-permute-start.19
  128.6 3.4 %collective-permute-done.20.refs_2_ = bf16[256,256]{1,0:T(8,128)(2,1)S(1)} collective-permute-done((bf16[256,256]{1,0:T(8,128)(2,1)}, bf16[256,256]{1,0:T(8,128)(2,1)S(1)}, u32[]{:S(2)}, u32[]{:S(2)}) %collective-permute-start.20) | collective-permute-done | bytes 131104 | tf_op jit(solution)/shard_map/ppermute | solution.py:347
  132.0 4.3 %collective-permute-start.21 = (bf16[256,256]{1,0:T(8,128)(2,1)S(1)}, bf16[256,256]{1,0:T(8,128)(2,1)S(1)}, u32[]{:S(2)}, u32[]{:S(2)}) collective-permute-start(bf16[256,256]{1,0:T(8,128)(2,1)S(1)} %collective-permute-done.20.refs_2_), channel_id=1, source_target_pairs={{2,3},{3,2},{6,7},{7,6},{10,11},{11,10},{14,15},{15,14},{18,19},{1... | collective-permute-start | bytes 393224 | tf_op jit(solution)/shard_map/ppermute | solution.py:349
  136.4 0.8 collective-permute-done.21.refs_3_
  137.2 0.9 copy-done.7
  138.1 0.9 copy-done.8
  139.0 0.9 copy-done.11
  139.9 5.2 %attention.1 = bf16[256,1024]{1,0:T(8,128)(2,1)} custom-call(s32[1]{0:T(128)} %bitcast.slab_ref, f32[256,1280]{1,0:T(8,128)S(1)} %copy-done.3, bf16[256,1024]{1,0:T(8,128)(2,1)S(1)} %collective-permute-done.17.back, bf16[1,1024]{1,0:T(2,128)(2,1)S(1)} %reshape.183.bias, f32[256,128]{1,0:T(8,128)S(1)} %copy-done.7, f32[256,128]{1,0:T(8,128)S(1)} %copy-done.8, ...), custom_call_target="tpu_custom_call" | custom-call | tf_op jit(solution)/shard_map/attention/pallas_call | solution.py:351
  (61 shorter events, 2.4 us)
Async XLA Ops:
  2.0 17.6 %collective-permute-start.12 = (bf16[256,1280]{1,0:T(8,128)(2,1)S(1)}, bf16[256,1280]{1,0:T(8,128)(2,1)S(1)}, u32[]{:S(2)}, u32[]{:S(2)}) collective-permute-start(bf16[256,1280]{1,0:T(8,128)(2,1)S(1)} %pad_maximum_fusion.1), channel_id=1, source_target_pairs={{8,16},{16,8},{9,17},{17,9},{10,18},{18,10},{11,19},{19,11},{12,20... | collective-permute-start | bytes 1966088 | tf_op jit(solution)/shard_map/ppermute | solution.py:298
  5.2 15.7 %collective-permute-start.2 = (bf16[256,1280]{1,0:T(8,128)(2,1)S(1)}, bf16[256,1280]{1,0:T(8,128)(2,1)}, u32[]{:S(2)}, u32[]{:S(2)}) collective-permute-start(bf16[256,1280]{1,0:T(8,128)(2,1)S(1)} %pad_maximum_fusion.1), channel_id=1, source_target_pairs={{0,8},{8,0},{16,24},{24,16},{1,9},{9,1},{17,25},{25,17},{2,10},{10... | collective-permute-start | bytes 1966088 | tf_op jit(solution)/shard_map/ppermute | solution.py:297
  5.4 21.3 %copy-start = (bf16[1,256,8192]{2,1,0:T(8,128)(2,1)S(1)}, bf16[1,256,8192]{2,1,0:T(8,128)(2,1)}, u32[]{:S(2)}) copy-start(bf16[1,256,8192]{2,1,0:T(8,128)(2,1)} %param.8) | copy-start | bytes 12582916
  19.6 21.1 %collective-permute-start.13 = (bf16[256,1280]{1,0:T(8,128)(2,1)S(1)}, bf16[256,1280]{1,0:T(8,128)(2,1)S(1)}, u32[]{:S(2)}, u32[]{:S(2)}) collective-permute-start(bf16[256,1280]{1,0:T(8,128)(2,1)S(1)} %collective-permute-done.12), channel_id=1, source_target_pairs={{8,0},{16,24},{9,1},{17,25},{10,2},{18,26},{11,3},{19,27},{12,4},{... | collective-permute-start | bytes 1966088 | tf_op jit(solution)/shard_map/ppermute | solution.py:299
  21.0 16.9 %collective-permute-start.3 = (bf16[256,1280]{1,0:T(8,128)(2,1)}, bf16[256,1280]{1,0:T(8,128)(2,1)S(1)}, u32[]{:S(2)}, u32[]{:S(2)}) collective-permute-start(bf16[256,1280]{1,0:T(8,128)(2,1)} %collective-permute-done.2.refs_3_), channel_id=1, source_target_pairs={{8,16},{16,8},{9,17},{17,9},{10,18},{18,10},{11,19},{19,11},{12,20... | collective-permute-start | bytes 1966088 | tf_op jit(solution)/shard_map/ppermute | solution.py:300
  25.5 50.2 %collective-permute-start.8 = (bf16[256,3072]{1,0:T(8,128)(2,1)}, bf16[256,3072]{1,0:T(8,128)(2,1)}, u32[]{:S(2)}, u32[]{:S(2)}) collective-permute-start(bf16[256,3072]{1,0:T(8,128)(2,1)} %pad_maximum_fusion), channel_id=1, source_target_pairs={{0,4},{4,0},{1,5},{5,1},{2,6},{6,2},{3,7},{7,3},{8,12},{12,8},{9,1... | collective-permute-start | bytes 4718600 | tf_op jit(solution)/shard_map/ppermute | solution.py:287
  37.8 13.2 %collective-permute-start.4 = (bf16[256,1280]{1,0:T(8,128)(2,1)S(1)}, bf16[256,1280]{1,0:T(8,128)(2,1)S(1)}, u32[]{:S(2)}, u32[]{:S(2)}) collective-permute-start(bf16[256,1280]{1,0:T(8,128)(2,1)S(1)} %collective-permute-done.3), channel_id=1, source_target_pairs={{8,0},{16,24},{9,1},{17,25},{10,2},{18,26},{11,3},{19,27},{12,4},{... | collective-permute-start | bytes 1966088 | tf_op jit(solution)/shard_map/ppermute | solution.py:301
  39.2 49.6 %copy-start.4 = (bf16[1024,1024]{1,0:T(8,128)(2,1)S(1)}, bf16[1024,1024]{1,0:T(8,128)(2,1)}, u32[]{:S(2)}) copy-start(bf16[1024,1024]{1,0:T(8,128)(2,1)} %refs_0_.1) | copy-start | bytes 6291460
  39.2 20.8 %collective-permute-start.1 = (f32[256]{0:T(256)S(1)}, f32[256]{0:T(256)S(1)}, u32[]{:S(2)}, u32[]{:S(2)}) collective-permute-start(f32[256]{0:T(256)S(1)} %add_rsqrt_fusion), channel_id=1, source_target_pairs={{0,4},{4,0},{1,5},{5,1},{2,6},{6,2},{3,7},{7,3},{8,12},{12,8},{9,1... | collective-permute-start | bytes 3080 | tf_op jit(solution)/shard_map/ppermute | solution.py:290
  40.5 19.7 %collective-permute-start.9 = (bf16[256,1280]{1,0:T(8,128)(2,1)}, bf16[256,1280]{1,0:T(8,128)(2,1)}, u32[]{:S(2)}, u32[]{:S(2)}) collective-permute-start(bf16[256,1280]{1,0:T(8,128)(2,1)} %collective-permute-done.2.refs_3_), channel_id=1, source_target_pairs={{0,2},{1,3},{2,0},{3,1},{4,6},{5,7},{6,4},{7,5},{8,10},{9,11},{10,... | collective-permute-start | bytes 1966088 | tf_op jit(solution)/shard_map/ppermute | solution.py:306
  40.7 22.4 %collective-permute-start.10 = (bf16[256,1280]{1,0:T(8,128)(2,1)}, bf16[256,1280]{1,0:T(8,128)(2,1)S(1)}, u32[]{:S(2)}, u32[]{:S(2)}) collective-permute-start(bf16[256,1280]{1,0:T(8,128)(2,1)} %collective-permute-done.2.refs_3_), channel_id=1, source_target_pairs={{0,1},{1,0},{2,3},{3,2},{4,5},{5,4},{6,7},{7,6},{8,9},{9,8},{10,11... | collective-permute-start | bytes 1966088 | tf_op jit(solution)/shard_map/ppermute | solution.py:307
  51.0 17.4 %collective-permute-start.14 = (bf16[256,1280]{1,0:T(8,128)(2,1)S(1)}, bf16[256,1280]{1,0:T(8,128)(2,1)}, u32[]{:S(2)}, u32[]{:S(2)}) collective-permute-start(bf16[256,1280]{1,0:T(8,128)(2,1)S(1)} %broadcast_select_fusion.refs_7_), channel_id=1, source_target_pairs={{0,2},{1,3},{2,0},{3,1},{4,6},{5,7},{6,4},{7,5},{8,10},{9,11},{10,... | collective-permute-start | bytes 1966088 | tf_op jit(solution)/shard_map/ppermute | solution.py:306
  60.0 22.5 %collective-permute-start.5 = (bf16[256,1280]{1,0:T(8,128)(2,1)S(1)}, bf16[256,1280]{1,0:T(8,128)(2,1)}, u32[]{:S(2)}, u32[]{:S(2)}) collective-permute-start(bf16[256,1280]{1,0:T(8,128)(2,1)S(1)} %broadcast_select_fusion.1.refs_0_), channel_id=1, source_target_pairs={{0,2},{1,3},{2,0},{3,1},{4,6},{5,7},{6,4},{7,5},{8,10},{9,11},{10,... | collective-permute-start | bytes 1966088 | tf_op jit(solution)/shard_map/ppermute | solution.py:306
  60.2 25.9 %collective-permute-start.15 = (bf16[256,1280]{1,0:T(8,128)(2,1)S(1)}, bf16[256,1280]{1,0:T(8,128)(2,1)}, u32[]{:S(2)}, u32[]{:S(2)}) collective-permute-start(bf16[256,1280]{1,0:T(8,128)(2,1)S(1)} %broadcast_select_fusion.refs_7_), channel_id=1, source_target_pairs={{0,1},{1,0},{2,3},{3,2},{4,5},{5,4},{6,7},{7,6},{8,9},{9,8},{10,11... | collective-permute-start | bytes 1966088 | tf_op jit(solution)/shard_map/ppermute | solution.py:307
  63.1 0.9 copy-start.9
  64.1 24.6 %collective-permute-start.11 = (bf16[256,1280]{1,0:T(8,128)(2,1)}, bf16[256,1280]{1,0:T(8,128)(2,1)}, u32[]{:S(2)}, u32[]{:S(2)}) collective-permute-start(bf16[256,1280]{1,0:T(8,128)(2,1)} %collective-permute-done.9.refs_4_), channel_id=1, source_target_pairs={{0,1},{1,0},{2,3},{3,2},{4,5},{5,4},{6,7},{7,6},{8,9},{9,8},{10,11... | collective-permute-start | bytes 1966088 | tf_op jit(solution)/shard_map/ppermute | solution.py:307
  68.4 20.3 %collective-permute-start.16 = (bf16[256,1280]{1,0:T(8,128)(2,1)}, bf16[256,1280]{1,0:T(8,128)(2,1)}, u32[]{:S(2)}, u32[]{:S(2)}) collective-permute-start(bf16[256,1280]{1,0:T(8,128)(2,1)} %collective-permute-done.14.refs_8_), channel_id=1, source_target_pairs={{0,1},{1,0},{2,3},{3,2},{4,5},{5,4},{6,7},{7,6},{8,9},{9,8},{10,11... | collective-permute-start | bytes 1966088 | tf_op jit(solution)/shard_map/ppermute | solution.py:307
  75.7 25.6 %collective-permute-start.6 = (bf16[256,1280]{1,0:T(8,128)(2,1)S(1)}, bf16[256,1280]{1,0:T(8,128)(2,1)}, u32[]{:S(2)}, u32[]{:S(2)}) collective-permute-start(bf16[256,1280]{1,0:T(8,128)(2,1)S(1)} %broadcast_select_fusion.1.refs_0_), channel_id=1, source_target_pairs={{0,1},{1,0},{2,3},{3,2},{4,5},{5,4},{6,7},{7,6},{8,9},{9,8},{10,11... | collective-permute-start | bytes 1966088 | tf_op jit(solution)/shard_map/ppermute | solution.py:307
  82.4 18.8 %collective-permute-start.7 = (bf16[256,1280]{1,0:T(8,128)(2,1)}, bf16[256,1280]{1,0:T(8,128)(2,1)}, u32[]{:S(2)}, u32[]{:S(2)}) collective-permute-start(bf16[256,1280]{1,0:T(8,128)(2,1)} %collective-permute-done.5.refs_1_), channel_id=1, source_target_pairs={{0,1},{1,0},{2,3},{3,2},{4,5},{5,4},{6,7},{7,6},{8,9},{9,8},{10,11... | collective-permute-start | bytes 1966088 | tf_op jit(solution)/shard_map/ppermute | solution.py:307
  86.1 15.1 %collective-permute-start = (bf16[256,1024]{1,0:T(8,128)(2,1)}, bf16[256,1024]{1,0:T(8,128)(2,1)}, u32[]{:S(2)}, u32[]{:S(2)}) collective-permute-start(bf16[256,1024]{1,0:T(8,128)(2,1)} %get-tuple-element.12), channel_id=1, source_target_pairs={{0,4},{4,0},{1,5},{5,1},{2,6},{6,2},{3,7},{7,3},{8,12},{12,8},{9,1... | collective-permute-start | bytes 1572872 | tf_op jit(solution)/shard_map/ppermute | solution.py:288
  88.7 0.9 copy-start.5
  89.6 1.1 copy-start.10
  90.7 0.9 copy-start.12
  91.7 0.9 copy-start.13
  92.6 0.8 copy-start.14
  93.4 7.9 %copy-start.1 = (bf16[1,256,8192]{2,1,0:T(8,128)(2,1)S(1)}, bf16[1,256,8192]{2,1,0:T(8,128)(2,1)}, u32[]{:S(2)}) copy-start(bf16[1,256,8192]{2,1,0:T(8,128)(2,1)} %param.8) | copy-start | bytes 12582916
  93.4 7.9 %copy-start.6 = (f32[256,1]{1,0:T(8,128)S(1)}, f32[256,1]{1,0:T(8,128)}, u32[]{:S(2)}) copy-start(f32[256,1]{1,0:T(8,128)} %copy.12.came_scale) | copy-start | bytes 3076
  101.2 7.4 %copy-start.17 = (f32[64]{0:T(128)S(1)}, f32[64]{0:T(128)}, u32[]{:S(2)}) copy-start(f32[64]{0:T(128)} %multiply_exponential_fusion) | copy-start | bytes 772
  101.2 8.2 %copy-start.18 = (bf16[128]{0:T(256)(128)(2,1)S(1)}, bf16[128]{0:T(256)(128)(2,1)}, u32[]{:S(2)}) copy-start(bf16[128]{0:T(256)(128)(2,1)} %param.15) | copy-start | bytes 772
  101.2 8.2 %copy-start.19 = (bf16[128]{0:T(256)(128)(2,1)S(1)}, bf16[128]{0:T(256)(128)(2,1)}, u32[]{:S(2)}) copy-start(bf16[128]{0:T(256)(128)(2,1)} %param.14) | copy-start | bytes 772
  106.3 1.1 copy-start.2
  107.3 29.1 %copy-start.16 = (bf16[1024]{0:T(1024)(128)(2,1)S(1)}, bf16[1024]{0:T(1024)(128)(2,1)}, u32[]{:S(2)}) copy-start(bf16[1024]{0:T(1024)(128)(2,1)} %param.13) | copy-start | bytes 6148
  107.3 29.8 %copy-start.3 = (f32[256,1280]{1,0:T(8,128)S(1)}, f32[256,1280]{1,0:T(8,128)}, u32[]{:S(2)}) copy-start(f32[256,1280]{1,0:T(8,128)} %copy-done.2) | copy-start | bytes 3932164
  107.3 29.8 %collective-permute-start.17 = (bf16[256,1024]{1,0:T(8,128)(2,1)}, bf16[256,1024]{1,0:T(8,128)(2,1)S(1)}, u32[]{:S(2)}, u32[]{:S(2)}) collective-permute-start(bf16[256,1024]{1,0:T(8,128)(2,1)} %get-tuple-element.9), channel_id=1, source_target_pairs={{0,4},{4,0},{1,5},{5,1},{2,6},{6,2},{3,7},{7,3},{8,12},{12,8},{9,1... | collective-permute-start | bytes 1572872 | tf_op jit(solution)/shard_map/ppermute | solution.py:327
  109.1 14.5 %collective-permute-start.18 = (bf16[256,256]{1,0:T(8,128)(2,1)S(1)}, bf16[256,256]{1,0:T(8,128)(2,1)S(1)}, u32[]{:S(2)}, u32[]{:S(2)}) collective-permute-start(bf16[256,256]{1,0:T(8,128)(2,1)S(1)} %get-tuple-element.10), channel_id=1, source_target_pairs={{0,4},{4,0},{1,5},{5,1},{2,6},{6,2},{3,7},{7,3},{8,12},{12,8},{9,1... | collective-permute-start | bytes 393224 | tf_op jit(solution)/shard_map/ppermute | solution.py:326
  123.6 0.7 copy-start.15
  126.1 5.9 %collective-permute-start.20 = (bf16[256,256]{1,0:T(8,128)(2,1)}, bf16[256,256]{1,0:T(8,128)(2,1)S(1)}, u32[]{:S(2)}, u32[]{:S(2)}) collective-permute-start(bf16[256,256]{1,0:T(8,128)(2,1)} %key_value.1.refs_0_), channel_id=1, source_target_pairs={{0,2},{1,3},{4,6},{5,7},{8,10},{9,11},{12,14},{13,15},{16,18},{17,... | collective-permute-start | bytes 393224 | tf_op jit(solution)/shard_map/ppermute | solution.py:347
  127.4 9.0 %collective-permute-start.19 = (bf16[256,256]{1,0:T(8,128)(2,1)}, bf16[256,256]{1,0:T(8,128)(2,1)S(1)}, u32[]{:S(2)}, u32[]{:S(2)}) collective-permute-start(bf16[256,256]{1,0:T(8,128)(2,1)} %key_value.1.refs_0_), channel_id=1, source_target_pairs={{0,1},{1,0},{2,3},{3,2},{4,5},{5,4},{6,7},{7,6},{8,9},{9,8},{10,11... | collective-permute-start | bytes 393224 | tf_op jit(solution)/shard_map/ppermute | solution.py:348
  132.0 5.1 %collective-permute-start.21 = (bf16[256,256]{1,0:T(8,128)(2,1)S(1)}, bf16[256,256]{1,0:T(8,128)(2,1)S(1)}, u32[]{:S(2)}, u32[]{:S(2)}) collective-permute-start(bf16[256,256]{1,0:T(8,128)(2,1)S(1)} %collective-permute-done.20.refs_2_), channel_id=1, source_target_pairs={{2,3},{3,2},{6,7},{7,6},{10,11},{11,10},{14,15},{15,14},{18,19},{1... | collective-permute-start | bytes 393224 | tf_op jit(solution)/shard_map/ppermute | solution.py:349
  137.2 0.9 copy-start.7
  138.1 0.9 copy-start.8
  139.0 0.9 copy-start.11

commit v3 on v1

--- a/solution.py
+++ b/solution.py
@@ -1,8 +1,11 @@
+import functools
 import math
 
 import jax
 import jax.numpy as jnp
 from jax import lax
+from jax.experimental import pallas as pl
+from jax.experimental.pallas import tpu as pltpu
 from jax.sharding import Mesh, PartitionSpec as P
 
 epsilon = 1e-06
@@ -97,7 +100,496 @@
     return sums[:local_rows] + back.astype(jnp.float32)
 
 
+def normed_rows(block, scale, gain):
+    return (block.astype(jnp.float32) * scale * gain).astype(jnp.bfloat16)
+
+
+def slot_lines():
+    line = lax.axis_index("line")
+    inner = (line == 1) | (line == 2)
+    third = jnp.where(inner, line ^ 3, line ^ 2)
+    fourth = jnp.where(inner, line ^ 2, line ^ 3)
+    return [line, line ^ 1, third, fourth]
+
+
+def started(copies, sems, first):
+    flights = [
+        pltpu.make_async_copy(source, target, sems.at[first + number])
+        for number, (source, target) in enumerate(copies)
+    ]
+    for flight in flights:
+        flight.start()
+    return flights
+
+
+def piece_copies(pieces, wide, slab):
+    piece = pieces[0].shape[0]
+    return [
+        (source, wide.at[pl.ds(pl.multiple_of(jnp.bitwise_xor(slab, flip) * piece, piece), piece), :])
+        for source, flip in zip(pieces, (0, 2, 1, 3))
+    ]
+
+
+def pack_body(sent_parts, weights, depth, *refs):
+    tokens, refs = (refs[0], refs[1:])
+    sources, refs = (refs[:weights], refs[weights:])
+    sems = refs[-1]
+    copies = []
+    outs = refs[:-1]
+    if weights:
+        mine, outs = (outs[0], outs[1:])
+        piece = mine.shape[0]
+        row = pl.multiple_of(lax.axis_index("ctx") * piece, piece)
+        at = 0
+        for source in sources:
+            target = mine.at[:, pl.ds(at, source.shape[1])]
+            copies.append((source.at[pl.ds(row, piece), :], target))
+            at += source.shape[1]
+    lines = slot_lines()
+    other = 1 - lax.axis_index("pair")
+    for out, parts in zip(outs, sent_parts):
+        at = 0
+        for slot, first, count in parts:
+            column = pl.multiple_of((2 * lines[slot] + other) * depth + first, 128)
+            copies.append((tokens.at[:, pl.ds(column, count)], out.at[:, pl.ds(at, count)]))
+            at += count
+    for flight in started(copies, sems, 0):
+        flight.wait()
+
+
+def pack(tokens, depth, sent_parts, weights=()):
+    rows = tokens.shape[0]
+    outside = pl.BlockSpec(memory_space=pltpu.HBM)
+    outs = []
+    if weights:
+        piece = weights[0].shape[0] // 4
+        outs.append(jax.ShapeDtypeStruct((piece, sum(w.shape[1] for w in weights)), jnp.bfloat16))
+    for parts in sent_parts:
+        outs.append(jax.ShapeDtypeStruct((rows, sum(p[2] for p in parts)), jnp.bfloat16))
+    copies = len(weights) + sum(len(parts) for parts in sent_parts)
+    moved = 4 * sum(out.shape[0] * out.shape[1] for out in outs)
+    return pl.pallas_call(
+        functools.partial(pack_body, sent_parts, len(weights), depth),
+        out_shape=outs,
+        in_specs=[outside] * (1 + len(weights)),
+        out_specs=[pl.BlockSpec(memory_space=pltpu.VMEM)] * len(outs),
+        scratch_shapes=[pltpu.SemaphoreType.DMA((copies,))],
+        cost_estimate=pl.CostEstimate(flops=0, bytes_accessed=moved, transcendentals=0),
+        name="pack",
+    )(tokens, *weights)
+
+
+def prepare_body(sent_parts, depth, tokens, *refs):
+    outs, refs = (refs[: len(sent_parts)], refs[len(sent_parts) :])
+    column_scale, line_scale, held, sems = refs
+    rows, width = held.shape
+    lines = slot_lines()
+    other = 1 - lax.axis_index("pair")
+    loads = [
+        (tokens.at[:, pl.ds(at, depth)], held.at[:, pl.ds(at, depth)])
+        for at in range(0, width, depth)
+    ]
+    loads = started(loads, sems, 0)
+    copies = []
+    for out, parts in zip(outs, sent_parts):
+        at = 0
+        for slot, first, count in parts:
+            column = pl.multiple_of((2 * lines[slot] + other) * depth + first, 128)
+            copies.append((tokens.at[:, pl.ds(column, count)], out.at[:, pl.ds(at, count)]))
+            at += count
+    copies = started(copies, sems, len(loads))
+    squares = jnp.zeros((rows, 128), jnp.float32)
+    for number, load in enumerate(loads):
+        load.wait()
+        for at in range(number * depth, (number + 1) * depth, 128):
+            floats = held[:, at : at + 128].astype(jnp.float32)
+            squares = squares + floats * floats
+    mean = jnp.sum(squares, axis=1, keepdims=True) / width
+    wide = jnp.broadcast_to(lax.rsqrt(mean + epsilon), (rows, 128))
+    column_scale[...] = wide
+    line_scale[...] = jnp.transpose(wide)[:1]
+    for copy in copies:
+        copy.wait()
+
+
+def prepare(tokens, depth, sent_parts):
+    rows, width = tokens.shape
+    outs = [
+        jax.ShapeDtypeStruct((rows, sum(p[2] for p in parts)), jnp.bfloat16)
+        for parts in sent_parts
+    ]
+    outs.append(jax.ShapeDtypeStruct((rows, 128), jnp.float32))
+    outs.append(jax.ShapeDtypeStruct((1, rows), jnp.float32))
+    copies = width // depth + sum(len(parts) for parts in sent_parts)
+    return pl.pallas_call(
+        functools.partial(prepare_body, sent_parts, depth),
+        out_shape=outs,
+        in_specs=[pl.BlockSpec(memory_space=pltpu.HBM)],
+        out_specs=[pl.BlockSpec(memory_space=pltpu.VMEM)] * len(outs),
+        scratch_shapes=[
+            pltpu.VMEM((rows, width), jnp.bfloat16),
+            pltpu.SemaphoreType.DMA((copies,)),
+        ],
+        cost_estimate=pl.CostEstimate(
+            flops=2 * rows * width, bytes_accessed=4 * rows * width, transcendentals=rows
+        ),
+        name="prepare",
+    )(tokens)
+
+
+def early_body(slots, guests, local, final, hidden, *refs):
+    count = 1 + max(part[0] for part in guests)
+    cames, refs = (refs[:count], refs[count:])
+    scale, came_scale, gain, *refs = refs
+    summed = slots[:-1] if final else slots
+    number = 3 * local + 4 * (len(summed) - local)
+    weights, refs = (refs[:number], refs[number:])
+    before = None
+    if not local:
+        before, *refs = refs
+    total, *refs = refs
+    if final:
+        last_rows, *refs = refs
+    held, guest, wide, stacked, sems = refs
+    _, rows, depth = held.shape
+    slab = lax.axis_index("ctx")
+    blocks = [2 * which + lax.axis_index("pair") for which in slot_lines()]
+    number = 0
+    parts = []
+    at = 0
+    for source, first, width in guests:
+        parts.append(
+            (cames[source].at[:, pl.ds(first, width)], guest.at[:, pl.ds(at, width)])
+        )
+        at += width
+    guest_flights = started(parts, sems, number)
+    number += len(parts)
+    flights = []
+    pending = list(weights)
+    for place, slot in enumerate(slots):
+        column = pl.multiple_of(blocks[slot] * depth, depth)
+        copies = [(hidden.at[:, pl.ds(column, depth)], held.at[place])]
+        if slot == 0:
+            at = 0
+            for _ in range(3):
+                weight = pending.pop(0)
+                copies.append((weight, wide.at[place, :, pl.ds(at, weight.shape[1])]))
+                at += weight.shape[1]
+        elif slot in summed:
+            copies += piece_copies(pending[:4], wide.at[place], slab)
+            pending = pending[4:]
+        flights.append(started(copies, sems, number))
+        number += len(copies)
+    turned_scale = jnp.transpose(jnp.broadcast_to(came_scale[...], (128, rows)))[:, :1]
+    for flight in guest_flights:
+        flight.wait()
+    width = total.shape[1]
+    step = 256
+    for place, slot in enumerate(slots):
+        for flight in flights[place]:
+            flight.wait()
+        column = pl.multiple_of(blocks[slot] * depth, depth)
+        row_gain = gain[:, pl.ds(column, depth)].astype(jnp.float32)
+        target = stacked.at[place] if slot in summed else last_rows
+        target[:rows] = normed_rows(held[place], scale[:, :1], row_gain)
+        target[rows:] = normed_rows(
+            guest[:, place * depth : (place + 1) * depth], turned_scale, row_gain
+        )
+        if slot not in summed:
+            continue
+        for at in range(0, width, step):
+            cols = pl.ds(at, step)
+            product = jnp.dot(
+                stacked[place], wide[place, :, cols], preferred_element_type=jnp.float32
+            )
+            if place > 0:
+                product = product + total[:, cols]
+            elif before is not None:
+                product = product + before[:, cols]
+            total[:, cols] = product
+
+
+def early_slots(
+    slots, guests, local, final, hidden, cames, scale, came_scale, gain, weights, before=None
+):
+    rows = hidden.shape[0]
+    depth = weights[0].shape[0] if local else 4 * weights[0].shape[0]
+    width = sum(w.shape[1] for w in weights[:3]) if local else weights[0].shape[1]
+    outside = pl.BlockSpec(memory_space=pltpu.HBM)
+    anywhere = pl.BlockSpec(memory_space=pl.ANY)
+    inside = pl.BlockSpec(memory_space=pltpu.VMEM)
+    summed = len(slots) - final
+    flops = 4 * rows * depth * summed * width
+    moved = 2 * (depth * width * summed + 2 * rows * depth * len(slots)) + 8 * rows * width
+    outs = [jax.ShapeDtypeStruct((2 * rows, width), jnp.float32)]
+    if final:
+        outs.append(jax.ShapeDtypeStruct((2 * rows, depth), jnp.bfloat16))
+    args = [hidden, *cames, scale, came_scale, gain, *weights]
+    in_specs = [outside] + [anywhere] * len(cames)
+    in_specs += [inside] * 3 + [outside] * (3 * local) + [anywhere] * (len(weights) - 3 * local)
+    if before is not None:
+        args.append(before)
+        in_specs.append(inside)
+    return pl.pallas_call(
+        functools.partial(early_body, slots, guests, local, final),
+        out_shape=outs,
+        in_specs=in_specs,
+        out_specs=[inside] * len(outs),
+        scratch_shapes=[
+            pltpu.VMEM((len(slots), rows, depth), jnp.bfloat16),
+            pltpu.VMEM((rows, len(slots) * depth), jnp.bfloat16),
+            pltpu.VMEM((summed, depth, width), jnp.bfloat16),
+            pltpu.VMEM((summed, 2 * rows, depth), jnp.bfloat16),
+            pltpu.SemaphoreType.DMA((len(guests) + len(slots) + len(weights),)),
+        ],
+        cost_estimate=pl.CostEstimate(flops=flops, bytes_accessed=moved, transcendentals=0),
+        compiler_params=pltpu.CompilerParams(vmem_limit_bytes=60 * 2**20),
+        name="early_slots",
+    )(*args)
+
+
+def late_body(first, splits, before, last_rows, *refs):
+    pieces, refs = (refs[:4], refs[4:])
+    kept, (sent, wide, sems) = (refs[: len(splits)], refs[len(splits) :])
+    rows, width = sent.shape
+    pieces = [p if p.shape[1] == width else p.at[:, pl.ds(first, width)] for p in pieces]
+    for flight in started(piece_copies(pieces, wide, lax.axis_index("ctx")), sems, 0):
+        flight.wait()
+    at = 0
+    for own, columns in zip(kept, splits):
+        cols = slice(at, at + columns)
+        product = jnp.dot(last_rows[...], wide[:, cols], preferred_element_type=jnp.float32)
+        product = product + before[:, first + at : first + at + columns]
+        own[...] = product[:rows]
+        sent[:, cols] = product[rows:].astype(jnp.bfloat16)
+        at += columns
+
+
+def late_slot(first, splits, before, last_rows, pieces):
+    rows, depth = (last_rows.shape[0] // 2, last_rows.shape[1])
+    anywhere = pl.BlockSpec(memory_space=pl.ANY)
+    inside = pl.BlockSpec(memory_space=pltpu.VMEM)
+    width = sum(splits)
+    outs = [jax.ShapeDtypeStruct((rows, w), jnp.float32) for w in splits]
+    outs.append(jax.ShapeDtypeStruct((rows, width), jnp.bfloat16))
+    return pl.pallas_call(
+        functools.partial(late_body, first, splits),
+        out_shape=outs,
+        in_specs=[inside] * 2 + [anywhere] * 4,
+        out_specs=[inside] * len(outs),
+        scratch_shapes=[
+            pltpu.VMEM((depth, width), jnp.bfloat16),
+            pltpu.SemaphoreType.DMA((4,)),
+        ],
+        cost_estimate=pl.CostEstimate(
+            flops=4 * rows * depth * width, bytes_accessed=2 * depth * width, transcendentals=0
+        ),
+        compiler_params=pltpu.CompilerParams(vmem_limit_bytes=16 * 2**20),
+        name="late_slot",
+    )(before, last_rows, *pieces)
+
+
+def turned(tensor, cosine, sine_table):
+    half = tensor.shape[-1] // 2
+    return tensor * cosine + pltpu.roll(tensor, half, 1) * sine_table
+
+
+def key_value_body(sums, back, bias, cosine, sine_table, out):
+    head = out.shape[1] // 2
+    total = sums[...] + back[:, : 2 * head].astype(jnp.float32) + bias[...]
+    out[:, :head] = turned(total[:, :head], cosine[...], sine_table[...]).astype(jnp.bfloat16)
+    out[:, head:] = total[:, head:].astype(jnp.bfloat16)
+
+
+def attention_body(scale, first, sums, back, bias, cosine, sine_table, *refs):
+    blocks, refs = (refs[:4], refs[4:])
+    if first:
+        done, *refs = refs
+    out, keys, values = refs
+    rows = out.shape[0]
+    head = cosine.shape[1]
+    slab = lax.axis_index("ctx")
+    for block, flip in zip(blocks, (0, 1, 2, 3)):
+        row = pl.multiple_of(jnp.bitwise_xor(slab, flip) * rows, rows)
+        keys[pl.ds(row, rows), :] = block[:, :head]
+        values[pl.ds(row, rows), :] = block[:, head:]
+    total_keys = keys.shape[0]
+    row_ids = slab * rows + lax.broadcasted_iota(jnp.int32, (rows, total_keys), 0)
+    visible = lax.broadcasted_iota(jnp.int32, (rows, total_keys), 1) <= row_ids
+    if first:
+        out[:, :first] = done[...]
+    for at in range(0, sums.shape[1], head):
+        cols = pl.ds(at, head)
+        skipped = back.shape[1] - sums.shape[1]
+        query = sums[:, cols] + back[:, skipped + at : skipped + at + head].astype(jnp.float32)
+        query = query + bias[:, first + at : first + at + head]
+        query = turned(query, cosine[...], sine_table[...]).astype(jnp.bfloat16)
+        scores = lax.dot_general(
+            query, keys[...], (((1,), (1,)), ((), ())), preferred_element_type=jnp.float32
+        )
+        scores = jnp.where(visible, scores * scale, masked_score)
+        exps = jnp.exp(scores - jnp.max(scores, axis=1, keepdims=True))
+        length = jnp.sum(exps, axis=1, keepdims=True)
+        mixed = jnp.dot(exps.astype(jnp.bfloat16), values[...], preferred_element_type=jnp.float32)
+        out[:, first + at : first + at + head] = (mixed / length).astype(jnp.bfloat16)
+
+
+def attention(sums, back, bias, cosine, sine_table, blocks, done=None):
+    rows, width = sums.shape
+    head = cosine.shape[1]
+    first = 0 if done is None else done.shape[1]
+    inside = pl.BlockSpec(memory_space=pltpu.VMEM)
+    args = [sums, back, bias, cosine, sine_table, *blocks]
+    if first:
+        args.append(done)
+    total = 4 * rows * rows * (width // head)
+    return pl.pallas_call(
+        functools.partial(attention_body, head ** (-0.5), first),
+        out_shape=jax.ShapeDtypeStruct((rows, first + width), jnp.bfloat16),
+        in_specs=[inside] * len(args),
+        out_specs=inside,
+        scratch_shapes=[
+            pltpu.VMEM((4 * rows, head), jnp.bfloat16),
+            pltpu.VMEM((4 * rows, head), jnp.bfloat16),
+        ],
+        cost_estimate=pl.CostEstimate(
+            flops=4 * total * head, bytes_accessed=8 * rows * width, transcendentals=total
+        ),
+        compiler_params=pltpu.CompilerParams(vmem_limit_bytes=24 * 2**20),
+        name="attention",
+    )(*args)
+
+
+def planned(hidden, norm_gain, w_query, w_key, w_value, bias_query, bias_key, bias_value):
+    tokens = hidden[0]
+    rows = tokens.shape[0]
+    depth = w_query.shape[0]
+    head = w_key.shape[1]
+    line, slab = (lax.axis_index("line"), lax.axis_index("ctx"))
+    inner = (line == 1) | (line == 2)
+    swap = [(0, 1), (1, 0)]
+    ends = [(0, 1), (1, 0), (2, 3), (3, 2)]
+    middle = [(1, 2), (2, 1)]
+    outward = [(1, 0), (2, 3)]
+    across = [(i, i ^ 2) for i in range(4)]
+    beside = [(i, i ^ 1) for i in range(4)]
+    held = lax.optimization_barrier
+    cut = depth // 8
+    parts_1 = ((0, 0, depth), (1, 0, cut))
+    parts_2 = ((1, cut, 7 * cut), (2, 0, 5 * cut))
+    parts_3 = ((2, 5 * cut, 3 * cut), (3, 0, depth))
+    mine, sent_1 = pack(tokens, depth, (parts_1,), (w_key, w_value, w_query))
+    half = mine.shape[1] // 2
+    kv_width = 2 * head
+    second = lax.ppermute(mine, "line", ends)
+    third_in = lax.ppermute(mine, "line", middle)
+    fourth_in = lax.ppermute(second, "line", middle)
+    came_1 = lax.ppermute(sent_1, "pair", swap)
+    sent_2, sent_3, scale, line_scale = prepare(tokens, depth, (parts_2, parts_3))
+    came_scale = lax.ppermute(line_scale, "pair", swap)
+    gain = norm_gain.reshape(1, -1)
+    bias_kv = jnp.concatenate([bias_key, bias_value]).reshape(1, -1).astype(jnp.float32)
+    bias_q = bias_query.reshape(1, -1).astype(jnp.float32)
+    positions = slab * rows + jnp.arange(rows, dtype=jnp.int32)
+    cosine, sine_table = rotary_tables(positions, head)
+    cosine = jnp.concatenate([cosine, cosine], axis=-1).reshape(rows, head)
+    sine_table = jnp.concatenate([-sine_table, sine_table], axis=-1).reshape(rows, head)
+    small = (scale, came_scale, gain, bias_kv, bias_q, cosine, sine_table)
+    second, third_in, came_1, sent_2, sent_3, small = held(
+        (second, third_in, came_1, sent_2, sent_3, small)
+    )
+    scale, came_scale, gain, bias_kv, bias_q, cosine, sine_table = small
+    third_out = lax.ppermute(third_in, "line", outward)
+    second_far = lax.ppermute(second, "ctx", across)
+    came_2 = lax.ppermute(sent_2, "pair", swap)
+    second_side = lax.ppermute(second, "ctx", beside)
+    fourth_out = lax.ppermute(fourth_in, "line", outward)
+    third = jnp.where(inner, third_in, third_out)
+    third, second_far, came_2, second_side, sent_3 = held(
+        (third, second_far, came_2, second_side, sent_3)
+    )
+    third_far = lax.ppermute(third, "ctx", across)
+    came_3 = lax.ppermute(sent_3, "pair", swap)
+    second_corner = lax.ppermute(second_far, "ctx", beside)
+    third_side = lax.ppermute(third, "ctx", beside)
+    before = early_slots(
+        (0, 1),
+        ((0, 0, 9 * cut), (1, 0, 7 * cut)),
+        True,
+        False,
+        tokens,
+        (came_1, came_2),
+        scale,
+        came_scale,
+        gain,
+        [w_key, w_value, w_query, second, second_far, second_side, second_corner],
+    )[0]
+    fourth = jnp.where(inner, fourth_in, fourth_out)
+    fourth, third_far, came_3, third_side, before = held(
+        (fourth, third_far, came_3, third_side, before)
+    )
+    fourth_far_1 = lax.ppermute(fourth[:, :half], "ctx", across)
+    third_corner = lax.ppermute(third_far, "ctx", beside)
+    fourth_side = lax.ppermute(fourth, "ctx", beside)
+    before, last_rows = early_slots(
+        (2, 3),
+        ((0, 7 * cut, 5 * cut), (1, 0, 11 * cut)),
+        False,
+        True,
+        tokens,
+        (came_2, came_3),
+        scale,
+        came_scale,
+        gain,
+        [third, third_far, third_side, third_corner],
+        before,
+    )
+    fourth_far_1, fourth, before, last_rows, fourth_side = held(
+        (fourth_far_1, fourth, before, last_rows, fourth_side)
+    )
+    fourth_far_2 = lax.ppermute(fourth[:, half:], "ctx", across)
+    fourth_corner_1 = lax.ppermute(fourth_far_1, "ctx", beside)
+    kv_sums, q_sums_1, back_1 = late_slot(
+        0,
+        (kv_width, half - kv_width),
+        before,
+        last_rows,
+        (fourth, fourth_far_1, fourth_side, fourth_corner_1),
+    )
+    back_1, fourth_far_2 = held((back_1, fourth_far_2))
+    back_1 = lax.ppermute(back_1, "pair", swap)
+    fourth_corner_2 = lax.ppermute(fourth_far_2, "ctx", beside)
+    q_sums_2, back_2 = late_slot(
+        half,
+        (half,),
+        before,
+        last_rows,
+        (fourth, fourth_far_2, fourth_side, fourth_corner_2),
+    )
+    back_2 = lax.ppermute(back_2, "pair", swap)
+
+    inside = pl.BlockSpec(memory_space=pltpu.VMEM)
+    key_value = pl.pallas_call(
+        key_value_body,
+        out_shape=jax.ShapeDtypeStruct((rows, kv_width), jnp.bfloat16),
+        in_specs=[inside] * 5,
+        out_specs=inside,
+        name="key_value",
+    )(kv_sums, back_1, bias_kv, cosine, sine_table)
+    kv_across = lax.ppermute(key_value, "ctx", [(0, 2), (1, 3)])
+    kv_beside = lax.ppermute(key_value, "ctx", beside)
+    kv_corner = lax.ppermute(key_value, "ctx", [(0, 3), (1, 2)])
+    blocks = (key_value, kv_beside, kv_across, kv_corner)
+    attended = attention(q_sums_1, back_1, bias_q, cosine, sine_table, blocks)
+    attended = attention(q_sums_2, back_2, bias_q, cosine, sine_table, blocks, attended)
+    return attended[None]
+
+
 def shards(hidden, norm_gain, w_query, w_key, w_value, bias_query, bias_key, bias_value):
+    if lax.axis_size("line") == 4 and lax.axis_size("ctx") == 4:
+        return planned(
+            hidden, norm_gain, w_query, w_key, w_value, bias_query, bias_key, bias_value
+        )
     local_rows = hidden.shape[1]
     head_width = w_key.shape[1]
     query_width = w_query.shape[1]

time: 168 us -> 124 us (0.74)
  the two profiles are of different devices: /device:TPU:1 before, /device:TPU:11 now
where the time goes in v3:
time: 124 us
  waiting for transfers between devices  50.2 us (40%)
  Pallas kernels  32.2 us (26%)
  starting transfers between devices  28.8 us (23%)
  local copies, waits for them, and re-layouts  9 us (7%)
  other arithmetic  3.26 us (3%)
    pallas_call x2, Pallas kernels, early_slots(): pl.pallas_call(functools.partial(early_body, slots, guests, local, final)...  15.9 us
    ppermute x1, waiting for transfers between devices, planned(): came_1 = lax.ppermute(sent_1, 'pair', swap)  10.5 us
    unnamed x42, local copies, waits for them, and re-layouts  8.31 us
    ppermute x1, waiting for transfers between devices, planned(): fourth_in = lax.ppermute(second, 'line', middle)  8.17 us
    ppermute x1, waiting for transfers between devices, planned(): back_1 = lax.ppermute(back_1, 'pair', swap)  6.41 us
    pallas_call x2, Pallas kernels, attention(): pl.pallas_call(functools.partial(attention_body, head ** (-0.5), first),...  5.55 us
    ppermute x1, waiting for transfers between devices, planned(): kv_across = lax.ppermute(key_value, 'ctx', [(0, 2), (1, 3)])  4.44 us
    ppermute x1, starting transfers between devices, planned(): third_in = lax.ppermute(mine, 'line', middle)  4.32 us
  transfers between devices with their start and end apart: 25, of which 13 were waited for; matrix products, arithmetic and copies ran while one was open for 3% of the time, Pallas kernels for 21%

profile of v3, /device:TPU:11, one launch (start us, length us, event | category | flops | bytes accessed | tf_op | source)
XLA Modules:
  0.0 123.7 jit_solution(17388096498395782562)
XLA Ops:
  0.0 2.4 %pack.1 = (bf16[256,1280]{1,0:T(8,128)(2,1)}, bf16[256,1152]{1,0:T(8,128)(2,1)}) custom-call(bf16[256,8192]{1,0:T(8,128)(2,1)} %bitcast.11, bf16[1024,128]{1,0:T(8,128)(2,1)} %refs_5_.1, bf16[1024,128]{1,0:T(8,128)(2,1)} %refs_6_.1, bf16[1024,1024]{1,0:T(8,128)(2,1)} %refs_7_.1), custom_call_target="tpu_custom_call" | custom-call | bytes 2490368 | tf_op jit(solution)/shard_map/pack/pallas_call | solution.py:171
  2.7 4.3 %collective-permute-start.3 = (bf16[256,1280]{1,0:T(8,128)(2,1)}, bf16[256,1280]{1,0:T(8,128)(2,1)S(1)}, u32[]{:S(2)}, u32[]{:S(2)}) collective-permute-start(bf16[256,1280]{1,0:T(8,128)(2,1)} %get-tuple-element.47), channel_id=1, source_target_pairs={{8,16},{16,8},{9,17},{17,9},{10,18},{18,10},{11,19},{19,11},{12,20... | collective-permute-start | bytes 1966088 | tf_op jit(solution)/shard_map/ppermute | solution.py:485
  7.0 3.9 %prepare.1 = (bf16[256,1536]{1,0:T(8,128)(2,1)}, bf16[256,1408]{1,0:T(8,128)(2,1)}, f32[256,128]{1,0:T(8,128)}, f32[1,256]{1,0:T(1,128)}) custom-call(bf16[256,8192]{1,0:T(8,128)(2,1)} %bitcast.12), custom_call_target="tpu_custom_call" | custom-call | flops 4194304 | bytes 8388608 | tf_op jit(solution)/shard_map/prepare/pallas_call | solution.py:224
  10.9 1.3 %collective-permute-start.5 = (f32[1,256]{1,0:T(1,128)}, f32[1,256]{1,0:T(1,128)S(1)}, u32[]{:S(2)}, u32[]{:S(2)}) collective-permute-start(f32[1,256]{1,0:T(1,128)} %get-tuple-element.52), channel_id=1, source_target_pairs={{0,4},{4,0},{1,5},{5,1},{2,6},{6,2},{3,7},{7,3},{8,12},{12,8},{9,1... | collective-permute-start | bytes 3080 | tf_op jit(solution)/shard_map/ppermute | solution.py:489
  13.0 0.8 maximum_bitcast_fusion
  13.9 0.6 maximum_convert_fusion.bias
  14.4 0.6 reshape.176.refs_4_
  15.1 10.5 %collective-permute-done.4.refs_0_ = bf16[256,1152]{1,0:T(8,128)(2,1)S(1)} collective-permute-done((bf16[256,1152]{1,0:T(8,128)(2,1)S(1)}, bf16[256,1152]{1,0:T(8,128)(2,1)S(1)}, u32[]{:S(2)}, u32[]{:S(2)}) %collective-permute-start.4) | collective-permute-done | bytes 589856 | tf_op jit(solution)/shard_map/ppermute | solution.py:487
  25.6 2.2 %collective-permute-start.1 = (bf16[256,1280]{1,0:T(8,128)(2,1)}, bf16[256,1280]{1,0:T(8,128)(2,1)}, u32[]{:S(2)}, u32[]{:S(2)}) collective-permute-start(bf16[256,1280]{1,0:T(8,128)(2,1)} %collective-permute-done.refs_8_), channel_id=1, source_target_pairs={{8,16},{16,8},{9,17},{17,9},{10,18},{18,10},{11,19},{19,11},{12,20... | collective-permute-start | bytes 1966088 | tf_op jit(solution)/shard_map/ppermute | solution.py:486
  27.8 2.1 %collective-permute-start.6 = (bf16[256,1280]{1,0:T(8,128)(2,1)S(1)}, bf16[256,1280]{1,0:T(8,128)(2,1)}, u32[]{:S(2)}, u32[]{:S(2)}) collective-permute-start(bf16[256,1280]{1,0:T(8,128)(2,1)S(1)} %collective-permute-done.3), channel_id=1, source_target_pairs={{8,0},{16,24},{9,1},{17,25},{10,2},{18,26},{11,3},{19,27},{12,4},{... | collective-permute-start | bytes 1966088 | tf_op jit(solution)/shard_map/ppermute | solution.py:502
  30.4 3.0 %collective-permute-start.9 = (bf16[256,1280]{1,0:T(8,128)(2,1)}, bf16[256,1280]{1,0:T(8,128)(2,1)}, u32[]{:S(2)}, u32[]{:S(2)}) collective-permute-start(bf16[256,1280]{1,0:T(8,128)(2,1)} %collective-permute-done.refs_8_), channel_id=1, source_target_pairs={{0,1},{1,0},{2,3},{3,2},{4,5},{5,4},{6,7},{7,6},{8,9},{9,8},{10,11... | collective-permute-start | bytes 1966088 | tf_op jit(solution)/shard_map/ppermute | solution.py:505
  33.4 8.2 %collective-permute-done.1 = bf16[256,1280]{1,0:T(8,128)(2,1)} collective-permute-done((bf16[256,1280]{1,0:T(8,128)(2,1)}, bf16[256,1280]{1,0:T(8,128)(2,1)}, u32[]{:S(2)}, u32[]{:S(2)}) %collective-permute-start.1) | collective-permute-done | bytes 655392 | tf_op jit(solution)/shard_map/ppermute | solution.py:486
  41.6 1.3 %collective-permute-start.2 = (bf16[256,1280]{1,0:T(8,128)(2,1)}, bf16[256,1280]{1,0:T(8,128)(2,1)S(1)}, u32[]{:S(2)}, u32[]{:S(2)}) collective-permute-start(bf16[256,1280]{1,0:T(8,128)(2,1)} %collective-permute-done.1), channel_id=1, source_target_pairs={{8,0},{16,24},{9,1},{17,25},{10,2},{18,26},{11,3},{19,27},{12,4},{... | collective-permute-start | bytes 1966088 | tf_op jit(solution)/shard_map/ppermute | solution.py:506
  43.0 1.0 collective-permute-done.7.refs_9_
  44.0 2.9 %collective-permute-done.8.refs_1_.refs_0_ = bf16[256,1536]{1,0:T(8,128)(2,1)S(1)} collective-permute-done((bf16[256,1536]{1,0:T(8,128)(2,1)}, bf16[256,1536]{1,0:T(8,128)(2,1)S(1)}, u32[]{:S(2)}, u32[]{:S(2)}) %collective-permute-start.8) | collective-permute-done | bytes 786464 | tf_op jit(solution)/shard_map/ppermute | solution.py:504
  46.8 3.2 %collective-permute-start.13 = (bf16[256,1280]{1,0:T(8,128)(2,1)}, bf16[256,1280]{1,0:T(8,128)(2,1)}, u32[]{:S(2)}, u32[]{:S(2)}) collective-permute-start(bf16[256,1280]{1,0:T(8,128)(2,1)} %collective-permute-done.7.refs_9_), channel_id=1, source_target_pairs={{0,1},{1,0},{2,3},{3,2},{4,5},{5,4},{6,7},{7,6},{8,9},{9,8},{10,11... | collective-permute-start | bytes 1966088 | tf_op jit(solution)/shard_map/ppermute | solution.py:513
  50.9 3.4 %collective-permute-done.2 = bf16[256,1280]{1,0:T(8,128)(2,1)S(1)} collective-permute-done((bf16[256,1280]{1,0:T(8,128)(2,1)}, bf16[256,1280]{1,0:T(8,128)(2,1)S(1)}, u32[]{:S(2)}, u32[]{:S(2)}) %collective-permute-start.2) | collective-permute-done | bytes 655392 | tf_op jit(solution)/shard_map/ppermute | solution.py:506
  54.2 1.2 broadcast_select_fusion.1.refs_0_
  55.4 8.3 %early_slots.2.refs_9_ = f32[512,1280]{1,0:T(8,128)} custom-call(bf16[256,8192]{1,0:T(8,128)(2,1)} %bitcast.13, bf16[256,1152]{1,0:T(8,128)(2,1)} %copy-done.13, bf16[256,1536]{1,0:T(8,128)(2,1)} %copy-done.9, f32[256,128]{1,0:T(8,128)} %get-tuple-element.61.refs_2_, f32[1,256]{1,0:T(1,128)} %copy-done.15, bf16[1,8192]{1,0:T(2,128)(2,1)} %reshape.176.refs_4_, ...), custom_call_target="tpu_custom_call" | custom-call | flops 2684354560 | bytes 9961472 | tf_op jit(solution)/shard_map/early_slots/pallas_call | solution.py:333
  63.8 2.8 %collective-permute-done.10.refs_6_ = bf16[256,1280]{1,0:T(8,128)(2,1)} collective-permute-done((bf16[256,1280]{1,0:T(8,128)(2,1)S(1)}, bf16[256,1280]{1,0:T(8,128)(2,1)}, u32[]{:S(2)}, u32[]{:S(2)}) %collective-permute-start.10) | collective-permute-done | bytes 655392 | tf_op jit(solution)/shard_map/ppermute | solution.py:511
  66.6 1.6 %collective-permute-done.11.refs_1_ = bf16[256,1408]{1,0:T(8,128)(2,1)S(1)} collective-permute-done((bf16[256,1408]{1,0:T(8,128)(2,1)S(1)}, bf16[256,1408]{1,0:T(8,128)(2,1)S(1)}, u32[]{:S(2)}, u32[]{:S(2)}) %collective-permute-start.11) | collective-permute-done | bytes 720928 | tf_op jit(solution)/shard_map/ppermute | solution.py:512
  68.1 0.9 copy-done.11
  69.1 1.0 collective-permute-start.15
  70.2 1.3 %collective-permute-start.14 = (bf16[256,640]{1,0:T(8,128)(2,1)S(1)}, bf16[256,640]{1,0:T(8,128)(2,1)S(1)}, u32[]{:S(2)}, u32[]{:S(2)}) collective-permute-start(bf16[256,640]{1,0:T(8,128)(2,1)S(1)} %slice.6), channel_id=1, source_target_pairs={{0,2},{1,3},{2,0},{3,1},{4,6},{5,7},{6,4},{7,5},{8,10},{9,11},{10,... | collective-permute-start | bytes 983048 | tf_op jit(solution)/shard_map/ppermute | solution.py:531
  71.4 1.5 %collective-permute-done.15.refs_8_ = bf16[256,1280]{1,0:T(8,128)(2,1)S(1)} collective-permute-done((bf16[256,1280]{1,0:T(8,128)(2,1)}, bf16[256,1280]{1,0:T(8,128)(2,1)S(1)}, u32[]{:S(2)}, u32[]{:S(2)}) %collective-permute-start.15) | collective-permute-done | bytes 655392 | tf_op jit(solution)/shard_map/ppermute | solution.py:532
  73.0 0.8 copy-done.12
  73.8 7.5 %early_slots.3 = (f32[512,1280]{1,0:T(8,128)}, bf16[512,1024]{1,0:T(8,128)(2,1)}) custom-call(bf16[256,8192]{1,0:T(8,128)(2,1)} %bitcast.14, bf16[256,1536]{1,0:T(8,128)(2,1)} %copy-done.9, bf16[256,1408]{1,0:T(8,128)(2,1)} %copy-done.11, f32[256,128]{1,0:T(8,128)} %get-tuple-element.61.refs_2_, f32[1,256]{1,0:T(1,128)} %copy-done.15, ...), custom_call_target="tpu_custom_call" | custom-call | flops 1342177280 | bytes 7340032 | tf_op jit(solution)/shard_map/early_slots/pallas_call | solution.py:333
  81.8 1.3 %collective-permute-start.18 = (bf16[256,640]{1,0:T(8,128)(2,1)S(1)}, bf16[256,640]{1,0:T(8,128)(2,1)S(1)}, u32[]{:S(2)}, u32[]{:S(2)}) collective-permute-start(bf16[256,640]{1,0:T(8,128)(2,1)S(1)} %slice.7), channel_id=1, source_target_pairs={{0,2},{1,3},{2,0},{3,1},{4,6},{5,7},{6,4},{7,5},{8,10},{9,11},{10,... | collective-permute-start | bytes 983048 | tf_op jit(solution)/shard_map/ppermute | solution.py:550
  83.1 1.7 %copy-done = f32[512,1280]{1,0:T(8,128)S(1)} copy-done((f32[512,1280]{1,0:T(8,128)S(1)}, f32[512,1280]{1,0:T(8,128)}, u32[]{:S(2)}) %copy-start) | copy-done | bytes 2621464
  84.9 1.2 copy-done.1
  86.1 1.3 %late_slot.2 = (f32[256,256]{1,0:T(8,128)S(1)}, f32[256,384]{1,0:T(8,128)S(1)}, bf16[256,640]{1,0:T(8,128)(2,1)S(1)}) custom-call(f32[512,1280]{1,0:T(8,128)S(1)} %copy-done, bf16[512,1024]{1,0:T(8,128)(2,1)S(1)} %copy-done.1, bf16[256,1280]{1,0:T(8,128)(2,1)S(1)} %broadcast_select_fusion.1.refs_0_, bf16[256,640]{1,0:T(8,128)(2,1)S(1)} %collective-permute-done.14.refs_1_, ...), custom_call_target="tpu_custom_call" | custom-call | flops 671088640 | bytes 1310720 | tf_op jit(solution)/shard_map/late_slot/pallas_call | solution.py:375
  87.4 3.7 %collective-permute-done.18.refs_1_ = bf16[256,640]{1,0:T(8,128)(2,1)S(1)} collective-permute-done((bf16[256,640]{1,0:T(8,128)(2,1)S(1)}, bf16[256,640]{1,0:T(8,128)(2,1)S(1)}, u32[]{:S(2)}, u32[]{:S(2)}) %collective-permute-start.18) | collective-permute-done | bytes 327712 | tf_op jit(solution)/shard_map/ppermute | solution.py:550
  91.1 1.0 collective-permute-start.19
  92.3 1.0 collective-permute-done.19.refs_3_
  93.3 1.3 %late_slot.3 = (f32[256,640]{1,0:T(8,128)S(1)}, bf16[256,640]{1,0:T(8,128)(2,1)S(1)}) custom-call(f32[512,1280]{1,0:T(8,128)S(1)} %copy-done, bf16[512,1024]{1,0:T(8,128)(2,1)S(1)} %copy-done.1, bf16[256,1280]{1,0:T(8,128)(2,1)S(1)} %broadcast_select_fusion.1.refs_0_, bf16[256,640]{1,0:T(8,128)(2,1)S(1)} %collective-permute-done.18.refs_1_, ...), custom_call_target="tpu_custom_call" | custom-call | flops 671088640 | bytes 1310720 | tf_op jit(solution)/shard_map/late_slot/pallas_call | solution.py:375
  94.9 6.4 %collective-permute-done.21.back = bf16[256,640]{1,0:T(8,128)(2,1)S(1)} collective-permute-done((bf16[256,640]{1,0:T(8,128)(2,1)S(1)}, bf16[256,640]{1,0:T(8,128)(2,1)S(1)}, u32[]{:S(2)}, u32[]{:S(2)}) %collective-permute-start.21) | collective-permute-done | bytes 327712 | tf_op jit(solution)/shard_map/ppermute | solution.py:560
  101.3 0.7 copy-done.4
  102.0 1.9 %key_value.1.refs_0_ = bf16[256,256]{1,0:T(8,128)(2,1)} custom-call(f32[256,256]{1,0:T(8,128)} %copy-done.8, bf16[256,640]{1,0:T(8,128)(2,1)} %copy-done.4, f32[1,256]{1,0:T(1,128)} %maximum_convert_fusion.bias, f32[256,128]{1,0:T(8,128)} %get-tuple-element.83.cosine, f32[256,128]{1,0:T(8,128)} %get-tuple-element.84.sine_table), custom_call_target="tpu_custom_call" | custom-call | tf_op jit(solution)/shard_map/key_value/pallas_call | solution.py:572
  103.9 1.3 %collective-permute-start.22 = (bf16[256,256]{1,0:T(8,128)(2,1)}, bf16[256,256]{1,0:T(8,128)(2,1)S(1)}, u32[]{:S(2)}, u32[]{:S(2)}) collective-permute-start(bf16[256,256]{1,0:T(8,128)(2,1)} %key_value.1.refs_0_), channel_id=1, source_target_pairs={{0,1},{1,0},{2,3},{3,2},{4,5},{5,4},{6,7},{7,6},{8,9},{9,8},{10,11... | collective-permute-start | bytes 393224 | tf_op jit(solution)/shard_map/ppermute | solution.py:580
  105.2 1.3 %collective-permute-start.23 = (bf16[256,256]{1,0:T(8,128)(2,1)}, bf16[256,256]{1,0:T(8,128)(2,1)S(1)}, u32[]{:S(2)}, u32[]{:S(2)}) collective-permute-start(bf16[256,256]{1,0:T(8,128)(2,1)} %key_value.1.refs_0_), channel_id=1, source_target_pairs={{0,2},{1,3},{4,6},{5,7},{8,10},{9,11},{12,14},{13,15},{16,18},{17,... | collective-permute-start | bytes 393224 | tf_op jit(solution)/shard_map/ppermute | solution.py:579
  106.5 1.5 %collective-permute-start.24 = (bf16[256,256]{1,0:T(8,128)(2,1)}, bf16[256,256]{1,0:T(8,128)(2,1)S(1)}, u32[]{:S(2)}, u32[]{:S(2)}) collective-permute-start(bf16[256,256]{1,0:T(8,128)(2,1)} %key_value.1.refs_0_), channel_id=1, source_target_pairs={{0,3},{1,2},{4,7},{5,6},{8,11},{9,10},{12,15},{13,14},{16,19},{17,... | collective-permute-start | bytes 393224 | tf_op jit(solution)/shard_map/ppermute | solution.py:581
  108.0 4.4 %collective-permute-done.23.refs_2_ = bf16[256,256]{1,0:T(8,128)(2,1)S(1)} collective-permute-done((bf16[256,256]{1,0:T(8,128)(2,1)}, bf16[256,256]{1,0:T(8,128)(2,1)S(1)}, u32[]{:S(2)}, u32[]{:S(2)}) %collective-permute-start.23) | collective-permute-done | bytes 131104 | tf_op jit(solution)/shard_map/ppermute | solution.py:579
  112.5 2.9 %collective-permute-done.24.refs_3_ = bf16[256,256]{1,0:T(8,128)(2,1)S(1)} collective-permute-done((bf16[256,256]{1,0:T(8,128)(2,1)}, bf16[256,256]{1,0:T(8,128)(2,1)S(1)}, u32[]{:S(2)}, u32[]{:S(2)}) %collective-permute-start.24) | collective-permute-done | bytes 131104 | tf_op jit(solution)/shard_map/ppermute | solution.py:581
  115.4 1.0 copy-done.5
  116.3 0.9 copy-done.6
  117.2 1.9 %attention.2.refs_4_ = bf16[256,384]{1,0:T(8,128)(2,1)S(1)} custom-call(f32[256,384]{1,0:T(8,128)S(1)} %get-tuple-element.88.sums, bf16[256,640]{1,0:T(8,128)(2,1)S(1)} %copy-done.5, f32[1,1024]{1,0:T(1,128)S(1)} %bitcast.9, f32[256,128]{1,0:T(8,128)S(1)} %copy-done.2, f32[256,128]{1,0:T(8,128)S(1)} %copy-done.3, bf16[256,256]{1,0:T(8,128)(2,1)S(1)} %copy-done.6, ...), custom_call_target="tpu_custom_call" | custom-call | flops 402653184 | bytes 786432 | tf_op jit(solution)/shard_map/attention/pallas_call | solution.py:446
  119.2 0.9 copy-done.7
  120.1 3.7 %attention.3 = bf16[256,1024]{1,0:T(8,128)(2,1)} custom-call(f32[256,640]{1,0:T(8,128)S(1)} %get-tuple-element.80.sums, bf16[256,640]{1,0:T(8,128)(2,1)S(1)} %collective-permute-done.20.back, f32[1,1024]{1,0:T(1,128)S(1)} %bitcast.10, f32[256,128]{1,0:T(8,128)S(1)} %copy-done.2, f32[256,128]{1,0:T(8,128)S(1)} %copy-done.3, bf16[256,256]{1,0:T(8,128)(2,1)S(1)} %copy-done.7, ...), custom_call_target="tpu_custom_call" | custom-call | flops 671088640 | bytes 1310720 | tf_op jit(solution)/shard_map/attention/pallas_call | solution.py:446
  (64 shorter events, 3.5 us)
Async XLA Ops:
  2.4 9.8 %copy-start.20 = (bf16[256,1152]{1,0:T(8,128)(2,1)S(1)}, bf16[256,1152]{1,0:T(8,128)(2,1)}, u32[]{:S(2)}) copy-start(bf16[256,1152]{1,0:T(8,128)(2,1)} %get-tuple-element.48) | copy-start | bytes 1769476
  2.4 11.5 %copy-start.17 = (bf16[128]{0:T(256)(128)(2,1)S(1)}, bf16[128]{0:T(256)(128)(2,1)}, u32[]{:S(2)}) copy-start(bf16[128]{0:T(256)(128)(2,1)} %param.15) | copy-start | bytes 772
  2.4 11.4 %copy-start.18 = (bf16[128]{0:T(256)(128)(2,1)S(1)}, bf16[128]{0:T(256)(128)(2,1)}, u32[]{:S(2)}) copy-start(bf16[128]{0:T(256)(128)(2,1)} %param.14) | copy-start | bytes 772
  2.4 12.0 %copy-start.14 = (bf16[8192]{0:T(1024)(128)(2,1)S(1)}, bf16[8192]{0:T(1024)(128)(2,1)}, u32[]{:S(2)}) copy-start(bf16[8192]{0:T(1024)(128)(2,1)} %param.9) | copy-start | bytes 49156
  2.4 12.6 %copy-start.16 = (bf16[1024]{0:T(1024)(128)(2,1)S(1)}, bf16[1024]{0:T(1024)(128)(2,1)}, u32[]{:S(2)}) copy-start(bf16[1024]{0:T(1024)(128)(2,1)} %param.13) | copy-start | bytes 6148
  2.4 23.1 %collective-permute-start = (bf16[256,1280]{1,0:T(8,128)(2,1)}, bf16[256,1280]{1,0:T(8,128)(2,1)}, u32[]{:S(2)}, u32[]{:S(2)}) collective-permute-start(bf16[256,1280]{1,0:T(8,128)(2,1)} %get-tuple-element.47), channel_id=1, source_target_pairs={{0,8},{8,0},{16,24},{24,16},{1,9},{9,1},{17,25},{25,17},{2,10},{10... | collective-permute-start | bytes 1966088 | tf_op jit(solution)/shard_map/ppermute | solution.py:484
  2.7 22.9 %collective-permute-start.3 = (bf16[256,1280]{1,0:T(8,128)(2,1)}, bf16[256,1280]{1,0:T(8,128)(2,1)S(1)}, u32[]{:S(2)}, u32[]{:S(2)}) collective-permute-start(bf16[256,1280]{1,0:T(8,128)(2,1)} %get-tuple-element.47), channel_id=1, source_target_pairs={{8,16},{16,8},{9,17},{17,9},{10,18},{18,10},{11,19},{19,11},{12,20... | collective-permute-start | bytes 1966088 | tf_op jit(solution)/shard_map/ppermute | solution.py:485
  10.9 39.7 %copy-start.19 = (bf16[256,1408]{1,0:T(8,128)(2,1)S(1)}, bf16[256,1408]{1,0:T(8,128)(2,1)}, u32[]{:S(2)}) copy-start(bf16[256,1408]{1,0:T(8,128)(2,1)} %get-tuple-element.58) | copy-start | bytes 2162692
  10.9 4.2 %collective-permute-start.5 = (f32[1,256]{1,0:T(1,128)}, f32[1,256]{1,0:T(1,128)S(1)}, u32[]{:S(2)}, u32[]{:S(2)}) collective-permute-start(f32[1,256]{1,0:T(1,128)} %get-tuple-element.52), channel_id=1, source_target_pairs={{0,4},{4,0},{1,5},{5,1},{2,6},{6,2},{3,7},{7,3},{8,12},{12,8},{9,1... | collective-permute-start | bytes 3080 | tf_op jit(solution)/shard_map/ppermute | solution.py:489
  12.2 13.3 %collective-permute-start.4 = (bf16[256,1152]{1,0:T(8,128)(2,1)S(1)}, bf16[256,1152]{1,0:T(8,128)(2,1)S(1)}, u32[]{:S(2)}, u32[]{:S(2)}) collective-permute-start(bf16[256,1152]{1,0:T(8,128)(2,1)S(1)} %copy-done.20), channel_id=1, source_target_pairs={{0,4},{4,0},{1,5},{5,1},{2,6},{6,2},{3,7},{7,3},{8,12},{12,8},{9,1... | collective-permute-start | bytes 1769480 | tf_op jit(solution)/shard_map/ppermute | solution.py:487
  15.1 40.3 %copy-start.15 = (f32[1,256]{1,0:T(1,128)}, f32[1,256]{1,0:T(1,128)S(1)}, u32[]{:S(2)}) copy-start(f32[1,256]{1,0:T(1,128)S(1)} %collective-permute-done.5.refs_3_) | copy-start | bytes 3076
  25.5 2.2 %copy-start.13 = (bf16[256,1152]{1,0:T(8,128)(2,1)}, bf16[256,1152]{1,0:T(8,128)(2,1)S(1)}, u32[]{:S(2)}) copy-start(bf16[256,1152]{1,0:T(8,128)(2,1)S(1)} %collective-permute-done.4.refs_0_) | copy-start | bytes 1769476
  25.6 16.0 %collective-permute-start.1 = (bf16[256,1280]{1,0:T(8,128)(2,1)}, bf16[256,1280]{1,0:T(8,128)(2,1)}, u32[]{:S(2)}, u32[]{:S(2)}) collective-permute-start(bf16[256,1280]{1,0:T(8,128)(2,1)} %collective-permute-done.refs_8_), channel_id=1, source_target_pairs={{8,16},{16,8},{9,17},{17,9},{10,18},{18,10},{11,19},{19,11},{12,20... | collective-permute-start | bytes 1966088 | tf_op jit(solution)/shard_map/ppermute | solution.py:486
  27.8 15.1 %collective-permute-start.6 = (bf16[256,1280]{1,0:T(8,128)(2,1)S(1)}, bf16[256,1280]{1,0:T(8,128)(2,1)}, u32[]{:S(2)}, u32[]{:S(2)}) collective-permute-start(bf16[256,1280]{1,0:T(8,128)(2,1)S(1)} %collective-permute-done.3), channel_id=1, source_target_pairs={{8,0},{16,24},{9,1},{17,25},{10,2},{18,26},{11,3},{19,27},{12,4},{... | collective-permute-start | bytes 1966088 | tf_op jit(solution)/shard_map/ppermute | solution.py:502
  29.9 16.9 %collective-permute-start.8 = (bf16[256,1536]{1,0:T(8,128)(2,1)}, bf16[256,1536]{1,0:T(8,128)(2,1)S(1)}, u32[]{:S(2)}, u32[]{:S(2)}) collective-permute-start(bf16[256,1536]{1,0:T(8,128)(2,1)} %get-tuple-element.55), channel_id=1, source_target_pairs={{0,4},{4,0},{1,5},{5,1},{2,6},{6,2},{3,7},{7,3},{8,12},{12,8},{9,1... | collective-permute-start | bytes 2359304 | tf_op jit(solution)/shard_map/ppermute | solution.py:504
  30.1 13.8 %collective-permute-start.7 = (bf16[256,1280]{1,0:T(8,128)(2,1)}, bf16[256,1280]{1,0:T(8,128)(2,1)}, u32[]{:S(2)}, u32[]{:S(2)}) collective-permute-start(bf16[256,1280]{1,0:T(8,128)(2,1)} %collective-permute-done.refs_8_), channel_id=1, source_target_pairs={{0,2},{1,3},{2,0},{3,1},{4,6},{5,7},{6,4},{7,5},{8,10},{9,11},{10,... | collective-permute-start | bytes 1966088 | tf_op jit(solution)/shard_map/ppermute | solution.py:503
  30.4 13.6 %collective-permute-start.9 = (bf16[256,1280]{1,0:T(8,128)(2,1)}, bf16[256,1280]{1,0:T(8,128)(2,1)}, u32[]{:S(2)}, u32[]{:S(2)}) collective-permute-start(bf16[256,1280]{1,0:T(8,128)(2,1)} %collective-permute-done.refs_8_), channel_id=1, source_target_pairs={{0,1},{1,0},{2,3},{3,2},{4,5},{5,4},{6,7},{7,6},{8,9},{9,8},{10,11... | collective-permute-start | bytes 1966088 | tf_op jit(solution)/shard_map/ppermute | solution.py:505
  41.6 12.7 %collective-permute-start.2 = (bf16[256,1280]{1,0:T(8,128)(2,1)}, bf16[256,1280]{1,0:T(8,128)(2,1)S(1)}, u32[]{:S(2)}, u32[]{:S(2)}) collective-permute-start(bf16[256,1280]{1,0:T(8,128)(2,1)} %collective-permute-done.1), channel_id=1, source_target_pairs={{8,0},{16,24},{9,1},{17,25},{10,2},{18,26},{11,3},{19,27},{12,4},{... | collective-permute-start | bytes 1966088 | tf_op jit(solution)/shard_map/ppermute | solution.py:506
  43.0 20.8 %copy-start.10 = (bf16[256,1280]{1,0:T(8,128)(2,1)}, bf16[256,1280]{1,0:T(8,128)(2,1)S(1)}, u32[]{:S(2)}) copy-start(bf16[256,1280]{1,0:T(8,128)(2,1)S(1)} %broadcast_select_fusion.refs_5_) | copy-start | bytes 1966084
  46.8 8.6 %copy-start.9 = (bf16[256,1536]{1,0:T(8,128)(2,1)}, bf16[256,1536]{1,0:T(8,128)(2,1)S(1)}, u32[]{:S(2)}) copy-start(bf16[256,1536]{1,0:T(8,128)(2,1)S(1)} %collective-permute-done.8.refs_1_.refs_0_) | copy-start | bytes 2359300
  46.8 8.6 %collective-permute-start.13 = (bf16[256,1280]{1,0:T(8,128)(2,1)}, bf16[256,1280]{1,0:T(8,128)(2,1)}, u32[]{:S(2)}, u32[]{:S(2)}) collective-permute-start(bf16[256,1280]{1,0:T(8,128)(2,1)} %collective-permute-done.7.refs_9_), channel_id=1, source_target_pairs={{0,1},{1,0},{2,3},{3,2},{4,5},{5,4},{6,7},{7,6},{8,9},{9,8},{10,11... | collective-permute-start | bytes 1966088 | tf_op jit(solution)/shard_map/ppermute | solution.py:513
  50.1 16.5 %collective-permute-start.10 = (bf16[256,1280]{1,0:T(8,128)(2,1)S(1)}, bf16[256,1280]{1,0:T(8,128)(2,1)}, u32[]{:S(2)}, u32[]{:S(2)}) collective-permute-start(bf16[256,1280]{1,0:T(8,128)(2,1)S(1)} %broadcast_select_fusion.refs_5_), channel_id=1, source_target_pairs={{0,2},{1,3},{2,0},{3,1},{4,6},{5,7},{6,4},{7,5},{8,10},{9,11},{10,... | collective-permute-start | bytes 1966088 | tf_op jit(solution)/shard_map/ppermute | solution.py:511
  50.3 16.2 %collective-permute-start.12 = (bf16[256,1280]{1,0:T(8,128)(2,1)S(1)}, bf16[256,1280]{1,0:T(8,128)(2,1)}, u32[]{:S(2)}, u32[]{:S(2)}) collective-permute-start(bf16[256,1280]{1,0:T(8,128)(2,1)S(1)} %broadcast_select_fusion.refs_5_), channel_id=1, source_target_pairs={{0,1},{1,0},{2,3},{3,2},{4,5},{5,4},{6,7},{7,6},{8,9},{9,8},{10,11... | collective-permute-start | bytes 1966088 | tf_op jit(solution)/shard_map/ppermute | solution.py:514
  50.6 17.5 %collective-permute-start.11 = (bf16[256,1408]{1,0:T(8,128)(2,1)S(1)}, bf16[256,1408]{1,0:T(8,128)(2,1)S(1)}, u32[]{:S(2)}, u32[]{:S(2)}) collective-permute-start(bf16[256,1408]{1,0:T(8,128)(2,1)S(1)} %copy-done.19), channel_id=1, source_target_pairs={{0,4},{4,0},{1,5},{5,1},{2,6},{6,2},{3,7},{7,3},{8,12},{12,8},{9,1... | collective-permute-start | bytes 2162696 | tf_op jit(solution)/shard_map/ppermute | solution.py:512
  68.1 0.9 copy-start.11
  69.1 3.9 %collective-permute-start.15 = (bf16[256,1280]{1,0:T(8,128)(2,1)}, bf16[256,1280]{1,0:T(8,128)(2,1)S(1)}, u32[]{:S(2)}, u32[]{:S(2)}) collective-permute-start(bf16[256,1280]{1,0:T(8,128)(2,1)} %collective-permute-done.10.refs_6_), channel_id=1, source_target_pairs={{0,1},{1,0},{2,3},{3,2},{4,5},{5,4},{6,7},{7,6},{8,9},{9,8},{10,11... | collective-permute-start | bytes 1966088 | tf_op jit(solution)/shard_map/ppermute | solution.py:532
  70.1 11.2 %collective-permute-start.16 = (bf16[256,1280]{1,0:T(8,128)(2,1)S(1)}, bf16[256,1280]{1,0:T(8,128)(2,1)S(1)}, u32[]{:S(2)}, u32[]{:S(2)}) collective-permute-start(bf16[256,1280]{1,0:T(8,128)(2,1)S(1)} %broadcast_select_fusion.1.refs_0_), channel_id=1, source_target_pairs={{0,1},{1,0},{2,3},{3,2},{4,5},{5,4},{6,7},{7,6},{8,9},{9,8},{10,11... | collective-permute-start | bytes 1966088 | tf_op jit(solution)/shard_map/ppermute | solution.py:533
  70.2 11.2 %collective-permute-start.14 = (bf16[256,640]{1,0:T(8,128)(2,1)S(1)}, bf16[256,640]{1,0:T(8,128)(2,1)S(1)}, u32[]{:S(2)}, u32[]{:S(2)}) collective-permute-start(bf16[256,640]{1,0:T(8,128)(2,1)S(1)} %slice.6), channel_id=1, source_target_pairs={{0,2},{1,3},{2,0},{3,1},{4,6},{5,7},{6,4},{7,5},{8,10},{9,11},{10,... | collective-permute-start | bytes 983048 | tf_op jit(solution)/shard_map/ppermute | solution.py:531
  73.0 0.8 copy-start.12
  81.4 1.7 %collective-permute-start.17 = (bf16[256,640]{1,0:T(8,128)(2,1)S(1)}, bf16[256,640]{1,0:T(8,128)(2,1)S(1)}, u32[]{:S(2)}, u32[]{:S(2)}) collective-permute-start(bf16[256,640]{1,0:T(8,128)(2,1)S(1)} %collective-permute-done.14.refs_1_), channel_id=1, source_target_pairs={{0,1},{1,0},{2,3},{3,2},{4,5},{5,4},{6,7},{7,6},{8,9},{9,8},{10,11... | collective-permute-start | bytes 983048 | tf_op jit(solution)/shard_map/ppermute | solution.py:551
  81.8 9.2 %collective-permute-start.18 = (bf16[256,640]{1,0:T(8,128)(2,1)S(1)}, bf16[256,640]{1,0:T(8,128)(2,1)S(1)}, u32[]{:S(2)}, u32[]{:S(2)}) collective-permute-start(bf16[256,640]{1,0:T(8,128)(2,1)S(1)} %slice.7), channel_id=1, source_target_pairs={{0,2},{1,3},{2,0},{3,1},{4,6},{5,7},{6,4},{7,5},{8,10},{9,11},{10,... | collective-permute-start | bytes 983048 | tf_op jit(solution)/shard_map/ppermute | solution.py:550
  83.1 1.7 %copy-start = (f32[512,1280]{1,0:T(8,128)S(1)}, f32[512,1280]{1,0:T(8,128)}, u32[]{:S(2)}) copy-start(f32[512,1280]{1,0:T(8,128)} %get-tuple-element.73.before) | copy-start | bytes 7864324
  84.9 1.2 copy-start.1
  87.4 7.2 %copy-start.8 = (f32[256,256]{1,0:T(8,128)}, f32[256,256]{1,0:T(8,128)S(1)}, u32[]{:S(2)}) copy-start(f32[256,256]{1,0:T(8,128)S(1)} %get-tuple-element.85.sums) | copy-start | bytes 786436
  91.1 24.3 %copy-start.2 = (f32[256,128]{1,0:T(8,128)S(1)}, f32[256,128]{1,0:T(8,128)}, u32[]{:S(2)}) copy-start(f32[256,128]{1,0:T(8,128)} %get-tuple-element.83.cosine) | copy-start | bytes 393220
  91.1 24.3 %copy-start.3 = (f32[256,128]{1,0:T(8,128)S(1)}, f32[256,128]{1,0:T(8,128)}, u32[]{:S(2)}) copy-start(f32[256,128]{1,0:T(8,128)} %get-tuple-element.84.sine_table) | copy-start | bytes 393220
  91.1 2.2 %collective-permute-start.19 = (bf16[256,640]{1,0:T(8,128)(2,1)S(1)}, bf16[256,640]{1,0:T(8,128)(2,1)S(1)}, u32[]{:S(2)}, u32[]{:S(2)}) collective-permute-start(bf16[256,640]{1,0:T(8,128)(2,1)S(1)} %collective-permute-done.18.refs_1_), channel_id=1, source_target_pairs={{0,1},{1,0},{2,3},{3,2},{4,5},{5,4},{6,7},{7,6},{8,9},{9,8},{10,11... | collective-permute-start | bytes 983048 | tf_op jit(solution)/shard_map/ppermute | solution.py:561
  92.0 9.3 %collective-permute-start.21 = (bf16[256,640]{1,0:T(8,128)(2,1)S(1)}, bf16[256,640]{1,0:T(8,128)(2,1)S(1)}, u32[]{:S(2)}, u32[]{:S(2)}) collective-permute-start(bf16[256,640]{1,0:T(8,128)(2,1)S(1)} %get-tuple-element.86), channel_id=1, source_target_pairs={{0,4},{4,0},{1,5},{5,1},{2,6},{6,2},{3,7},{7,3},{8,12},{12,8},{9,1... | collective-permute-start | bytes 983048 | tf_op jit(solution)/shard_map/ppermute | solution.py:560
  94.6 24.5 %collective-permute-start.20 = (bf16[256,640]{1,0:T(8,128)(2,1)S(1)}, bf16[256,640]{1,0:T(8,128)(2,1)S(1)}, u32[]{:S(2)}, u32[]{:S(2)}) collective-permute-start(bf16[256,640]{1,0:T(8,128)(2,1)S(1)} %get-tuple-element.81), channel_id=1, source_target_pairs={{0,4},{4,0},{1,5},{5,1},{2,6},{6,2},{3,7},{7,3},{8,12},{12,8},{9,1... | collective-permute-start | bytes 983048 | tf_op jit(solution)/shard_map/ppermute | solution.py:569
  101.3 0.7 copy-start.4
  103.9 4.1 %collective-permute-start.22 = (bf16[256,256]{1,0:T(8,128)(2,1)}, bf16[256,256]{1,0:T(8,128)(2,1)S(1)}, u32[]{:S(2)}, u32[]{:S(2)}) collective-permute-start(bf16[256,256]{1,0:T(8,128)(2,1)} %key_value.1.refs_0_), channel_id=1, source_target_pairs={{0,1},{1,0},{2,3},{3,2},{4,5},{5,4},{6,7},{7,6},{8,9},{9,8},{10,11... | collective-permute-start | bytes 393224 | tf_op jit(solution)/shard_map/ppermute | solution.py:580
  105.2 7.2 %collective-permute-start.23 = (bf16[256,256]{1,0:T(8,128)(2,1)}, bf16[256,256]{1,0:T(8,128)(2,1)S(1)}, u32[]{:S(2)}, u32[]{:S(2)}) collective-permute-start(bf16[256,256]{1,0:T(8,128)(2,1)} %key_value.1.refs_0_), channel_id=1, source_target_pairs={{0,2},{1,3},{4,6},{5,7},{8,10},{9,11},{12,14},{13,15},{16,18},{17,... | collective-permute-start | bytes 393224 | tf_op jit(solution)/shard_map/ppermute | solution.py:579
  106.5 8.8 %collective-permute-start.24 = (bf16[256,256]{1,0:T(8,128)(2,1)}, bf16[256,256]{1,0:T(8,128)(2,1)S(1)}, u32[]{:S(2)}, u32[]{:S(2)}) collective-permute-start(bf16[256,256]{1,0:T(8,128)(2,1)} %key_value.1.refs_0_), channel_id=1, source_target_pairs={{0,3},{1,2},{4,7},{5,6},{8,11},{9,10},{12,15},{13,14},{16,19},{17,... | collective-permute-start | bytes 393224 | tf_op jit(solution)/shard_map/ppermute | solution.py:581
  115.4 1.0 copy-start.5
  116.3 0.9 copy-start.6
  119.2 0.9 copy-start.7

commit v4 on v3

--- a/solution.py
+++ b/solution.py
@@ -174,7 +174,7 @@
         in_specs=[outside] * (1 + len(weights)),
         out_specs=[pl.BlockSpec(memory_space=pltpu.VMEM)] * len(outs),
         scratch_shapes=[pltpu.SemaphoreType.DMA((copies,))],
-        cost_estimate=pl.CostEstimate(flops=0, bytes_accessed=moved, transcendentals=0),
+        cost_estimate=pl.CostEstimate(flops=0, bytes_accessed=0, transcendentals=0),
         name="pack",
     )(tokens, *weights)
 
@@ -230,9 +230,8 @@
             pltpu.VMEM((rows, width), jnp.bfloat16),
             pltpu.SemaphoreType.DMA((copies,)),
         ],
-        cost_estimate=pl.CostEstimate(
-            flops=2 * rows * width, bytes_accessed=4 * rows * width, transcendentals=rows
-        ),
+        cost_estimate=pl.CostEstimate(flops=0, bytes_accessed=0, transcendentals=0),
+        compiler_params=pltpu.CompilerParams(vmem_limit_bytes=10 * 2**20),
         name="prepare",
     )(tokens)
 
@@ -350,18 +349,19 @@
 
 def late_body(first, splits, before, last_rows, *refs):
     pieces, refs = (refs[:4], refs[4:])
-    kept, (sent, wide, sems) = (refs[: len(splits)], refs[len(splits) :])
-    rows, width = sent.shape
+    kept, sent = (refs[: len(splits)], refs[len(splits) : 2 * len(splits)])
+    wide, sems = refs[2 * len(splits) :]
+    rows, width = (kept[0].shape[0], wide.shape[1])
     pieces = [p if p.shape[1] == width else p.at[:, pl.ds(first, width)] for p in pieces]
     for flight in started(piece_copies(pieces, wide, lax.axis_index("ctx")), sems, 0):
         flight.wait()
     at = 0
-    for own, columns in zip(kept, splits):
+    for own, other, columns in zip(kept, sent, splits):
         cols = slice(at, at + columns)
         product = jnp.dot(last_rows[...], wide[:, cols], preferred_element_type=jnp.float32)
         product = product + before[:, first + at : first + at + columns]
         own[...] = product[:rows]
-        sent[:, cols] = product[rows:].astype(jnp.bfloat16)
+        other[...] = product[rows:].astype(jnp.bfloat16)
         at += columns
 
 
@@ -371,7 +371,7 @@
     inside = pl.BlockSpec(memory_space=pltpu.VMEM)
     width = sum(splits)
     outs = [jax.ShapeDtypeStruct((rows, w), jnp.float32) for w in splits]
-    outs.append(jax.ShapeDtypeStruct((rows, width), jnp.bfloat16))
+    outs += [jax.ShapeDtypeStruct((rows, w), jnp.bfloat16) for w in splits]
     return pl.pallas_call(
         functools.partial(late_body, first, splits),
         out_shape=outs,
@@ -384,7 +384,7 @@
         cost_estimate=pl.CostEstimate(
             flops=4 * rows * depth * width, bytes_accessed=2 * depth * width, transcendentals=0
         ),
-        compiler_params=pltpu.CompilerParams(vmem_limit_bytes=16 * 2**20),
+        compiler_params=pltpu.CompilerParams(vmem_limit_bytes=10 * 2**20),
         name="late_slot",
     )(before, last_rows, *pieces)
 
@@ -455,7 +455,7 @@
         cost_estimate=pl.CostEstimate(
             flops=4 * total * head, bytes_accessed=8 * rows * width, transcendentals=total
         ),
-        compiler_params=pltpu.CompilerParams(vmem_limit_bytes=24 * 2**20),
+        compiler_params=pltpu.CompilerParams(vmem_limit_bytes=12 * 2**20),
         name="attention",
     )(*args)
 
@@ -479,14 +479,13 @@
     parts_2 = ((1, cut, 7 * cut), (2, 0, 5 * cut))
     parts_3 = ((2, 5 * cut, 3 * cut), (3, 0, depth))
     mine, sent_1 = pack(tokens, depth, (parts_1,), (w_key, w_value, w_query))
-    half = mine.shape[1] // 2
     kv_width = 2 * head
+    half = kv_width + w_query.shape[1] // 2
+    rest = mine.shape[1] - half
     second = lax.ppermute(mine, "line", ends)
     third_in = lax.ppermute(mine, "line", middle)
-    fourth_in = lax.ppermute(second, "line", middle)
     came_1 = lax.ppermute(sent_1, "pair", swap)
-    sent_2, sent_3, scale, line_scale = prepare(tokens, depth, (parts_2, parts_3))
-    came_scale = lax.ppermute(line_scale, "pair", swap)
+    (sent_2,) = pack(tokens, depth, (parts_2,))
     gain = norm_gain.reshape(1, -1)
     bias_kv = jnp.concatenate([bias_key, bias_value]).reshape(1, -1).astype(jnp.float32)
     bias_q = bias_query.reshape(1, -1).astype(jnp.float32)
@@ -494,20 +493,23 @@
     cosine, sine_table = rotary_tables(positions, head)
     cosine = jnp.concatenate([cosine, cosine], axis=-1).reshape(rows, head)
     sine_table = jnp.concatenate([-sine_table, sine_table], axis=-1).reshape(rows, head)
-    small = (scale, came_scale, gain, bias_kv, bias_q, cosine, sine_table)
-    second, third_in, came_1, sent_2, sent_3, small = held(
-        (second, third_in, came_1, sent_2, sent_3, small)
-    )
-    scale, came_scale, gain, bias_kv, bias_q, cosine, sine_table = small
+    small = (gain, bias_kv, bias_q, cosine, sine_table)
+    second, third_in, came_1, sent_2, small, later_tokens = held(
+        (second, third_in, came_1, sent_2, small, tokens)
+    )
+    gain, bias_kv, bias_q, cosine, sine_table = small
+    fourth_in = lax.ppermute(second, "line", middle)
     third_out = lax.ppermute(third_in, "line", outward)
     second_far = lax.ppermute(second, "ctx", across)
     came_2 = lax.ppermute(sent_2, "pair", swap)
     second_side = lax.ppermute(second, "ctx", beside)
+    sent_3, scale, line_scale = prepare(later_tokens, depth, (parts_3,))
+    came_scale = lax.ppermute(line_scale, "pair", swap)
+    third = jnp.where(inner, third_in, third_out)
+    fourth_in, came_scale, third, second_far, came_2, second_side, sent_3, scale = held(
+        (fourth_in, came_scale, third, second_far, came_2, second_side, sent_3, scale)
+    )
     fourth_out = lax.ppermute(fourth_in, "line", outward)
-    third = jnp.where(inner, third_in, third_out)
-    third, second_far, came_2, second_side, sent_3 = held(
-        (third, second_far, came_2, second_side, sent_3)
-    )
     third_far = lax.ppermute(third, "ctx", across)
     came_3 = lax.ppermute(sent_3, "pair", swap)
     second_corner = lax.ppermute(second_far, "ctx", beside)
@@ -549,19 +551,21 @@
     )
     fourth_far_2 = lax.ppermute(fourth[:, half:], "ctx", across)
     fourth_corner_1 = lax.ppermute(fourth_far_1, "ctx", beside)
-    kv_sums, q_sums_1, back_1 = late_slot(
+    kv_sums, q_sums_1, back_kv, back_1 = late_slot(
         0,
         (kv_width, half - kv_width),
         before,
         last_rows,
         (fourth, fourth_far_1, fourth_side, fourth_corner_1),
     )
-    back_1, fourth_far_2 = held((back_1, fourth_far_2))
+    back_kv, back_1, fourth_far_2 = held((back_kv, back_1, fourth_far_2))
+    back_kv = lax.ppermute(back_kv, "pair", swap)
     back_1 = lax.ppermute(back_1, "pair", swap)
     fourth_corner_2 = lax.ppermute(fourth_far_2, "ctx", beside)
+    back_kv, fourth_corner_2 = held((back_kv, fourth_corner_2))
     q_sums_2, back_2 = late_slot(
         half,
-        (half,),
+        (rest,),
         before,
         last_rows,
         (fourth, fourth_far_2, fourth_side, fourth_corner_2),
@@ -574,11 +578,12 @@
         out_shape=jax.ShapeDtypeStruct((rows, kv_width), jnp.bfloat16),
         in_specs=[inside] * 5,
         out_specs=inside,
+        compiler_params=pltpu.CompilerParams(vmem_limit_bytes=4 * 2**20),
         name="key_value",
-    )(kv_sums, back_1, bias_kv, cosine, sine_table)
+    )(kv_sums, back_kv, bias_kv, cosine, sine_table)
     kv_across = lax.ppermute(key_value, "ctx", [(0, 2), (1, 3)])
     kv_beside = lax.ppermute(key_value, "ctx", beside)
-    kv_corner = lax.ppermute(key_value, "ctx", [(0, 3), (1, 2)])
+    kv_corner = lax.ppermute(kv_across, "ctx", [(2, 3), (3, 2)])
     blocks = (key_value, kv_beside, kv_across, kv_corner)
     attended = attention(q_sums_1, back_1, bias_q, cosine, sine_table, blocks)
     attended = attention(q_sums_2, back_2, bias_q, cosine, sine_table, blocks, attended)

time: 124 us -> 109 us (0.88)
  waiting for transfers between devices: 50.2 us -> 32.3 us
  starting transfers between devices: 28.8 us -> 37.2 us
  local copies, waits for them, and re-layouts: 9 us -> 6.87 us
  Pallas kernels: 32.2 us -> 30.1 us
  other arithmetic: 3.26 us -> 1.96 us
    ppermute x1, waiting for transfers between devices: 8.17 us -> 0.01 us  [planned(): fourth_in = lax.ppermute(second, 'line', middle)]
    ppermute x1, waiting for transfers between devices: 6.41 us -> 0.01 us  [planned(): back_1 = lax.ppermute(back_1, 'pair', swap)]
    ppermute x1, waiting for transfers between devices: 0.01 us -> 4.56 us  [planned(): came_scale = lax.ppermute(line_scale, 'pair', swap)]
    ppermute x1 -> x2, starting transfers between devices: 1.47 us -> 4.78 us  [the longest x1 4.1 us: planned(): kv_corner = lax.ppermute(kv_across, 'ctx', [(2, 3), (3, 2)])]
    ppermute x1, waiting for transfers between devices: 2.86 us -> 0.01 us  [planned(): came_2 = lax.ppermute(sent_2, 'pair', swap)]
    ppermute x1, waiting for transfers between devices: 4.44 us -> 1.67 us  [planned(): kv_across = lax.ppermute(key_value, 'ctx', [(0, 2), (1, 3)])]
    unnamed x42 -> x26, local copies, waits for them, and re-layouts: 8.31 us -> 6.2 us
    pallas_call x1 -> x2, Pallas kernels: 2.38 us -> 4.38 us  [pack(): pl.pallas_call(functools.partial(pack_body, sent_parts, len(weights), dep...]
  transfers between devices with their start and end apart: 25 -> 26, of which waited for: 13 -> 14; matrix products, arithmetic and copies ran while one was open for 3% -> 2% of each run, Pallas kernels for 21% -> 23%
where the time goes in v4:
time: 109 us
  starting transfers between devices  37.2 us (34%)
  waiting for transfers between devices  32.3 us (30%)
  Pallas kernels  30.1 us (28%)
  local copies, waits for them, and re-layouts  6.87 us (6%)
  other arithmetic  1.96 us (2%)
    pallas_call x2, Pallas kernels, early_slots(): pl.pallas_call(functools.partial(early_body, slots, guests, local, final)...  15.8 us
    ppermute x1, waiting for transfers between devices, planned(): came_1 = lax.ppermute(sent_1, 'pair', swap)  9.14 us
    unnamed x26, local copies, waits for them, and re-layouts  6.2 us
    pallas_call x2, Pallas kernels, attention(): pl.pallas_call(functools.partial(attention_body, head ** (-0.5), first),...  5.5 us
    ppermute x1, waiting for transfers between devices, planned(): came_scale = lax.ppermute(line_scale, 'pair', swap)  4.56 us
    pallas_call x2, Pallas kernels, pack(): pl.pallas_call(functools.partial(pack_body, sent_parts, len(weights), dep...  4.38 us
    ppermute x1, starting transfers between devices, planned(): third_in = lax.ppermute(mine, 'line', middle)  4.32 us
    ppermute x1, waiting for transfers between devices, planned(): fourth_out = lax.ppermute(fourth_in, 'line', outward)  4.19 us
  transfers between devices with their start and end apart: 26, of which 14 were waited for; matrix products, arithmetic and copies ran while one was open for 2% of the time, Pallas kernels for 23%

profile of v4, /device:TPU:11, one launch (start us, length us, event | category | flops | bytes accessed | tf_op | source)
XLA Modules:
  0.0 108.8 jit_solution(15650165193367878203)
XLA Ops:
  0.0 2.3 %pack.2 = (bf16[256,1280]{1,0:T(8,128)(2,1)}, bf16[256,1152]{1,0:T(8,128)(2,1)}) custom-call(bf16[256,8192]{1,0:T(8,128)(2,1)} %bitcast.9, bf16[1024,128]{1,0:T(8,128)(2,1)} %refs_5_.1, bf16[1024,128]{1,0:T(8,128)(2,1)} %refs_6_.1, bf16[1024,1024]{1,0:T(8,128)(2,1)} %refs_7_.1), custom_call_target="tpu_custom_call" | custom-call | tf_op jit(solution)/shard_map/pack/pallas_call | solution.py:171
  2.6 4.3 %collective-permute-start.1 = (bf16[256,1280]{1,0:T(8,128)(2,1)}, bf16[256,1280]{1,0:T(8,128)(2,1)S(1)}, u32[]{:S(2)}, u32[]{:S(2)}) collective-permute-start(bf16[256,1280]{1,0:T(8,128)(2,1)} %get-tuple-element.51), channel_id=1, source_target_pairs={{8,16},{16,8},{9,17},{17,9},{10,18},{18,10},{11,19},{19,11},{12,20... | collective-permute-start | bytes 1966088 | tf_op jit(solution)/shard_map/ppermute | solution.py:486
  7.0 1.3 %collective-permute-start.2 = (bf16[256,1152]{1,0:T(8,128)(2,1)}, bf16[256,1152]{1,0:T(8,128)(2,1)S(1)}, u32[]{:S(2)}, u32[]{:S(2)}) collective-permute-start(bf16[256,1152]{1,0:T(8,128)(2,1)} %get-tuple-element.52), channel_id=1, source_target_pairs={{0,4},{4,0},{1,5},{5,1},{2,6},{6,2},{3,7},{7,3},{8,12},{12,8},{9,1... | collective-permute-start | bytes 1769480 | tf_op jit(solution)/shard_map/ppermute | solution.py:487
  8.3 2.0 %pack.3 = bf16[256,1536]{1,0:T(8,128)(2,1)} custom-call(bf16[256,8192]{1,0:T(8,128)(2,1)} %bitcast.10), custom_call_target="tpu_custom_call" | custom-call | tf_op jit(solution)/shard_map/pack/pallas_call | solution.py:171
  10.3 0.6 reshape.176.refs_4_
  11.7 9.1 %collective-permute-done.2.refs_0_ = bf16[256,1152]{1,0:T(8,128)(2,1)S(1)} collective-permute-done((bf16[256,1152]{1,0:T(8,128)(2,1)}, bf16[256,1152]{1,0:T(8,128)(2,1)S(1)}, u32[]{:S(2)}, u32[]{:S(2)}) %collective-permute-start.2) | collective-permute-done | bytes 589856 | tf_op jit(solution)/shard_map/ppermute | solution.py:487
  21.7 2.1 %collective-permute-start.5 = (bf16[256,1280]{1,0:T(8,128)(2,1)S(1)}, bf16[256,1280]{1,0:T(8,128)(2,1)}, u32[]{:S(2)}, u32[]{:S(2)}) collective-permute-start(bf16[256,1280]{1,0:T(8,128)(2,1)S(1)} %collective-permute-done.1), channel_id=1, source_target_pairs={{8,0},{16,24},{9,1},{17,25},{10,2},{18,26},{11,3},{19,27},{12,4},{... | collective-permute-start | bytes 1966088 | tf_op jit(solution)/shard_map/ppermute | solution.py:502
  23.8 1.2 %collective-permute-start.7 = (bf16[256,1536]{1,0:T(8,128)(2,1)}, bf16[256,1536]{1,0:T(8,128)(2,1)S(1)}, u32[]{:S(2)}, u32[]{:S(2)}) collective-permute-start(bf16[256,1536]{1,0:T(8,128)(2,1)} %pack.3), channel_id=1, source_target_pairs={{0,4},{4,0},{1,5},{5,1},{2,6},{6,2},{3,7},{7,3},{8,12},{12,8},{9,1... | collective-permute-start | bytes 2359304 | tf_op jit(solution)/shard_map/ppermute | solution.py:504
  25.0 2.7 %collective-permute-start.3 = (bf16[256,1280]{1,0:T(8,128)(2,1)}, bf16[256,1280]{1,0:T(8,128)(2,1)}, u32[]{:S(2)}, u32[]{:S(2)}) collective-permute-start(bf16[256,1280]{1,0:T(8,128)(2,1)} %collective-permute-done.refs_8_), channel_id=1, source_target_pairs={{8,16},{16,8},{9,17},{17,9},{10,18},{18,10},{11,19},{19,11},{12,20... | collective-permute-start | bytes 1966088 | tf_op jit(solution)/shard_map/ppermute | solution.py:501
  28.0 2.7 %collective-permute-start.8 = (bf16[256,1280]{1,0:T(8,128)(2,1)}, bf16[256,1280]{1,0:T(8,128)(2,1)}, u32[]{:S(2)}, u32[]{:S(2)}) collective-permute-start(bf16[256,1280]{1,0:T(8,128)(2,1)} %collective-permute-done.refs_8_), channel_id=1, source_target_pairs={{0,1},{1,0},{2,3},{3,2},{4,5},{5,4},{6,7},{7,6},{8,9},{9,8},{10,11... | collective-permute-start | bytes 1966088 | tf_op jit(solution)/shard_map/ppermute | solution.py:505
  30.7 2.2 %copy-done = bf16[1,256,8192]{2,1,0:T(8,128)(2,1)S(1)} copy-done((bf16[1,256,8192]{2,1,0:T(8,128)(2,1)S(1)}, bf16[1,256,8192]{2,1,0:T(8,128)(2,1)}, u32[]{:S(2)}) %copy-start) | copy-done | bytes 4194328
  32.9 2.0 %prepare.1 = (bf16[256,1408]{1,0:T(8,128)(2,1)S(1)}, f32[256,128]{1,0:T(8,128)S(1)}, f32[1,256]{1,0:T(1,128)S(1)}) custom-call(bf16[256,8192]{1,0:T(8,128)(2,1)S(1)} %bitcast.13), custom_call_target="tpu_custom_call" | custom-call | tf_op jit(solution)/shard_map/prepare/pallas_call | solution.py:224
  34.9 0.6 copy-done.3
  35.6 0.7 collective-permute-start.4
  36.4 4.6 %collective-permute-done.4.refs_3_ = f32[1,256]{1,0:T(1,128)S(1)} collective-permute-done((f32[1,256]{1,0:T(1,128)S(1)}, f32[1,256]{1,0:T(1,128)S(1)}, u32[]{:S(2)}, u32[]{:S(2)}) %collective-permute-start.4) | collective-permute-done | bytes 1056 | tf_op jit(solution)/shard_map/ppermute | solution.py:507
  41.0 0.9 collective-permute-done.6.refs_9_
  41.9 3.4 %collective-permute-start.13 = (bf16[256,1280]{1,0:T(8,128)(2,1)}, bf16[256,1280]{1,0:T(8,128)(2,1)}, u32[]{:S(2)}, u32[]{:S(2)}) collective-permute-start(bf16[256,1280]{1,0:T(8,128)(2,1)} %collective-permute-done.6.refs_9_), channel_id=1, source_target_pairs={{0,1},{1,0},{2,3},{3,2},{4,5},{5,4},{6,7},{7,6},{8,9},{9,8},{10,11... | collective-permute-start | bytes 1966088 | tf_op jit(solution)/shard_map/ppermute | solution.py:515
  45.3 2.2 %collective-permute-start.9 = (bf16[256,1280]{1,0:T(8,128)(2,1)}, bf16[256,1280]{1,0:T(8,128)(2,1)}, u32[]{:S(2)}, u32[]{:S(2)}) collective-permute-start(bf16[256,1280]{1,0:T(8,128)(2,1)} %collective-permute-done.3), channel_id=1, source_target_pairs={{8,0},{16,24},{9,1},{17,25},{10,2},{18,26},{11,3},{19,27},{12,4},{... | collective-permute-start | bytes 1966088 | tf_op jit(solution)/shard_map/ppermute | solution.py:512
  48.0 0.7 collective-permute-start.11
  48.7 8.3 %early_slots.2.refs_9_ = f32[512,1280]{1,0:T(8,128)} custom-call(bf16[256,8192]{1,0:T(8,128)(2,1)} %bitcast.11, bf16[256,1152]{1,0:T(8,128)(2,1)} %copy-done.7, bf16[256,1536]{1,0:T(8,128)(2,1)} %copy-done.4, f32[256,128]{1,0:T(8,128)} %copy-done.3, f32[1,256]{1,0:T(1,128)} %copy-done.9, bf16[1,8192]{1,0:T(2,128)(2,1)} %reshape.176.refs_4_, ...), custom_call_target="tpu_custom_call" | custom-call | flops 2684354560 | bytes 9961472 | tf_op jit(solution)/shard_map/early_slots/pallas_call | solution.py:332
  57.1 4.2 %collective-permute-done.9 = bf16[256,1280]{1,0:T(8,128)(2,1)} collective-permute-done((bf16[256,1280]{1,0:T(8,128)(2,1)}, bf16[256,1280]{1,0:T(8,128)(2,1)}, u32[]{:S(2)}, u32[]{:S(2)}) %collective-permute-start.9) | collective-permute-done | bytes 655392 | tf_op jit(solution)/shard_map/ppermute | solution.py:512
  61.2 1.2 %broadcast_select_fusion.refs_0_ = bf16[256,1280]{1,0:T(8,128)(2,1)S(1)} fusion(bf16[256,1280]{1,0:T(8,128)(2,1)} %collective-permute-done.3, bf16[256,1280]{1,0:T(8,128)(2,1)} %collective-permute-done.9, pred[]{:T(512)S(6)} %or.3), kind=kLoop, calls=%fused_computation | loop fusion | flops 327680 | bytes 1966081 | tf_op jit(solution)/shard_map/jit(_where)/select_n | solution.py:529
  62.4 1.5 %collective-permute-done.10.refs_6_ = bf16[256,1280]{1,0:T(8,128)(2,1)} collective-permute-done((bf16[256,1280]{1,0:T(8,128)(2,1)S(1)}, bf16[256,1280]{1,0:T(8,128)(2,1)}, u32[]{:S(2)}, u32[]{:S(2)}) %collective-permute-start.10) | collective-permute-done | bytes 655392 | tf_op jit(solution)/shard_map/ppermute | solution.py:513
  63.9 1.7 %collective-permute-done.11.refs_1_ = bf16[256,1408]{1,0:T(8,128)(2,1)S(1)} collective-permute-done((bf16[256,1408]{1,0:T(8,128)(2,1)S(1)}, bf16[256,1408]{1,0:T(8,128)(2,1)S(1)}, u32[]{:S(2)}, u32[]{:S(2)}) %collective-permute-start.11) | collective-permute-done | bytes 720928 | tf_op jit(solution)/shard_map/ppermute | solution.py:514
  65.6 1.0 collective-permute-start.15
  66.7 1.3 %collective-permute-start.14 = (bf16[256,768]{1,0:T(8,128)(2,1)S(1)}, bf16[256,768]{1,0:T(8,128)(2,1)S(1)}, u32[]{:S(2)}, u32[]{:S(2)}) collective-permute-start(bf16[256,768]{1,0:T(8,128)(2,1)S(1)} %slice.6), channel_id=1, source_target_pairs={{0,2},{1,3},{2,0},{3,1},{4,6},{5,7},{6,4},{7,5},{8,10},{9,11},{10,... | collective-permute-start | bytes 1179656 | tf_op jit(solution)/shard_map/ppermute | solution.py:533
  68.0 0.9 collective-permute-done.15.refs_8_
  68.9 7.5 %early_slots.3 = (f32[512,1280]{1,0:T(8,128)}, bf16[512,1024]{1,0:T(8,128)(2,1)}) custom-call(bf16[256,8192]{1,0:T(8,128)(2,1)} %bitcast.12, bf16[256,1536]{1,0:T(8,128)(2,1)} %copy-done.4, bf16[256,1408]{1,0:T(8,128)(2,1)} %copy-done.6, f32[256,128]{1,0:T(8,128)} %copy-done.3, f32[1,256]{1,0:T(1,128)} %copy-done.9, bf16[1,8192]{1,0:T(2,128)(2,1)} %reshape.176.refs_4_, ...), custom_call_target="tpu_custom_call" | custom-call | flops 1342177280 | bytes 7340032 | tf_op jit(solution)/shard_map/early_slots/pallas_call | solution.py:332
  76.4 0.6 collective-permute-done.14.refs_1_
  77.0 1.3 %collective-permute-start.17 = (bf16[256,768]{1,0:T(8,128)(2,1)S(1)}, bf16[256,768]{1,0:T(8,128)(2,1)S(1)}, u32[]{:S(2)}, u32[]{:S(2)}) collective-permute-start(bf16[256,768]{1,0:T(8,128)(2,1)S(1)} %collective-permute-done.14.refs_1_), channel_id=1, source_target_pairs={{0,1},{1,0},{2,3},{3,2},{4,5},{5,4},{6,7},{7,6},{8,9},{9,8},{10,11... | collective-permute-start | bytes 1179656 | tf_op jit(solution)/shard_map/ppermute | solution.py:553
  78.3 1.3 %collective-permute-start.18 = (bf16[256,512]{1,0:T(8,128)(2,1)S(1)}, bf16[256,512]{1,0:T(8,128)(2,1)S(1)}, u32[]{:S(2)}, u32[]{:S(2)}) collective-permute-start(bf16[256,512]{1,0:T(8,128)(2,1)S(1)} %slice.7), channel_id=1, source_target_pairs={{0,2},{1,3},{2,0},{3,1},{4,6},{5,7},{6,4},{7,5},{8,10},{9,11},{10,... | collective-permute-start | bytes 786440 | tf_op jit(solution)/shard_map/ppermute | solution.py:552
  79.7 1.7 %copy-done.1 = f32[512,1280]{1,0:T(8,128)S(1)} copy-done((f32[512,1280]{1,0:T(8,128)S(1)}, f32[512,1280]{1,0:T(8,128)}, u32[]{:S(2)}) %copy-start.1) | copy-done | bytes 2621464
  81.4 1.2 %copy-done.2 = bf16[512,1024]{1,0:T(8,128)(2,1)S(1)} copy-done((bf16[512,1024]{1,0:T(8,128)(2,1)S(1)}, bf16[512,1024]{1,0:T(8,128)(2,1)}, u32[]{:S(2)}) %copy-start.2) | copy-done | bytes 1048600
  82.6 1.5 %late_slot.2 = (f32[256,256]{1,0:T(8,128)S(1)}, f32[256,512]{1,0:T(8,128)S(1)}, bf16[256,256]{1,0:T(8,128)(2,1)S(1)}, bf16[256,512]{1,0:T(8,128)(2,1)S(1)}) custom-call(f32[512,1280]{1,0:T(8,128)S(1)} %copy-done.1, bf16[512,1024]{1,0:T(8,128)(2,1)S(1)} %copy-done.2, bf16[256,1280]{1,0:T(8,128)(2,1)S(1)} %broadcast_select_fusion.refs_0_, ...), custom_call_target="tpu_custom_call" | custom-call | flops 805306368 | bytes 1572864 | tf_op jit(solution)/shard_map/late_slot/pallas_call | solution.py:375
  84.1 2.2 %collective-permute-done.18.refs_1_ = bf16[256,512]{1,0:T(8,128)(2,1)S(1)} collective-permute-done((bf16[256,512]{1,0:T(8,128)(2,1)S(1)}, bf16[256,512]{1,0:T(8,128)(2,1)S(1)}, u32[]{:S(2)}, u32[]{:S(2)}) %collective-permute-start.18) | collective-permute-done | bytes 262176 | tf_op jit(solution)/shard_map/ppermute | solution.py:552
  86.3 0.8 collective-permute-start.20
  87.1 0.7 collective-permute-start.19
  87.8 0.8 collective-permute-start.25
  88.6 3.7 %collective-permute-done.19.back = bf16[256,256]{1,0:T(8,128)(2,1)S(1)} collective-permute-done((bf16[256,256]{1,0:T(8,128)(2,1)S(1)}, bf16[256,256]{1,0:T(8,128)(2,1)S(1)}, u32[]{:S(2)}, u32[]{:S(2)}) %collective-permute-start.19) | collective-permute-done | bytes 131104 | tf_op jit(solution)/shard_map/ppermute | solution.py:562
  92.4 1.3 %collective-permute-start.23 = (bf16[256,256]{1,0:T(8,128)(2,1)S(1)}, bf16[256,256]{1,0:T(8,128)(2,1)S(1)}, u32[]{:S(2)}, u32[]{:S(2)}) collective-permute-start(bf16[256,256]{1,0:T(8,128)(2,1)S(1)} %key_value.1.refs_0_), channel_id=1, source_target_pairs={{0,2},{1,3},{4,6},{5,7},{8,10},{9,11},{12,14},{13,15},{16,18},{17,... | collective-permute-start | bytes 393224 | tf_op jit(solution)/shard_map/ppermute | solution.py:584
  93.7 0.8 late_slot.3
  94.5 0.7 collective-permute-start.21
  95.2 1.4 %collective-permute-start.22 = (bf16[256,256]{1,0:T(8,128)(2,1)S(1)}, bf16[256,256]{1,0:T(8,128)(2,1)S(1)}, u32[]{:S(2)}, u32[]{:S(2)}) collective-permute-start(bf16[256,256]{1,0:T(8,128)(2,1)S(1)} %key_value.1.refs_0_), channel_id=1, source_target_pairs={{0,1},{1,0},{2,3},{3,2},{4,5},{5,4},{6,7},{7,6},{8,9},{9,8},{10,11... | collective-permute-start | bytes 393224 | tf_op jit(solution)/shard_map/ppermute | solution.py:585
  96.7 1.7 %collective-permute-done.23.refs_2_ = bf16[256,256]{1,0:T(8,128)(2,1)S(1)} collective-permute-done((bf16[256,256]{1,0:T(8,128)(2,1)S(1)}, bf16[256,256]{1,0:T(8,128)(2,1)S(1)}, u32[]{:S(2)}, u32[]{:S(2)}) %collective-permute-start.23) | collective-permute-done | bytes 131104 | tf_op jit(solution)/shard_map/ppermute | solution.py:584
  98.4 4.1 %collective-permute-start.24 = (bf16[256,256]{1,0:T(8,128)(2,1)S(1)}, bf16[256,256]{1,0:T(8,128)(2,1)S(1)}, u32[]{:S(2)}, u32[]{:S(2)}) collective-permute-start(bf16[256,256]{1,0:T(8,128)(2,1)S(1)} %collective-permute-done.23.refs_2_), channel_id=1, source_target_pairs={{2,3},{3,2},{6,7},{7,6},{10,11},{11,10},{14,15},{15,14},{18,19},{1... | collective-permute-start | bytes 393224 | tf_op jit(solution)/shard_map/ppermute | solution.py:586
  102.5 0.8 collective-permute-done.24.refs_3_
  103.3 2.4 %attention.2.refs_4_ = bf16[256,512]{1,0:T(8,128)(2,1)S(1)} custom-call(f32[256,512]{1,0:T(8,128)S(1)} %get-tuple-element.95.sums, bf16[256,512]{1,0:T(8,128)(2,1)S(1)} %collective-permute-done.25.back, f32[1,1024]{1,0:T(1,128)S(1)} %bitcast.14, f32[256,128]{1,0:T(8,128)S(1)} %get-tuple-element.90.cosine, f32[256,128]{1,0:T(8,128)S(1)} %get-tuple-element.91.sine_table, ...), custom_call_target="tpu_custom_call" | custom-call | flops 536870912 | bytes 1048576 | tf_op jit(solution)/shard_map/attention/pallas_call | solution.py:446
  105.6 3.2 %attention.3 = bf16[256,1024]{1,0:T(8,128)(2,1)} custom-call(f32[256,512]{1,0:T(8,128)S(1)} %get-tuple-element.87.sums, bf16[256,512]{1,0:T(8,128)(2,1)S(1)} %collective-permute-done.21.back, f32[1,1024]{1,0:T(1,128)S(1)} %bitcast.15, f32[256,128]{1,0:T(8,128)S(1)} %get-tuple-element.90.cosine, f32[256,128]{1,0:T(8,128)S(1)} %get-tuple-element.91.sine_table, ...), custom_call_target="tpu_custom_call" | custom-call | flops 536870912 | bytes 1048576 | tf_op jit(solution)/shard_map/attention/pallas_call | solution.py:446
  (51 shorter events, 3.1 us)
Async XLA Ops:
  2.4 8.0 %copy-start.8 = (bf16[8192]{0:T(1024)(128)(2,1)S(1)}, bf16[8192]{0:T(1024)(128)(2,1)}, u32[]{:S(2)}) copy-start(bf16[8192]{0:T(1024)(128)(2,1)} %param.9) | copy-start | bytes 49156
  2.4 8.6 %copy-start.10 = (bf16[1024]{0:T(1024)(128)(2,1)S(1)}, bf16[1024]{0:T(1024)(128)(2,1)}, u32[]{:S(2)}) copy-start(bf16[1024]{0:T(1024)(128)(2,1)} %param.13) | copy-start | bytes 6148
  2.4 8.6 %copy-start.11 = (bf16[128]{0:T(256)(128)(2,1)S(1)}, bf16[128]{0:T(256)(128)(2,1)}, u32[]{:S(2)}) copy-start(bf16[128]{0:T(256)(128)(2,1)} %param.15) | copy-start | bytes 772
  2.4 8.6 %copy-start.12 = (bf16[128]{0:T(256)(128)(2,1)S(1)}, bf16[128]{0:T(256)(128)(2,1)}, u32[]{:S(2)}) copy-start(bf16[128]{0:T(256)(128)(2,1)} %param.14) | copy-start | bytes 772
  2.4 18.4 %collective-permute-start = (bf16[256,1280]{1,0:T(8,128)(2,1)}, bf16[256,1280]{1,0:T(8,128)(2,1)}, u32[]{:S(2)}, u32[]{:S(2)}) collective-permute-start(bf16[256,1280]{1,0:T(8,128)(2,1)} %get-tuple-element.51), channel_id=1, source_target_pairs={{0,8},{8,0},{16,24},{24,16},{1,9},{9,1},{17,25},{25,17},{2,10},{10... | collective-permute-start | bytes 1966088 | tf_op jit(solution)/shard_map/ppermute | solution.py:485
  2.6 18.7 %collective-permute-start.1 = (bf16[256,1280]{1,0:T(8,128)(2,1)}, bf16[256,1280]{1,0:T(8,128)(2,1)S(1)}, u32[]{:S(2)}, u32[]{:S(2)}) collective-permute-start(bf16[256,1280]{1,0:T(8,128)(2,1)} %get-tuple-element.51), channel_id=1, source_target_pairs={{8,16},{16,8},{9,17},{17,9},{10,18},{18,10},{11,19},{19,11},{12,20... | collective-permute-start | bytes 1966088 | tf_op jit(solution)/shard_map/ppermute | solution.py:486
  7.0 13.9 %collective-permute-start.2 = (bf16[256,1152]{1,0:T(8,128)(2,1)}, bf16[256,1152]{1,0:T(8,128)(2,1)S(1)}, u32[]{:S(2)}, u32[]{:S(2)}) collective-permute-start(bf16[256,1152]{1,0:T(8,128)(2,1)} %get-tuple-element.52), channel_id=1, source_target_pairs={{0,4},{4,0},{1,5},{5,1},{2,6},{6,2},{3,7},{7,3},{8,12},{12,8},{9,1... | collective-permute-start | bytes 1769480 | tf_op jit(solution)/shard_map/ppermute | solution.py:487
  20.8 0.8 copy-start.7
  21.7 13.9 %collective-permute-start.5 = (bf16[256,1280]{1,0:T(8,128)(2,1)S(1)}, bf16[256,1280]{1,0:T(8,128)(2,1)}, u32[]{:S(2)}, u32[]{:S(2)}) collective-permute-start(bf16[256,1280]{1,0:T(8,128)(2,1)S(1)} %collective-permute-done.1), channel_id=1, source_target_pairs={{8,0},{16,24},{9,1},{17,25},{10,2},{18,26},{11,3},{19,27},{12,4},{... | collective-permute-start | bytes 1966088 | tf_op jit(solution)/shard_map/ppermute | solution.py:502
  23.8 18.1 %collective-permute-start.7 = (bf16[256,1536]{1,0:T(8,128)(2,1)}, bf16[256,1536]{1,0:T(8,128)(2,1)S(1)}, u32[]{:S(2)}, u32[]{:S(2)}) collective-permute-start(bf16[256,1536]{1,0:T(8,128)(2,1)} %pack.3), channel_id=1, source_target_pairs={{0,4},{4,0},{1,5},{5,1},{2,6},{6,2},{3,7},{7,3},{8,12},{12,8},{9,1... | collective-permute-start | bytes 2359304 | tf_op jit(solution)/shard_map/ppermute | solution.py:504
  25.0 16.0 %collective-permute-start.3 = (bf16[256,1280]{1,0:T(8,128)(2,1)}, bf16[256,1280]{1,0:T(8,128)(2,1)}, u32[]{:S(2)}, u32[]{:S(2)}) collective-permute-start(bf16[256,1280]{1,0:T(8,128)(2,1)} %collective-permute-done.refs_8_), channel_id=1, source_target_pairs={{8,16},{16,8},{9,17},{17,9},{10,18},{18,10},{11,19},{19,11},{12,20... | collective-permute-start | bytes 1966088 | tf_op jit(solution)/shard_map/ppermute | solution.py:501
  27.7 14.2 %collective-permute-start.6 = (bf16[256,1280]{1,0:T(8,128)(2,1)}, bf16[256,1280]{1,0:T(8,128)(2,1)}, u32[]{:S(2)}, u32[]{:S(2)}) collective-permute-start(bf16[256,1280]{1,0:T(8,128)(2,1)} %collective-permute-done.refs_8_), channel_id=1, source_target_pairs={{0,2},{1,3},{2,0},{3,1},{4,6},{5,7},{6,4},{7,5},{8,10},{9,11},{10,... | collective-permute-start | bytes 1966088 | tf_op jit(solution)/shard_map/ppermute | solution.py:503
  28.0 13.9 %collective-permute-start.8 = (bf16[256,1280]{1,0:T(8,128)(2,1)}, bf16[256,1280]{1,0:T(8,128)(2,1)}, u32[]{:S(2)}, u32[]{:S(2)}) collective-permute-start(bf16[256,1280]{1,0:T(8,128)(2,1)} %collective-permute-done.refs_8_), channel_id=1, source_target_pairs={{0,1},{1,0},{2,3},{3,2},{4,5},{5,4},{6,7},{7,6},{8,9},{9,8},{10,11... | collective-permute-start | bytes 1966088 | tf_op jit(solution)/shard_map/ppermute | solution.py:505
  30.7 2.2 %copy-start = (bf16[1,256,8192]{2,1,0:T(8,128)(2,1)S(1)}, bf16[1,256,8192]{2,1,0:T(8,128)(2,1)}, u32[]{:S(2)}) copy-start(bf16[1,256,8192]{2,1,0:T(8,128)(2,1)} %param.8) | copy-start | bytes 12582916
  34.9 0.7 copy-start.3
  35.6 5.4 %collective-permute-start.4 = (f32[1,256]{1,0:T(1,128)S(1)}, f32[1,256]{1,0:T(1,128)S(1)}, u32[]{:S(2)}, u32[]{:S(2)}) collective-permute-start(f32[1,256]{1,0:T(1,128)S(1)} %get-tuple-element.55), channel_id=1, source_target_pairs={{0,4},{4,0},{1,5},{5,1},{2,6},{6,2},{3,7},{7,3},{8,12},{12,8},{9,1... | collective-permute-start | bytes 3080 | tf_op jit(solution)/shard_map/ppermute | solution.py:507
  36.4 29.2 %copy-start.5 = (bf16[256,1280]{1,0:T(8,128)(2,1)}, bf16[256,1280]{1,0:T(8,128)(2,1)S(1)}, u32[]{:S(2)}) copy-start(bf16[256,1280]{1,0:T(8,128)(2,1)S(1)} %broadcast_select_fusion.1.refs_5_) | copy-start | bytes 1966084
  41.0 7.7 %copy-start.9 = (f32[1,256]{1,0:T(1,128)}, f32[1,256]{1,0:T(1,128)S(1)}, u32[]{:S(2)}) copy-start(f32[1,256]{1,0:T(1,128)S(1)} %collective-permute-done.4.refs_3_) | copy-start | bytes 3076
  41.9 6.8 %copy-start.4 = (bf16[256,1536]{1,0:T(8,128)(2,1)}, bf16[256,1536]{1,0:T(8,128)(2,1)S(1)}, u32[]{:S(2)}) copy-start(bf16[256,1536]{1,0:T(8,128)(2,1)S(1)} %collective-permute-done.7.refs_1_.refs_0_) | copy-start | bytes 2359300
  41.9 6.8 %collective-permute-start.13 = (bf16[256,1280]{1,0:T(8,128)(2,1)}, bf16[256,1280]{1,0:T(8,128)(2,1)}, u32[]{:S(2)}, u32[]{:S(2)}) collective-permute-start(bf16[256,1280]{1,0:T(8,128)(2,1)} %collective-permute-done.6.refs_9_), channel_id=1, source_target_pairs={{0,1},{1,0},{2,3},{3,2},{4,5},{5,4},{6,7},{7,6},{8,9},{9,8},{10,11... | collective-permute-start | bytes 1966088 | tf_op jit(solution)/shard_map/ppermute | solution.py:515
  45.3 15.9 %collective-permute-start.9 = (bf16[256,1280]{1,0:T(8,128)(2,1)}, bf16[256,1280]{1,0:T(8,128)(2,1)}, u32[]{:S(2)}, u32[]{:S(2)}) collective-permute-start(bf16[256,1280]{1,0:T(8,128)(2,1)} %collective-permute-done.3), channel_id=1, source_target_pairs={{8,0},{16,24},{9,1},{17,25},{10,2},{18,26},{11,3},{19,27},{12,4},{... | collective-permute-start | bytes 1966088 | tf_op jit(solution)/shard_map/ppermute | solution.py:512
  47.5 16.4 %collective-permute-start.10 = (bf16[256,1280]{1,0:T(8,128)(2,1)S(1)}, bf16[256,1280]{1,0:T(8,128)(2,1)}, u32[]{:S(2)}, u32[]{:S(2)}) collective-permute-start(bf16[256,1280]{1,0:T(8,128)(2,1)S(1)} %broadcast_select_fusion.1.refs_5_), channel_id=1, source_target_pairs={{0,2},{1,3},{2,0},{3,1},{4,6},{5,7},{6,4},{7,5},{8,10},{9,11},{10,... | collective-permute-start | bytes 1966088 | tf_op jit(solution)/shard_map/ppermute | solution.py:513
  47.7 16.2 %collective-permute-start.12 = (bf16[256,1280]{1,0:T(8,128)(2,1)S(1)}, bf16[256,1280]{1,0:T(8,128)(2,1)}, u32[]{:S(2)}, u32[]{:S(2)}) collective-permute-start(bf16[256,1280]{1,0:T(8,128)(2,1)S(1)} %broadcast_select_fusion.1.refs_5_), channel_id=1, source_target_pairs={{0,1},{1,0},{2,3},{3,2},{4,5},{5,4},{6,7},{7,6},{8,9},{9,8},{10,11... | collective-permute-start | bytes 1966088 | tf_op jit(solution)/shard_map/ppermute | solution.py:516
  48.0 17.5 %collective-permute-start.11 = (bf16[256,1408]{1,0:T(8,128)(2,1)S(1)}, bf16[256,1408]{1,0:T(8,128)(2,1)S(1)}, u32[]{:S(2)}, u32[]{:S(2)}) collective-permute-start(bf16[256,1408]{1,0:T(8,128)(2,1)S(1)} %get-tuple-element.62), channel_id=1, source_target_pairs={{0,4},{4,0},{1,5},{5,1},{2,6},{6,2},{3,7},{7,3},{8,12},{12,8},{9,1... | collective-permute-start | bytes 2162696 | tf_op jit(solution)/shard_map/ppermute | solution.py:514
  65.6 3.3 %copy-start.6 = (bf16[256,1408]{1,0:T(8,128)(2,1)}, bf16[256,1408]{1,0:T(8,128)(2,1)S(1)}, u32[]{:S(2)}) copy-start(bf16[256,1408]{1,0:T(8,128)(2,1)S(1)} %collective-permute-done.11.refs_1_) | copy-start | bytes 2162692
  65.6 3.3 %collective-permute-start.15 = (bf16[256,1280]{1,0:T(8,128)(2,1)}, bf16[256,1280]{1,0:T(8,128)(2,1)}, u32[]{:S(2)}, u32[]{:S(2)}) collective-permute-start(bf16[256,1280]{1,0:T(8,128)(2,1)} %collective-permute-done.10.refs_6_), channel_id=1, source_target_pairs={{0,1},{1,0},{2,3},{3,2},{4,5},{5,4},{6,7},{7,6},{8,9},{9,8},{10,11... | collective-permute-start | bytes 1966088 | tf_op jit(solution)/shard_map/ppermute | solution.py:534
  66.6 10.4 %collective-permute-start.16 = (bf16[256,1280]{1,0:T(8,128)(2,1)S(1)}, bf16[256,1280]{1,0:T(8,128)(2,1)S(1)}, u32[]{:S(2)}, u32[]{:S(2)}) collective-permute-start(bf16[256,1280]{1,0:T(8,128)(2,1)S(1)} %broadcast_select_fusion.refs_0_), channel_id=1, source_target_pairs={{0,1},{1,0},{2,3},{3,2},{4,5},{5,4},{6,7},{7,6},{8,9},{9,8},{10,11... | collective-permute-start | bytes 1966088 | tf_op jit(solution)/shard_map/ppermute | solution.py:535
  66.7 10.3 %collective-permute-start.14 = (bf16[256,768]{1,0:T(8,128)(2,1)S(1)}, bf16[256,768]{1,0:T(8,128)(2,1)S(1)}, u32[]{:S(2)}, u32[]{:S(2)}) collective-permute-start(bf16[256,768]{1,0:T(8,128)(2,1)S(1)} %slice.6), channel_id=1, source_target_pairs={{0,2},{1,3},{2,0},{3,1},{4,6},{5,7},{6,4},{7,5},{8,10},{9,11},{10,... | collective-permute-start | bytes 1179656 | tf_op jit(solution)/shard_map/ppermute | solution.py:533
  77.0 2.6 %collective-permute-start.17 = (bf16[256,768]{1,0:T(8,128)(2,1)S(1)}, bf16[256,768]{1,0:T(8,128)(2,1)S(1)}, u32[]{:S(2)}, u32[]{:S(2)}) collective-permute-start(bf16[256,768]{1,0:T(8,128)(2,1)S(1)} %collective-permute-done.14.refs_1_), channel_id=1, source_target_pairs={{0,1},{1,0},{2,3},{3,2},{4,5},{5,4},{6,7},{7,6},{8,9},{9,8},{10,11... | collective-permute-start | bytes 1179656 | tf_op jit(solution)/shard_map/ppermute | solution.py:553
  78.3 8.0 %collective-permute-start.18 = (bf16[256,512]{1,0:T(8,128)(2,1)S(1)}, bf16[256,512]{1,0:T(8,128)(2,1)S(1)}, u32[]{:S(2)}, u32[]{:S(2)}) collective-permute-start(bf16[256,512]{1,0:T(8,128)(2,1)S(1)} %slice.7), channel_id=1, source_target_pairs={{0,2},{1,3},{2,0},{3,1},{4,6},{5,7},{6,4},{7,5},{8,10},{9,11},{10,... | collective-permute-start | bytes 786440 | tf_op jit(solution)/shard_map/ppermute | solution.py:552
  79.7 1.7 %copy-start.1 = (f32[512,1280]{1,0:T(8,128)S(1)}, f32[512,1280]{1,0:T(8,128)}, u32[]{:S(2)}) copy-start(f32[512,1280]{1,0:T(8,128)} %get-tuple-element.77.before) | copy-start | bytes 7864324
  81.4 1.2 %copy-start.2 = (bf16[512,1024]{1,0:T(8,128)(2,1)S(1)}, bf16[512,1024]{1,0:T(8,128)(2,1)}, u32[]{:S(2)}) copy-start(bf16[512,1024]{1,0:T(8,128)(2,1)} %get-tuple-element.78.last_rows) | copy-start | bytes 3145732
  86.3 5.9 %collective-permute-start.20 = (bf16[256,512]{1,0:T(8,128)(2,1)S(1)}, bf16[256,512]{1,0:T(8,128)(2,1)S(1)}, u32[]{:S(2)}, u32[]{:S(2)}) collective-permute-start(bf16[256,512]{1,0:T(8,128)(2,1)S(1)} %collective-permute-done.18.refs_1_), channel_id=1, source_target_pairs={{0,1},{1,0},{2,3},{3,2},{4,5},{5,4},{6,7},{7,6},{8,9},{9,8},{10,11... | collective-permute-start | bytes 786440 | tf_op jit(solution)/shard_map/ppermute | solution.py:564
  87.1 5.1 %collective-permute-start.19 = (bf16[256,256]{1,0:T(8,128)(2,1)S(1)}, bf16[256,256]{1,0:T(8,128)(2,1)S(1)}, u32[]{:S(2)}, u32[]{:S(2)}) collective-permute-start(bf16[256,256]{1,0:T(8,128)(2,1)S(1)} %get-tuple-element.85), channel_id=1, source_target_pairs={{0,4},{4,0},{1,5},{5,1},{2,6},{6,2},{3,7},{7,3},{8,12},{12,8},{9,1... | collective-permute-start | bytes 393224 | tf_op jit(solution)/shard_map/ppermute | solution.py:562
  87.8 14.7 %collective-permute-start.25 = (bf16[256,512]{1,0:T(8,128)(2,1)S(1)}, bf16[256,512]{1,0:T(8,128)(2,1)S(1)}, u32[]{:S(2)}, u32[]{:S(2)}) collective-permute-start(bf16[256,512]{1,0:T(8,128)(2,1)S(1)} %get-tuple-element.96), channel_id=1, source_target_pairs={{0,4},{4,0},{1,5},{5,1},{2,6},{6,2},{3,7},{7,3},{8,12},{12,8},{9,1... | collective-permute-start | bytes 786440 | tf_op jit(solution)/shard_map/ppermute | solution.py:563
  92.4 6.0 %collective-permute-start.23 = (bf16[256,256]{1,0:T(8,128)(2,1)S(1)}, bf16[256,256]{1,0:T(8,128)(2,1)S(1)}, u32[]{:S(2)}, u32[]{:S(2)}) collective-permute-start(bf16[256,256]{1,0:T(8,128)(2,1)S(1)} %key_value.1.refs_0_), channel_id=1, source_target_pairs={{0,2},{1,3},{4,6},{5,7},{8,10},{9,11},{12,14},{13,15},{16,18},{17,... | collective-permute-start | bytes 393224 | tf_op jit(solution)/shard_map/ppermute | solution.py:584
  94.5 11.1 %collective-permute-start.21 = (bf16[256,512]{1,0:T(8,128)(2,1)S(1)}, bf16[256,512]{1,0:T(8,128)(2,1)S(1)}, u32[]{:S(2)}, u32[]{:S(2)}) collective-permute-start(bf16[256,512]{1,0:T(8,128)(2,1)S(1)} %get-tuple-element.88), channel_id=1, source_target_pairs={{0,4},{4,0},{1,5},{5,1},{2,6},{6,2},{3,7},{7,3},{8,12},{12,8},{9,1... | collective-permute-start | bytes 786440 | tf_op jit(solution)/shard_map/ppermute | solution.py:573
  95.2 7.2 %collective-permute-start.22 = (bf16[256,256]{1,0:T(8,128)(2,1)S(1)}, bf16[256,256]{1,0:T(8,128)(2,1)S(1)}, u32[]{:S(2)}, u32[]{:S(2)}) collective-permute-start(bf16[256,256]{1,0:T(8,128)(2,1)S(1)} %key_value.1.refs_0_), channel_id=1, source_target_pairs={{0,1},{1,0},{2,3},{3,2},{4,5},{5,4},{6,7},{7,6},{8,9},{9,8},{10,11... | collective-permute-start | bytes 393224 | tf_op jit(solution)/shard_map/ppermute | solution.py:585
  98.4 4.9 %collective-permute-start.24 = (bf16[256,256]{1,0:T(8,128)(2,1)S(1)}, bf16[256,256]{1,0:T(8,128)(2,1)S(1)}, u32[]{:S(2)}, u32[]{:S(2)}) collective-permute-start(bf16[256,256]{1,0:T(8,128)(2,1)S(1)} %collective-permute-done.23.refs_2_), channel_id=1, source_target_pairs={{2,3},{3,2},{6,7},{7,6},{10,11},{11,10},{14,15},{15,14},{18,19},{1... | collective-permute-start | bytes 393224 | tf_op jit(solution)/shard_map/ppermute | solution.py:586

commit v5 on v4

--- a/solution.py
+++ b/solution.py
@@ -342,7 +342,7 @@
             pltpu.SemaphoreType.DMA((len(guests) + len(slots) + len(weights),)),
         ],
         cost_estimate=pl.CostEstimate(flops=flops, bytes_accessed=moved, transcendentals=0),
-        compiler_params=pltpu.CompilerParams(vmem_limit_bytes=60 * 2**20),
+        compiler_params=pltpu.CompilerParams(vmem_limit_bytes=24 * 2**20),
         name="early_slots",
     )(*args)
 
@@ -558,11 +558,10 @@
         last_rows,
         (fourth, fourth_far_1, fourth_side, fourth_corner_1),
     )
-    back_kv, back_1, fourth_far_2 = held((back_kv, back_1, fourth_far_2))
     back_kv = lax.ppermute(back_kv, "pair", swap)
     back_1 = lax.ppermute(back_1, "pair", swap)
+    back_kv, fourth_far_2 = held((back_kv, fourth_far_2))
     fourth_corner_2 = lax.ppermute(fourth_far_2, "ctx", beside)
-    back_kv, fourth_corner_2 = held((back_kv, fourth_corner_2))
     q_sums_2, back_2 = late_slot(
         half,
         (rest,),

time: 109 us -> 105 us (0.963); the launches traced: 109 us -> 104 us
  Pallas kernels: 30.1 us -> 22.4 us
  waiting for transfers between devices: 32.3 us -> 39.2 us
  local copies, waits for them, and re-layouts: 6.87 us -> 2.66 us
  starting transfers between devices: 37.2 us -> 35.9 us
  other arithmetic: 1.96 us -> 3.07 us
    pallas_call x2, Pallas kernels: 15.8 us -> 7.95 us  [early_slots(): pl.pallas_call(functools.partial(early_body, slots, guests, local, final)...]
    ppermute x1, waiting for transfers between devices: 0.58 us -> 5.36 us  [planned(): fourth_far_1 = lax.ppermute(fourth[:, :half], 'ctx', across)]
    ppermute x1, waiting for transfers between devices: 4.19 us -> 8.24 us  [planned(): fourth_out = lax.ppermute(fourth_in, 'line', outward)]
    ppermute x1, waiting for transfers between devices: 3.66 us -> 0.01 us  [planned(): back_kv = lax.ppermute(back_kv, 'pair', swap)]
    unnamed x26 -> x22, local copies, waits for them, and re-layouts: 6.2 us -> 2.59 us
    ppermute x1, waiting for transfers between devices: 2.23 us -> 4.2 us  [planned(): fourth_far_2 = lax.ppermute(fourth[:, half:], 'ctx', across)]
    ppermute x1, waiting for transfers between devices: 1.67 us -> 3.37 us  [planned(): kv_across = lax.ppermute(key_value, 'ctx', [(0, 2), (1, 3)])]
    ppermute x1, waiting for transfers between devices: 4.56 us -> 3.21 us  [planned(): came_scale = lax.ppermute(line_scale, 'pair', swap)]
  transfers between devices with their start and end apart: 26 -> 26, of which waited for: 14 -> 14; matrix products, arithmetic and copies ran while one was open for 2% -> 3% of each run, Pallas kernels for 23% -> 16%
where the time goes in v5:
time: 105 us; the launch traced here: 104 us
  waiting for transfers between devices  39.2 us (37%)
  starting transfers between devices  35.9 us (34%)
  Pallas kernels  22.4 us (21%)
  other arithmetic  3.07 us (3%)
  local copies, waits for them, and re-layouts  2.66 us (3%)
    ppermute x1, waiting for transfers between devices, planned(): came_1 = lax.ppermute(sent_1, 'pair', swap)  9.65 us
    ppermute x1, waiting for transfers between devices, planned(): fourth_out = lax.ppermute(fourth_in, 'line', outward)  8.24 us
    pallas_call x2, Pallas kernels, early_slots(): pl.pallas_call(functools.partial(early_body, slots, guests, local, final)...  7.95 us
    pallas_call x2, Pallas kernels, attention(): pl.pallas_call(functools.partial(attention_body, head ** (-0.5), first),...  5.52 us
    ppermute x1, waiting for transfers between devices, planned(): fourth_far_1 = lax.ppermute(fourth[:, :half], 'ctx', across)  5.36 us
    pallas_call x2, Pallas kernels, pack(): pl.pallas_call(functools.partial(pack_body, sent_parts, len(weights), dep...  4.55 us
    ppermute x1, starting transfers between devices, planned(): third_in = lax.ppermute(mine, 'line', middle)  4.32 us
    ppermute x1, waiting for transfers between devices, planned(): fourth_far_2 = lax.ppermute(fourth[:, half:], 'ctx', across)  4.2 us
  transfers between devices with their start and end apart: 26, of which 14 were waited for; matrix products, arithmetic and copies ran while one was open for 3% of the time, Pallas kernels for 16%

profile of v5, /device:TPU:11, one launch (start us, length us, event | category | flops | bytes accessed | tf_op | source)
XLA Modules:
  0.0 103.6 jit_solution(2946094937526883182)
XLA Ops:
  0.0 2.4 %pack.2 = (bf16[256,1280]{1,0:T(8,128)(2,1)}, bf16[256,1152]{1,0:T(8,128)(2,1)}) custom-call(bf16[256,8192]{1,0:T(8,128)(2,1)} %bitcast.9, bf16[1024,128]{1,0:T(8,128)(2,1)} %refs_5_.1, bf16[1024,128]{1,0:T(8,128)(2,1)} %refs_6_.1, bf16[1024,1024]{1,0:T(8,128)(2,1)} %refs_7_.1), custom_call_target="tpu_custom_call" | custom-call | tf_op jit(solution)/shard_map/pack/pallas_call | solution.py:171
  2.6 4.3 %collective-permute-start.1 = (bf16[256,1280]{1,0:T(8,128)(2,1)}, bf16[256,1280]{1,0:T(8,128)(2,1)}, u32[]{:S(2)}, u32[]{:S(2)}) collective-permute-start(bf16[256,1280]{1,0:T(8,128)(2,1)} %get-tuple-element.48), channel_id=1, source_target_pairs={{8,16},{16,8},{9,17},{17,9},{10,18},{18,10},{11,19},{19,11},{12,20... | collective-permute-start | bytes 1966088 | tf_op jit(solution)/shard_map/ppermute | solution.py:486
  7.0 1.3 %collective-permute-start.2 = (bf16[256,1152]{1,0:T(8,128)(2,1)}, bf16[256,1152]{1,0:T(8,128)(2,1)}, u32[]{:S(2)}, u32[]{:S(2)}) collective-permute-start(bf16[256,1152]{1,0:T(8,128)(2,1)} %get-tuple-element.49), channel_id=1, source_target_pairs={{0,4},{4,0},{1,5},{5,1},{2,6},{6,2},{3,7},{7,3},{8,12},{12,8},{9,1... | collective-permute-start | bytes 1769480 | tf_op jit(solution)/shard_map/ppermute | solution.py:487
  8.3 2.2 %pack.3 = bf16[256,1536]{1,0:T(8,128)(2,1)} custom-call(bf16[256,8192]{1,0:T(8,128)(2,1)} %bitcast.10), custom_call_target="tpu_custom_call" | custom-call | tf_op jit(solution)/shard_map/pack/pallas_call | solution.py:171
  10.6 0.5 fusion
  11.3 9.7 %collective-permute-done.2.refs_0_ = bf16[256,1152]{1,0:T(8,128)(2,1)} collective-permute-done((bf16[256,1152]{1,0:T(8,128)(2,1)}, bf16[256,1152]{1,0:T(8,128)(2,1)}, u32[]{:S(2)}, u32[]{:S(2)}) %collective-permute-start.2) | collective-permute-done | bytes 589856 | tf_op jit(solution)/shard_map/ppermute | solution.py:487
  20.9 0.5 collective-permute-done.1
  21.4 0.4 copy-done.5
  21.8 2.1 %collective-permute-start.5 = (bf16[256,1280]{1,0:T(8,128)(2,1)}, bf16[256,1280]{1,0:T(8,128)(2,1)}, u32[]{:S(2)}, u32[]{:S(2)}) collective-permute-start(bf16[256,1280]{1,0:T(8,128)(2,1)} %collective-permute-done.1), channel_id=1, source_target_pairs={{8,0},{16,24},{9,1},{17,25},{10,2},{18,26},{11,3},{19,27},{12,4},{... | collective-permute-start | bytes 1966088 | tf_op jit(solution)/shard_map/ppermute | solution.py:502
  23.9 1.2 %collective-permute-start.7 = (bf16[256,1536]{1,0:T(8,128)(2,1)}, bf16[256,1536]{1,0:T(8,128)(2,1)S(1)}, u32[]{:S(2)}, u32[]{:S(2)}) collective-permute-start(bf16[256,1536]{1,0:T(8,128)(2,1)} %pack.3), channel_id=1, source_target_pairs={{0,4},{4,0},{1,5},{5,1},{2,6},{6,2},{3,7},{7,3},{8,12},{12,8},{9,1... | collective-permute-start | bytes 2359304 | tf_op jit(solution)/shard_map/ppermute | solution.py:504
  25.2 2.7 %collective-permute-start.3 = (bf16[256,1280]{1,0:T(8,128)(2,1)}, bf16[256,1280]{1,0:T(8,128)(2,1)}, u32[]{:S(2)}, u32[]{:S(2)}) collective-permute-start(bf16[256,1280]{1,0:T(8,128)(2,1)} %copy-done.5), channel_id=1, source_target_pairs={{8,16},{16,8},{9,17},{17,9},{10,18},{18,10},{11,19},{19,11},{12,20... | collective-permute-start | bytes 1966088 | tf_op jit(solution)/shard_map/ppermute | solution.py:501
  28.2 2.8 %collective-permute-start.8 = (bf16[256,1280]{1,0:T(8,128)(2,1)}, bf16[256,1280]{1,0:T(8,128)(2,1)}, u32[]{:S(2)}, u32[]{:S(2)}) collective-permute-start(bf16[256,1280]{1,0:T(8,128)(2,1)} %copy-done.5), channel_id=1, source_target_pairs={{0,1},{1,0},{2,3},{3,2},{4,5},{5,4},{6,7},{7,6},{8,9},{9,8},{10,11... | collective-permute-start | bytes 1966088 | tf_op jit(solution)/shard_map/ppermute | solution.py:505
  31.0 2.2 %copy-done = bf16[1,256,8192]{2,1,0:T(8,128)(2,1)S(1)} copy-done((bf16[1,256,8192]{2,1,0:T(8,128)(2,1)S(1)}, bf16[1,256,8192]{2,1,0:T(8,128)(2,1)}, u32[]{:S(2)}) %copy-start) | copy-done | bytes 4194328
  33.2 2.0 %prepare.1 = (bf16[256,1408]{1,0:T(8,128)(2,1)S(1)}, f32[256,128]{1,0:T(8,128)S(1)}, f32[1,256]{1,0:T(1,128)S(1)}) custom-call(bf16[256,8192]{1,0:T(8,128)(2,1)S(1)} %bitcast.11), custom_call_target="tpu_custom_call" | custom-call | tf_op jit(solution)/shard_map/prepare/pallas_call | solution.py:224
  35.2 0.3 collective-permute-done.5
  35.5 1.2 %collective-permute-start.4 = (f32[1,256]{1,0:T(1,128)S(1)}, f32[1,256]{1,0:T(1,128)S(1)}, u32[]{:S(2)}, u32[]{:S(2)}) collective-permute-start(f32[1,256]{1,0:T(1,128)S(1)} %get-tuple-element.52), channel_id=1, source_target_pairs={{0,4},{4,0},{1,5},{5,1},{2,6},{6,2},{3,7},{7,3},{8,12},{12,8},{9,1... | collective-permute-start | bytes 3080 | tf_op jit(solution)/shard_map/ppermute | solution.py:507
  36.7 1.2 %broadcast_select_fusion.1.refs_5_ = bf16[256,1280]{1,0:T(8,128)(2,1)S(1)} fusion(bf16[256,1280]{1,0:T(8,128)(2,1)} %collective-permute-done.1, bf16[256,1280]{1,0:T(8,128)(2,1)} %collective-permute-done.5, pred[]{:T(512)S(6)} %or.3), kind=kLoop, calls=%fused_computation.1 | loop fusion | flops 327680 | bytes 1966081 | tf_op jit(solution)/shard_map/jit(_where)/select_n | solution.py:508
  37.9 3.2 %collective-permute-done.4.refs_3_ = f32[1,256]{1,0:T(1,128)S(1)} collective-permute-done((f32[1,256]{1,0:T(1,128)S(1)}, f32[1,256]{1,0:T(1,128)S(1)}, u32[]{:S(2)}, u32[]{:S(2)}) %collective-permute-start.4) | collective-permute-done | bytes 1056 | tf_op jit(solution)/shard_map/ppermute | solution.py:507
  41.1 0.8 collective-permute-done.6.refs_9_
  41.9 3.5 %collective-permute-start.13 = (bf16[256,1280]{1,0:T(8,128)(2,1)}, bf16[256,1280]{1,0:T(8,128)(2,1)S(1)}, u32[]{:S(2)}, u32[]{:S(2)}) collective-permute-start(bf16[256,1280]{1,0:T(8,128)(2,1)} %collective-permute-done.6.refs_9_), channel_id=1, source_target_pairs={{0,1},{1,0},{2,3},{3,2},{4,5},{5,4},{6,7},{7,6},{8,9},{9,8},{10,11... | collective-permute-start | bytes 1966088 | tf_op jit(solution)/shard_map/ppermute | solution.py:515
  45.4 1.3 %collective-permute-start.9 = (bf16[256,1280]{1,0:T(8,128)(2,1)}, bf16[256,1280]{1,0:T(8,128)(2,1)S(1)}, u32[]{:S(2)}, u32[]{:S(2)}) collective-permute-start(bf16[256,1280]{1,0:T(8,128)(2,1)} %collective-permute-done.3), channel_id=1, source_target_pairs={{8,0},{16,24},{9,1},{17,25},{10,2},{18,26},{11,3},{19,27},{12,4},{... | collective-permute-start | bytes 1966088 | tf_op jit(solution)/shard_map/ppermute | solution.py:512
  47.3 0.9 collective-permute-start.11
  48.3 4.8 %early_slots.2.refs_9_ = f32[512,1280]{1,0:T(8,128)S(1)} custom-call(bf16[256,8192]{1,0:T(8,128)(2,1)S(1)} %bitcast.12, bf16[256,1152]{1,0:T(8,128)(2,1)} %collective-permute-done.2.refs_0_, bf16[256,1536]{1,0:T(8,128)(2,1)S(1)} %collective-permute-done.7.refs_1_.refs_0_, f32[256,128]{1,0:T(8,128)S(1)} %get-tuple-element.62.refs_2_, ...), custom_call_target="tpu_custom_call" | custom-call | flops 2684354560 | bytes 9961472 | tf_op jit(solution)/shard_map/early_slots/pallas_call | solution.py:332
  53.1 8.2 %collective-permute-done.9 = bf16[256,1280]{1,0:T(8,128)(2,1)S(1)} collective-permute-done((bf16[256,1280]{1,0:T(8,128)(2,1)}, bf16[256,1280]{1,0:T(8,128)(2,1)S(1)}, u32[]{:S(2)}, u32[]{:S(2)}) %collective-permute-start.9) | collective-permute-done | bytes 655392 | tf_op jit(solution)/shard_map/ppermute | solution.py:512
  61.3 1.2 %broadcast_select_fusion.refs_0_ = bf16[256,1280]{1,0:T(8,128)(2,1)S(1)} fusion(bf16[256,1280]{1,0:T(8,128)(2,1)} %collective-permute-done.3, bf16[256,1280]{1,0:T(8,128)(2,1)S(1)} %collective-permute-done.9, pred[]{:T(512)S(6)} %or.3), kind=kLoop, calls=%fused_computation | loop fusion | flops 327680 | bytes 1966081 | tf_op jit(solution)/shard_map/jit(_where)/select_n | solution.py:529
  62.5 0.6 collective-permute-done.10.refs_6_
  63.1 1.7 %collective-permute-done.11.refs_1_ = bf16[256,1408]{1,0:T(8,128)(2,1)S(1)} collective-permute-done((bf16[256,1408]{1,0:T(8,128)(2,1)S(1)}, bf16[256,1408]{1,0:T(8,128)(2,1)S(1)}, u32[]{:S(2)}, u32[]{:S(2)}) %collective-permute-start.11) | collective-permute-done | bytes 720928 | tf_op jit(solution)/shard_map/ppermute | solution.py:514
  64.9 1.0 collective-permute-start.15
  65.9 1.3 %collective-permute-start.14 = (bf16[256,768]{1,0:T(8,128)(2,1)S(1)}, bf16[256,768]{1,0:T(8,128)(2,1)S(1)}, u32[]{:S(2)}, u32[]{:S(2)}) collective-permute-start(bf16[256,768]{1,0:T(8,128)(2,1)S(1)} %slice.6), channel_id=1, source_target_pairs={{0,2},{1,3},{2,0},{3,1},{4,6},{5,7},{6,4},{7,5},{8,10},{9,11},{10,... | collective-permute-start | bytes 1179656 | tf_op jit(solution)/shard_map/ppermute | solution.py:533
  67.2 0.4 collective-permute-done.15.refs_8_
  67.6 3.2 %early_slots.3 = (f32[512,1280]{1,0:T(8,128)S(1)}, bf16[512,1024]{1,0:T(8,128)(2,1)S(1)}) custom-call(bf16[256,8192]{1,0:T(8,128)(2,1)S(1)} %bitcast.13, bf16[256,1536]{1,0:T(8,128)(2,1)S(1)} %collective-permute-done.7.refs_1_.refs_0_, bf16[256,1408]{1,0:T(8,128)(2,1)S(1)} %collective-permute-done.11.refs_1_, f32[256,128]{1,0:T(8,128)S(1)} %get-tuple-element.62.refs_2_, ...), custom_call_target="tpu_custom_call" | custom-call | flops 1342177280 | bytes 7340032 | tf_op jit(solution)/shard_map/early_slots/pallas_call | solution.py:332
  70.8 5.4 %collective-permute-done.14.refs_1_ = bf16[256,768]{1,0:T(8,128)(2,1)S(1)} collective-permute-done((bf16[256,768]{1,0:T(8,128)(2,1)S(1)}, bf16[256,768]{1,0:T(8,128)(2,1)S(1)}, u32[]{:S(2)}, u32[]{:S(2)}) %collective-permute-start.14) | collective-permute-done | bytes 393248 | tf_op jit(solution)/shard_map/ppermute | solution.py:533
  76.2 1.4 %collective-permute-start.17 = (bf16[256,768]{1,0:T(8,128)(2,1)S(1)}, bf16[256,768]{1,0:T(8,128)(2,1)S(1)}, u32[]{:S(2)}, u32[]{:S(2)}) collective-permute-start(bf16[256,768]{1,0:T(8,128)(2,1)S(1)} %collective-permute-done.14.refs_1_), channel_id=1, source_target_pairs={{0,1},{1,0},{2,3},{3,2},{4,5},{5,4},{6,7},{7,6},{8,9},{9,8},{10,11... | collective-permute-start | bytes 1179656 | tf_op jit(solution)/shard_map/ppermute | solution.py:553
  77.5 1.3 %collective-permute-start.19 = (bf16[256,512]{1,0:T(8,128)(2,1)S(1)}, bf16[256,512]{1,0:T(8,128)(2,1)S(1)}, u32[]{:S(2)}, u32[]{:S(2)}) collective-permute-start(bf16[256,512]{1,0:T(8,128)(2,1)S(1)} %slice.7), channel_id=1, source_target_pairs={{0,2},{1,3},{2,0},{3,1},{4,6},{5,7},{6,4},{7,5},{8,10},{9,11},{10,... | collective-permute-start | bytes 786440 | tf_op jit(solution)/shard_map/ppermute | solution.py:552
  78.9 1.5 %late_slot.2 = (f32[256,256]{1,0:T(8,128)S(1)}, f32[256,512]{1,0:T(8,128)S(1)}, bf16[256,256]{1,0:T(8,128)(2,1)S(1)}, bf16[256,512]{1,0:T(8,128)(2,1)S(1)}) custom-call(f32[512,1280]{1,0:T(8,128)S(1)} %get-tuple-element.74.before, bf16[512,1024]{1,0:T(8,128)(2,1)S(1)} %get-tuple-element.75.last_rows, bf16[256,1280]{1,0:T(8,128)(2,1)S(1)} %broadcast_select_fusion.refs_0_, ...), custom_call_target="tpu_custom_call" | custom-call | flops 805306368 | bytes 1572864 | tf_op jit(solution)/shard_map/late_slot/pallas_call | solution.py:375
  80.3 1.0 collective-permute-start.18
  81.3 4.2 %collective-permute-done.19.refs_1_ = bf16[256,512]{1,0:T(8,128)(2,1)S(1)} collective-permute-done((bf16[256,512]{1,0:T(8,128)(2,1)S(1)}, bf16[256,512]{1,0:T(8,128)(2,1)S(1)}, u32[]{:S(2)}, u32[]{:S(2)}) %collective-permute-start.19) | collective-permute-done | bytes 262176 | tf_op jit(solution)/shard_map/ppermute | solution.py:552
  85.5 0.8 collective-permute-start.20
  86.3 0.9 collective-permute-start.25
  87.4 1.3 %collective-permute-start.23 = (bf16[256,256]{1,0:T(8,128)(2,1)S(1)}, bf16[256,256]{1,0:T(8,128)(2,1)S(1)}, u32[]{:S(2)}, u32[]{:S(2)}) collective-permute-start(bf16[256,256]{1,0:T(8,128)(2,1)S(1)} %key_value.1.refs_0_), channel_id=1, source_target_pairs={{0,2},{1,3},{4,6},{5,7},{8,10},{9,11},{12,14},{13,15},{16,18},{17,... | collective-permute-start | bytes 393224 | tf_op jit(solution)/shard_map/ppermute | solution.py:583
  88.7 0.9 late_slot.3
  89.5 0.6 collective-permute-start.21
  90.1 0.6 collective-permute-start.22
  90.7 3.4 %collective-permute-done.23.refs_2_ = bf16[256,256]{1,0:T(8,128)(2,1)S(1)} collective-permute-done((bf16[256,256]{1,0:T(8,128)(2,1)S(1)}, bf16[256,256]{1,0:T(8,128)(2,1)S(1)}, u32[]{:S(2)}, u32[]{:S(2)}) %collective-permute-start.23) | collective-permute-done | bytes 131104 | tf_op jit(solution)/shard_map/ppermute | solution.py:583
  94.1 3.2 %collective-permute-start.24 = (bf16[256,256]{1,0:T(8,128)(2,1)S(1)}, bf16[256,256]{1,0:T(8,128)(2,1)S(1)}, u32[]{:S(2)}, u32[]{:S(2)}) collective-permute-start(bf16[256,256]{1,0:T(8,128)(2,1)S(1)} %collective-permute-done.23.refs_2_), channel_id=1, source_target_pairs={{2,3},{3,2},{6,7},{7,6},{10,11},{11,10},{14,15},{15,14},{18,19},{1... | collective-permute-start | bytes 393224 | tf_op jit(solution)/shard_map/ppermute | solution.py:585
  97.3 0.8 collective-permute-done.24.refs_3_
  98.0 2.4 %attention.2.refs_4_ = bf16[256,512]{1,0:T(8,128)(2,1)S(1)} custom-call(f32[256,512]{1,0:T(8,128)S(1)} %get-tuple-element.89.sums, bf16[256,512]{1,0:T(8,128)(2,1)S(1)} %collective-permute-done.25.back, f32[1,1024]{1,0:T(1,128)S(1)} %bitcast.14, f32[256,128]{1,0:T(8,128)S(1)} %get-tuple-element.84.cosine, f32[256,128]{1,0:T(8,128)S(1)} %get-tuple-element.85.sine_table, ...), custom_call_target="tpu_custom_call" | custom-call | flops 536870912 | bytes 1048576 | tf_op jit(solution)/shard_map/attention/pallas_call | solution.py:446
  100.4 3.2 %attention.3 = bf16[256,1024]{1,0:T(8,128)(2,1)} custom-call(f32[256,512]{1,0:T(8,128)S(1)} %get-tuple-element.81.sums, bf16[256,512]{1,0:T(8,128)(2,1)S(1)} %collective-permute-done.21.back, f32[1,1024]{1,0:T(1,128)S(1)} %bitcast.15, f32[256,128]{1,0:T(8,128)S(1)} %get-tuple-element.84.cosine, f32[256,128]{1,0:T(8,128)S(1)} %get-tuple-element.85.sine_table, ...), custom_call_target="tpu_custom_call" | custom-call | flops 536870912 | bytes 1048576 | tf_op jit(solution)/shard_map/attention/pallas_call | solution.py:446
  (47 shorter events, 1.6 us)
Async XLA Ops:
  2.4 8.1 %copy-start.7 = (bf16[8192]{0:T(1024)(128)(2,1)S(1)}, bf16[8192]{0:T(1024)(128)(2,1)}, u32[]{:S(2)}) copy-start(bf16[8192]{0:T(1024)(128)(2,1)} %param.9) | copy-start | bytes 49156
  2.4 8.2 %copy-start.8 = (bf16[1024]{0:T(1024)(128)(2,1)S(1)}, bf16[1024]{0:T(1024)(128)(2,1)}, u32[]{:S(2)}) copy-start(bf16[1024]{0:T(1024)(128)(2,1)} %param.13) | copy-start | bytes 6148
  2.4 8.2 %copy-start.9 = (bf16[128]{0:T(256)(128)(2,1)S(1)}, bf16[128]{0:T(256)(128)(2,1)}, u32[]{:S(2)}) copy-start(bf16[128]{0:T(256)(128)(2,1)} %param.15) | copy-start | bytes 772
  2.4 8.2 %copy-start.10 = (bf16[128]{0:T(256)(128)(2,1)S(1)}, bf16[128]{0:T(256)(128)(2,1)}, u32[]{:S(2)}) copy-start(bf16[128]{0:T(256)(128)(2,1)} %param.14) | copy-start | bytes 772
  2.4 18.5 %collective-permute-start = (bf16[256,1280]{1,0:T(8,128)(2,1)}, bf16[256,1280]{1,0:T(8,128)(2,1)S(1)}, u32[]{:S(2)}, u32[]{:S(2)}) collective-permute-start(bf16[256,1280]{1,0:T(8,128)(2,1)} %get-tuple-element.48), channel_id=1, source_target_pairs={{0,8},{8,0},{16,24},{24,16},{1,9},{9,1},{17,25},{25,17},{2,10},{10... | collective-permute-start | bytes 1966088 | tf_op jit(solution)/shard_map/ppermute | solution.py:485
  2.6 18.8 %collective-permute-start.1 = (bf16[256,1280]{1,0:T(8,128)(2,1)}, bf16[256,1280]{1,0:T(8,128)(2,1)}, u32[]{:S(2)}, u32[]{:S(2)}) collective-permute-start(bf16[256,1280]{1,0:T(8,128)(2,1)} %get-tuple-element.48), channel_id=1, source_target_pairs={{8,16},{16,8},{9,17},{17,9},{10,18},{18,10},{11,19},{19,11},{12,20... | collective-permute-start | bytes 1966088 | tf_op jit(solution)/shard_map/ppermute | solution.py:486
  7.0 14.0 %collective-permute-start.2 = (bf16[256,1152]{1,0:T(8,128)(2,1)}, bf16[256,1152]{1,0:T(8,128)(2,1)}, u32[]{:S(2)}, u32[]{:S(2)}) collective-permute-start(bf16[256,1152]{1,0:T(8,128)(2,1)} %get-tuple-element.49), channel_id=1, source_target_pairs={{0,4},{4,0},{1,5},{5,1},{2,6},{6,2},{3,7},{7,3},{8,12},{12,8},{9,1... | collective-permute-start | bytes 1769480 | tf_op jit(solution)/shard_map/ppermute | solution.py:487
  8.3 40.0 %copy-start.2 = (bf16[1024,1024]{1,0:T(8,128)(2,1)S(1)}, bf16[1024,1024]{1,0:T(8,128)(2,1)}, u32[]{:S(2)}) copy-start(bf16[1024,1024]{1,0:T(8,128)(2,1)} %refs_7_.1) | copy-start | bytes 6291460
  20.9 0.8 copy-start.5
  21.8 13.7 %collective-permute-start.5 = (bf16[256,1280]{1,0:T(8,128)(2,1)}, bf16[256,1280]{1,0:T(8,128)(2,1)}, u32[]{:S(2)}, u32[]{:S(2)}) collective-permute-start(bf16[256,1280]{1,0:T(8,128)(2,1)} %collective-permute-done.1), channel_id=1, source_target_pairs={{8,0},{16,24},{9,1},{17,25},{10,2},{18,26},{11,3},{19,27},{12,4},{... | collective-permute-start | bytes 1966088 | tf_op jit(solution)/shard_map/ppermute | solution.py:502
  23.9 18.0 %collective-permute-start.7 = (bf16[256,1536]{1,0:T(8,128)(2,1)}, bf16[256,1536]{1,0:T(8,128)(2,1)S(1)}, u32[]{:S(2)}, u32[]{:S(2)}) collective-permute-start(bf16[256,1536]{1,0:T(8,128)(2,1)} %pack.3), channel_id=1, source_target_pairs={{0,4},{4,0},{1,5},{5,1},{2,6},{6,2},{3,7},{7,3},{8,12},{12,8},{9,1... | collective-permute-start | bytes 2359304 | tf_op jit(solution)/shard_map/ppermute | solution.py:504
  25.2 16.0 %collective-permute-start.3 = (bf16[256,1280]{1,0:T(8,128)(2,1)}, bf16[256,1280]{1,0:T(8,128)(2,1)}, u32[]{:S(2)}, u32[]{:S(2)}) collective-permute-start(bf16[256,1280]{1,0:T(8,128)(2,1)} %copy-done.5), channel_id=1, source_target_pairs={{8,16},{16,8},{9,17},{17,9},{10,18},{18,10},{11,19},{19,11},{12,20... | collective-permute-start | bytes 1966088 | tf_op jit(solution)/shard_map/ppermute | solution.py:501
  27.8 14.1 %collective-permute-start.6 = (bf16[256,1280]{1,0:T(8,128)(2,1)}, bf16[256,1280]{1,0:T(8,128)(2,1)}, u32[]{:S(2)}, u32[]{:S(2)}) collective-permute-start(bf16[256,1280]{1,0:T(8,128)(2,1)} %copy-done.5), channel_id=1, source_target_pairs={{0,2},{1,3},{2,0},{3,1},{4,6},{5,7},{6,4},{7,5},{8,10},{9,11},{10,... | collective-permute-start | bytes 1966088 | tf_op jit(solution)/shard_map/ppermute | solution.py:503
  28.2 13.8 %collective-permute-start.8 = (bf16[256,1280]{1,0:T(8,128)(2,1)}, bf16[256,1280]{1,0:T(8,128)(2,1)}, u32[]{:S(2)}, u32[]{:S(2)}) collective-permute-start(bf16[256,1280]{1,0:T(8,128)(2,1)} %copy-done.5), channel_id=1, source_target_pairs={{0,1},{1,0},{2,3},{3,2},{4,5},{5,4},{6,7},{7,6},{8,9},{9,8},{10,11... | collective-permute-start | bytes 1966088 | tf_op jit(solution)/shard_map/ppermute | solution.py:505
  31.0 2.2 %copy-start = (bf16[1,256,8192]{2,1,0:T(8,128)(2,1)S(1)}, bf16[1,256,8192]{2,1,0:T(8,128)(2,1)}, u32[]{:S(2)}) copy-start(bf16[1,256,8192]{2,1,0:T(8,128)(2,1)} %param.8) | copy-start | bytes 12582916
  33.2 15.1 %copy-start.1 = (bf16[1,256,8192]{2,1,0:T(8,128)(2,1)S(1)}, bf16[1,256,8192]{2,1,0:T(8,128)(2,1)}, u32[]{:S(2)}) copy-start(bf16[1,256,8192]{2,1,0:T(8,128)(2,1)} %param.8) | copy-start | bytes 12582916
  33.2 15.1 %copy-start.3 = (bf16[1024,128]{1,0:T(8,128)(2,1)S(1)}, bf16[1024,128]{1,0:T(8,128)(2,1)}, u32[]{:S(2)}) copy-start(bf16[1024,128]{1,0:T(8,128)(2,1)} %refs_5_.1) | copy-start | bytes 786436
  33.2 15.1 %copy-start.4 = (bf16[1024,128]{1,0:T(8,128)(2,1)S(1)}, bf16[1024,128]{1,0:T(8,128)(2,1)}, u32[]{:S(2)}) copy-start(bf16[1024,128]{1,0:T(8,128)(2,1)} %refs_6_.1) | copy-start | bytes 786436
  33.2 15.1 %copy-start.6 = (bf16[256,1280]{1,0:T(8,128)(2,1)S(1)}, bf16[256,1280]{1,0:T(8,128)(2,1)}, u32[]{:S(2)}) copy-start(bf16[256,1280]{1,0:T(8,128)(2,1)} %copy-done.5) | copy-start | bytes 1966084
  35.5 5.6 %collective-permute-start.4 = (f32[1,256]{1,0:T(1,128)S(1)}, f32[1,256]{1,0:T(1,128)S(1)}, u32[]{:S(2)}, u32[]{:S(2)}) collective-permute-start(f32[1,256]{1,0:T(1,128)S(1)} %get-tuple-element.52), channel_id=1, source_target_pairs={{0,4},{4,0},{1,5},{5,1},{2,6},{6,2},{3,7},{7,3},{8,12},{12,8},{9,1... | collective-permute-start | bytes 3080 | tf_op jit(solution)/shard_map/ppermute | solution.py:507
  41.9 6.3 %collective-permute-start.13 = (bf16[256,1280]{1,0:T(8,128)(2,1)}, bf16[256,1280]{1,0:T(8,128)(2,1)S(1)}, u32[]{:S(2)}, u32[]{:S(2)}) collective-permute-start(bf16[256,1280]{1,0:T(8,128)(2,1)} %collective-permute-done.6.refs_9_), channel_id=1, source_target_pairs={{0,1},{1,0},{2,3},{3,2},{4,5},{5,4},{6,7},{7,6},{8,9},{9,8},{10,11... | collective-permute-start | bytes 1966088 | tf_op jit(solution)/shard_map/ppermute | solution.py:515
  45.4 15.9 %collective-permute-start.9 = (bf16[256,1280]{1,0:T(8,128)(2,1)}, bf16[256,1280]{1,0:T(8,128)(2,1)S(1)}, u32[]{:S(2)}, u32[]{:S(2)}) collective-permute-start(bf16[256,1280]{1,0:T(8,128)(2,1)} %collective-permute-done.3), channel_id=1, source_target_pairs={{8,0},{16,24},{9,1},{17,25},{10,2},{18,26},{11,3},{19,27},{12,4},{... | collective-permute-start | bytes 1966088 | tf_op jit(solution)/shard_map/ppermute | solution.py:512
  46.7 16.4 %collective-permute-start.10 = (bf16[256,1280]{1,0:T(8,128)(2,1)S(1)}, bf16[256,1280]{1,0:T(8,128)(2,1)S(1)}, u32[]{:S(2)}, u32[]{:S(2)}) collective-permute-start(bf16[256,1280]{1,0:T(8,128)(2,1)S(1)} %broadcast_select_fusion.1.refs_5_), channel_id=1, source_target_pairs={{0,2},{1,3},{2,0},{3,1},{4,6},{5,7},{6,4},{7,5},{8,10},{9,11},{10,... | collective-permute-start | bytes 1966088 | tf_op jit(solution)/shard_map/ppermute | solution.py:513
  47.0 16.1 %collective-permute-start.12 = (bf16[256,1280]{1,0:T(8,128)(2,1)S(1)}, bf16[256,1280]{1,0:T(8,128)(2,1)S(1)}, u32[]{:S(2)}, u32[]{:S(2)}) collective-permute-start(bf16[256,1280]{1,0:T(8,128)(2,1)S(1)} %broadcast_select_fusion.1.refs_5_), channel_id=1, source_target_pairs={{0,1},{1,0},{2,3},{3,2},{4,5},{5,4},{6,7},{7,6},{8,9},{9,8},{10,11... | collective-permute-start | bytes 1966088 | tf_op jit(solution)/shard_map/ppermute | solution.py:516
  47.3 17.5 %collective-permute-start.11 = (bf16[256,1408]{1,0:T(8,128)(2,1)S(1)}, bf16[256,1408]{1,0:T(8,128)(2,1)S(1)}, u32[]{:S(2)}, u32[]{:S(2)}) collective-permute-start(bf16[256,1408]{1,0:T(8,128)(2,1)S(1)} %get-tuple-element.59), channel_id=1, source_target_pairs={{0,4},{4,0},{1,5},{5,1},{2,6},{6,2},{3,7},{7,3},{8,12},{12,8},{9,1... | collective-permute-start | bytes 2162696 | tf_op jit(solution)/shard_map/ppermute | solution.py:514
  64.9 2.7 %collective-permute-start.15 = (bf16[256,1280]{1,0:T(8,128)(2,1)S(1)}, bf16[256,1280]{1,0:T(8,128)(2,1)S(1)}, u32[]{:S(2)}, u32[]{:S(2)}) collective-permute-start(bf16[256,1280]{1,0:T(8,128)(2,1)S(1)} %collective-permute-done.10.refs_6_), channel_id=1, source_target_pairs={{0,1},{1,0},{2,3},{3,2},{4,5},{5,4},{6,7},{7,6},{8,9},{9,8},{10,11... | collective-permute-start | bytes 1966088 | tf_op jit(solution)/shard_map/ppermute | solution.py:534
  65.9 10.3 %collective-permute-start.16 = (bf16[256,1280]{1,0:T(8,128)(2,1)S(1)}, bf16[256,1280]{1,0:T(8,128)(2,1)S(1)}, u32[]{:S(2)}, u32[]{:S(2)}) collective-permute-start(bf16[256,1280]{1,0:T(8,128)(2,1)S(1)} %broadcast_select_fusion.refs_0_), channel_id=1, source_target_pairs={{0,1},{1,0},{2,3},{3,2},{4,5},{5,4},{6,7},{7,6},{8,9},{9,8},{10,11... | collective-permute-start | bytes 1966088 | tf_op jit(solution)/shard_map/ppermute | solution.py:535
  65.9 10.2 %collective-permute-start.14 = (bf16[256,768]{1,0:T(8,128)(2,1)S(1)}, bf16[256,768]{1,0:T(8,128)(2,1)S(1)}, u32[]{:S(2)}, u32[]{:S(2)}) collective-permute-start(bf16[256,768]{1,0:T(8,128)(2,1)S(1)} %slice.6), channel_id=1, source_target_pairs={{0,2},{1,3},{2,0},{3,1},{4,6},{5,7},{6,4},{7,5},{8,10},{9,11},{10,... | collective-permute-start | bytes 1179656 | tf_op jit(solution)/shard_map/ppermute | solution.py:533
  76.2 2.7 %collective-permute-start.17 = (bf16[256,768]{1,0:T(8,128)(2,1)S(1)}, bf16[256,768]{1,0:T(8,128)(2,1)S(1)}, u32[]{:S(2)}, u32[]{:S(2)}) collective-permute-start(bf16[256,768]{1,0:T(8,128)(2,1)S(1)} %collective-permute-done.14.refs_1_), channel_id=1, source_target_pairs={{0,1},{1,0},{2,3},{3,2},{4,5},{5,4},{6,7},{7,6},{8,9},{9,8},{10,11... | collective-permute-start | bytes 1179656 | tf_op jit(solution)/shard_map/ppermute | solution.py:553
  77.5 8.0 %collective-permute-start.19 = (bf16[256,512]{1,0:T(8,128)(2,1)S(1)}, bf16[256,512]{1,0:T(8,128)(2,1)S(1)}, u32[]{:S(2)}, u32[]{:S(2)}) collective-permute-start(bf16[256,512]{1,0:T(8,128)(2,1)S(1)} %slice.7), channel_id=1, source_target_pairs={{0,2},{1,3},{2,0},{3,1},{4,6},{5,7},{6,4},{7,5},{8,10},{9,11},{10,... | collective-permute-start | bytes 786440 | tf_op jit(solution)/shard_map/ppermute | solution.py:552
  80.3 5.2 %collective-permute-start.18 = (bf16[256,256]{1,0:T(8,128)(2,1)S(1)}, bf16[256,256]{1,0:T(8,128)(2,1)S(1)}, u32[]{:S(2)}, u32[]{:S(2)}) collective-permute-start(bf16[256,256]{1,0:T(8,128)(2,1)S(1)} %get-tuple-element.79), channel_id=1, source_target_pairs={{0,4},{4,0},{1,5},{5,1},{2,6},{6,2},{3,7},{7,3},{8,12},{12,8},{9,1... | collective-permute-start | bytes 393224 | tf_op jit(solution)/shard_map/ppermute | solution.py:561
  85.5 3.1 %collective-permute-start.20 = (bf16[256,512]{1,0:T(8,128)(2,1)S(1)}, bf16[256,512]{1,0:T(8,128)(2,1)S(1)}, u32[]{:S(2)}, u32[]{:S(2)}) collective-permute-start(bf16[256,512]{1,0:T(8,128)(2,1)S(1)} %collective-permute-done.19.refs_1_), channel_id=1, source_target_pairs={{0,1},{1,0},{2,3},{3,2},{4,5},{5,4},{6,7},{7,6},{8,9},{9,8},{10,11... | collective-permute-start | bytes 786440 | tf_op jit(solution)/shard_map/ppermute | solution.py:564
  86.3 10.9 %collective-permute-start.25 = (bf16[256,512]{1,0:T(8,128)(2,1)S(1)}, bf16[256,512]{1,0:T(8,128)(2,1)S(1)}, u32[]{:S(2)}, u32[]{:S(2)}) collective-permute-start(bf16[256,512]{1,0:T(8,128)(2,1)S(1)} %get-tuple-element.90), channel_id=1, source_target_pairs={{0,4},{4,0},{1,5},{5,1},{2,6},{6,2},{3,7},{7,3},{8,12},{12,8},{9,1... | collective-permute-start | bytes 786440 | tf_op jit(solution)/shard_map/ppermute | solution.py:562
  87.4 6.7 %collective-permute-start.23 = (bf16[256,256]{1,0:T(8,128)(2,1)S(1)}, bf16[256,256]{1,0:T(8,128)(2,1)S(1)}, u32[]{:S(2)}, u32[]{:S(2)}) collective-permute-start(bf16[256,256]{1,0:T(8,128)(2,1)S(1)} %key_value.1.refs_0_), channel_id=1, source_target_pairs={{0,2},{1,3},{4,6},{5,7},{8,10},{9,11},{12,14},{13,15},{16,18},{17,... | collective-permute-start | bytes 393224 | tf_op jit(solution)/shard_map/ppermute | solution.py:583
  89.5 10.9 %collective-permute-start.21 = (bf16[256,512]{1,0:T(8,128)(2,1)S(1)}, bf16[256,512]{1,0:T(8,128)(2,1)S(1)}, u32[]{:S(2)}, u32[]{:S(2)}) collective-permute-start(bf16[256,512]{1,0:T(8,128)(2,1)S(1)} %get-tuple-element.82), channel_id=1, source_target_pairs={{0,4},{4,0},{1,5},{5,1},{2,6},{6,2},{3,7},{7,3},{8,12},{12,8},{9,1... | collective-permute-start | bytes 786440 | tf_op jit(solution)/shard_map/ppermute | solution.py:572
  90.1 7.1 %collective-permute-start.22 = (bf16[256,256]{1,0:T(8,128)(2,1)S(1)}, bf16[256,256]{1,0:T(8,128)(2,1)S(1)}, u32[]{:S(2)}, u32[]{:S(2)}) collective-permute-start(bf16[256,256]{1,0:T(8,128)(2,1)S(1)} %key_value.1.refs_0_), channel_id=1, source_target_pairs={{0,1},{1,0},{2,3},{3,2},{4,5},{5,4},{6,7},{7,6},{8,9},{9,8},{10,11... | collective-permute-start | bytes 393224 | tf_op jit(solution)/shard_map/ppermute | solution.py:584
  94.1 4.0 %collective-permute-start.24 = (bf16[256,256]{1,0:T(8,128)(2,1)S(1)}, bf16[256,256]{1,0:T(8,128)(2,1)S(1)}, u32[]{:S(2)}, u32[]{:S(2)}) collective-permute-start(bf16[256,256]{1,0:T(8,128)(2,1)S(1)} %collective-permute-done.23.refs_2_), channel_id=1, source_target_pairs={{2,3},{3,2},{6,7},{7,6},{10,11},{11,10},{14,15},{15,14},{18,19},{1... | collective-permute-start | bytes 393224 | tf_op jit(solution)/shard_map/ppermute | solution.py:585

commit v6 on v5

--- a/solution.py
+++ b/solution.py
@@ -396,12 +396,16 @@
 
 def key_value_body(sums, back, bias, cosine, sine_table, out):
     head = out.shape[1] // 2
-    total = sums[...] + back[:, : 2 * head].astype(jnp.float32) + bias[...]
+    total = sums[:, : 2 * head] + back[:, : 2 * head].astype(jnp.float32) + bias[...]
     out[:, :head] = turned(total[:, :head], cosine[...], sine_table[...]).astype(jnp.bfloat16)
     out[:, head:] = total[:, head:].astype(jnp.bfloat16)
 
 
-def attention_body(scale, first, sums, back, bias, cosine, sine_table, *refs):
+def attention_body(scale, first, skips, *refs):
+    groups = len(skips)
+    sums, refs = (refs[:groups], refs[groups:])
+    backs, refs = (refs[:groups], refs[groups:])
+    bias, cosine, sine_table, *refs = refs
     blocks, refs = (refs[:4], refs[4:])
     if first:
         done, *refs = refs
@@ -418,33 +422,37 @@
     visible = lax.broadcasted_iota(jnp.int32, (rows, total_keys), 1) <= row_ids
     if first:
         out[:, :first] = done[...]
-    for at in range(0, sums.shape[1], head):
-        cols = pl.ds(at, head)
-        skipped = back.shape[1] - sums.shape[1]
-        query = sums[:, cols] + back[:, skipped + at : skipped + at + head].astype(jnp.float32)
-        query = query + bias[:, first + at : first + at + head]
-        query = turned(query, cosine[...], sine_table[...]).astype(jnp.bfloat16)
-        scores = lax.dot_general(
-            query, keys[...], (((1,), (1,)), ((), ())), preferred_element_type=jnp.float32
-        )
-        scores = jnp.where(visible, scores * scale, masked_score)
-        exps = jnp.exp(scores - jnp.max(scores, axis=1, keepdims=True))
-        length = jnp.sum(exps, axis=1, keepdims=True)
-        mixed = jnp.dot(exps.astype(jnp.bfloat16), values[...], preferred_element_type=jnp.float32)
-        out[:, first + at : first + at + head] = (mixed / length).astype(jnp.bfloat16)
-
-
-def attention(sums, back, bias, cosine, sine_table, blocks, done=None):
-    rows, width = sums.shape
+    at = first
+    for own, other, skip in zip(sums, backs, skips):
+        for column in range(skip, own.shape[1], head):
+            cols = slice(column, column + head)
+            query = own[:, cols] + other[:, cols].astype(jnp.float32) + bias[:, at : at + head]
+            query = turned(query, cosine[...], sine_table[...]).astype(jnp.bfloat16)
+            scores = lax.dot_general(
+                query, keys[...], (((1,), (1,)), ((), ())), preferred_element_type=jnp.float32
+            )
+            scores = jnp.where(visible, scores * scale, masked_score)
+            exps = jnp.exp(scores - jnp.max(scores, axis=1, keepdims=True))
+            length = jnp.sum(exps, axis=1, keepdims=True)
+            mixed = jnp.dot(
+                exps.astype(jnp.bfloat16), values[...], preferred_element_type=jnp.float32
+            )
+            out[:, at : at + head] = (mixed / length).astype(jnp.bfloat16)
+            at += head
+
+
+def attention(sums, backs, skips, bias, cosine, sine_table, blocks, done=None):
+    rows = sums[0].shape[0]
+    width = sum(own.shape[1] - skip for own, skip in zip(sums, skips))
     head = cosine.shape[1]
     first = 0 if done is None else done.shape[1]
     inside = pl.BlockSpec(memory_space=pltpu.VMEM)
-    args = [sums, back, bias, cosine, sine_table, *blocks]
+    args = [*sums, *backs, bias, cosine, sine_table, *blocks]
     if first:
         args.append(done)
     total = 4 * rows * rows * (width // head)
     return pl.pallas_call(
-        functools.partial(attention_body, head ** (-0.5), first),
+        functools.partial(attention_body, head ** (-0.5), first, skips),
         out_shape=jax.ShapeDtypeStruct((rows, first + width), jnp.bfloat16),
         in_specs=[inside] * len(args),
         out_specs=inside,
@@ -475,9 +483,9 @@
     beside = [(i, i ^ 1) for i in range(4)]
     held = lax.optimization_barrier
     cut = depth // 8
-    parts_1 = ((0, 0, depth), (1, 0, cut))
-    parts_2 = ((1, cut, 7 * cut), (2, 0, 5 * cut))
-    parts_3 = ((2, 5 * cut, 3 * cut), (3, 0, depth))
+    parts_1 = ((0, 0, depth), (1, 0, 2 * cut))
+    parts_2 = ((1, 2 * cut, 6 * cut), (2, 0, 6 * cut))
+    parts_3 = ((2, 6 * cut, 2 * cut), (3, 0, depth))
     mine, sent_1 = pack(tokens, depth, (parts_1,), (w_key, w_value, w_query))
     kv_width = 2 * head
     half = kv_width + w_query.shape[1] // 2
@@ -516,7 +524,7 @@
     third_side = lax.ppermute(third, "ctx", beside)
     before = early_slots(
         (0, 1),
-        ((0, 0, 9 * cut), (1, 0, 7 * cut)),
+        ((0, 0, 10 * cut), (1, 0, 6 * cut)),
         True,
         False,
         tokens,
@@ -535,7 +543,7 @@
     fourth_side = lax.ppermute(fourth, "ctx", beside)
     before, last_rows = early_slots(
         (2, 3),
-        ((0, 7 * cut, 5 * cut), (1, 0, 11 * cut)),
+        ((0, 6 * cut, 6 * cut), (1, 0, 10 * cut)),
         False,
         True,
         tokens,
@@ -551,18 +559,19 @@
     )
     fourth_far_2 = lax.ppermute(fourth[:, half:], "ctx", across)
     fourth_corner_1 = lax.ppermute(fourth_far_1, "ctx", beside)
-    kv_sums, q_sums_1, back_kv, back_1 = late_slot(
+    early_width = kv_width
+    sums_0, sums_1, back_0, back_1 = late_slot(
         0,
-        (kv_width, half - kv_width),
+        (early_width, half - early_width),
         before,
         last_rows,
         (fourth, fourth_far_1, fourth_side, fourth_corner_1),
     )
-    back_kv = lax.ppermute(back_kv, "pair", swap)
+    back_0 = lax.ppermute(back_0, "pair", swap)
     back_1 = lax.ppermute(back_1, "pair", swap)
-    back_kv, fourth_far_2 = held((back_kv, fourth_far_2))
+    back_0, fourth_far_2 = held((back_0, fourth_far_2))
     fourth_corner_2 = lax.ppermute(fourth_far_2, "ctx", beside)
-    q_sums_2, back_2 = late_slot(
+    sums_2, back_2 = late_slot(
         half,
         (rest,),
         before,
@@ -579,13 +588,14 @@
         out_specs=inside,
         compiler_params=pltpu.CompilerParams(vmem_limit_bytes=4 * 2**20),
         name="key_value",
-    )(kv_sums, back_kv, bias_kv, cosine, sine_table)
+    )(sums_0, back_0, bias_kv, cosine, sine_table)
     kv_across = lax.ppermute(key_value, "ctx", [(0, 2), (1, 3)])
     kv_beside = lax.ppermute(key_value, "ctx", beside)
     kv_corner = lax.ppermute(kv_across, "ctx", [(2, 3), (3, 2)])
     blocks = (key_value, kv_beside, kv_across, kv_corner)
-    attended = attention(q_sums_1, back_1, bias_q, cosine, sine_table, blocks)
-    attended = attention(q_sums_2, back_2, bias_q, cosine, sine_table, blocks, attended)
+    tables = (bias_q, cosine, sine_table, blocks)
+    attended = attention((sums_0, sums_1), (back_0, back_1), (kv_width, 0), *tables)
+    attended = attention((sums_2,), (back_2,), (0,), *tables, attended)
     return attended[None]
 
 

time: 105 us -> 104 us (level)
    ppermute x1, waiting for transfers between devices: 9.65 us -> 0.93 us  [planned(): came_1 = lax.ppermute(sent_1, 'pair', swap)]
    ppermute x1, waiting for transfers between devices: 0.01 us -> 7.11 us  [planned(): second = lax.ppermute(mine, 'line', ends)]
    ppermute x1, waiting for transfers between devices: 0.47 us -> 3.02 us  [planned(): third_in = lax.ppermute(mine, 'line', middle)]
    ppermute x1, waiting for transfers between devices: 1.74 us -> 0.33 us  [planned(): came_3 = lax.ppermute(sent_3, 'pair', swap)]
  transfers between devices with their start and end apart: 26 -> 26, of which waited for: 14 -> 15; matrix products, arithmetic and copies ran while one was open for 3% -> 3% of each run, Pallas kernels for 16% -> 16%
where the time goes in v6:
time: 104 us; the launch traced here: 103 us
  waiting for transfers between devices  38.3 us (37%)
  starting transfers between devices  36.4 us (35%)
  Pallas kernels  22.4 us (22%)
  other arithmetic  3.07 us (3%)
  local copies, waits for them, and re-layouts  2.3 us (2%)
    ppermute x1, waiting for transfers between devices, planned(): fourth_out = lax.ppermute(fourth_in, 'line', outward)  8.08 us
    pallas_call x2, Pallas kernels, early_slots(): pl.pallas_call(functools.partial(early_body, slots, guests, local, final)...  7.93 us
    ppermute x1, waiting for transfers between devices, planned(): second = lax.ppermute(mine, 'line', ends)  7.11 us
    pallas_call x2, Pallas kernels, attention(): pl.pallas_call(functools.partial(attention_body, head ** (-0.5), first, s...  5.51 us
    ppermute x1, waiting for transfers between devices, planned(): fourth_far_1 = lax.ppermute(fourth[:, :half], 'ctx', across)  5.39 us
    pallas_call x2, Pallas kernels, pack(): pl.pallas_call(functools.partial(pack_body, sent_parts, len(weights), dep...  4.59 us
    ppermute x1, starting transfers between devices, planned(): third_in = lax.ppermute(mine, 'line', middle)  4.32 us
    ppermute x1, waiting for transfers between devices, planned(): fourth_far_2 = lax.ppermute(fourth[:, half:], 'ctx', across)  4.07 us
  transfers between devices with their start and end apart: 26, of which 15 were waited for; matrix products, arithmetic and copies ran while one was open for 3% of the time, Pallas kernels for 16%

profile of v6, /device:TPU:11, one launch (start us, length us, event | category | flops | bytes accessed | tf_op | source)
XLA Modules:
  0.0 102.8 jit_solution(7918736587056990196)
XLA Ops:
  0.0 2.4 %pack.2 = (bf16[256,1280]{1,0:T(8,128)(2,1)}, bf16[256,1280]{1,0:T(8,128)(2,1)}) custom-call(bf16[256,8192]{1,0:T(8,128)(2,1)} %bitcast.9, bf16[1024,128]{1,0:T(8,128)(2,1)} %refs_5_.1, bf16[1024,128]{1,0:T(8,128)(2,1)} %refs_6_.1, bf16[1024,1024]{1,0:T(8,128)(2,1)} %refs_7_.1), custom_call_target="tpu_custom_call" | custom-call | tf_op jit(solution)/shard_map/pack/pallas_call | solution.py:171
  2.7 4.3 %collective-permute-start.1 = (bf16[256,1280]{1,0:T(8,128)(2,1)}, bf16[256,1280]{1,0:T(8,128)(2,1)}, u32[]{:S(2)}, u32[]{:S(2)}) collective-permute-start(bf16[256,1280]{1,0:T(8,128)(2,1)} %get-tuple-element.48), channel_id=1, source_target_pairs={{8,16},{16,8},{9,17},{17,9},{10,18},{18,10},{11,19},{19,11},{12,20... | collective-permute-start | bytes 1966088 | tf_op jit(solution)/shard_map/ppermute | solution.py:494
  7.0 1.3 %collective-permute-start.2 = (bf16[256,1280]{1,0:T(8,128)(2,1)}, bf16[256,1280]{1,0:T(8,128)(2,1)}, u32[]{:S(2)}, u32[]{:S(2)}) collective-permute-start(bf16[256,1280]{1,0:T(8,128)(2,1)} %get-tuple-element.49), channel_id=1, source_target_pairs={{0,4},{4,0},{1,5},{5,1},{2,6},{6,2},{3,7},{7,3},{8,12},{12,8},{9,1... | collective-permute-start | bytes 1966088 | tf_op jit(solution)/shard_map/ppermute | solution.py:495
  8.3 2.2 %pack.3 = bf16[256,1536]{1,0:T(8,128)(2,1)} custom-call(bf16[256,8192]{1,0:T(8,128)(2,1)} %bitcast.10), custom_call_target="tpu_custom_call" | custom-call | tf_op jit(solution)/shard_map/pack/pallas_call | solution.py:171
  10.6 0.5 fusion
  11.3 7.1 %collective-permute-done.refs_8_ = bf16[256,1280]{1,0:T(8,128)(2,1)S(1)} collective-permute-done((bf16[256,1280]{1,0:T(8,128)(2,1)}, bf16[256,1280]{1,0:T(8,128)(2,1)S(1)}, u32[]{:S(2)}, u32[]{:S(2)}) %collective-permute-start) | collective-permute-done | bytes 655392 | tf_op jit(solution)/shard_map/ppermute | solution.py:493
  18.4 3.0 %collective-permute-done.1 = bf16[256,1280]{1,0:T(8,128)(2,1)} collective-permute-done((bf16[256,1280]{1,0:T(8,128)(2,1)}, bf16[256,1280]{1,0:T(8,128)(2,1)}, u32[]{:S(2)}, u32[]{:S(2)}) %collective-permute-start.1) | collective-permute-done | bytes 655392 | tf_op jit(solution)/shard_map/ppermute | solution.py:494
  21.5 0.9 collective-permute-done.2.refs_0_
  22.4 2.2 %collective-permute-start.5 = (bf16[256,1280]{1,0:T(8,128)(2,1)}, bf16[256,1280]{1,0:T(8,128)(2,1)}, u32[]{:S(2)}, u32[]{:S(2)}) collective-permute-start(bf16[256,1280]{1,0:T(8,128)(2,1)} %collective-permute-done.1), channel_id=1, source_target_pairs={{8,0},{16,24},{9,1},{17,25},{10,2},{18,26},{11,3},{19,27},{12,4},{... | collective-permute-start | bytes 1966088 | tf_op jit(solution)/shard_map/ppermute | solution.py:510
  24.6 1.2 %collective-permute-start.7 = (bf16[256,1536]{1,0:T(8,128)(2,1)}, bf16[256,1536]{1,0:T(8,128)(2,1)S(1)}, u32[]{:S(2)}, u32[]{:S(2)}) collective-permute-start(bf16[256,1536]{1,0:T(8,128)(2,1)} %pack.3), channel_id=1, source_target_pairs={{0,4},{4,0},{1,5},{5,1},{2,6},{6,2},{3,7},{7,3},{8,12},{12,8},{9,1... | collective-permute-start | bytes 2359304 | tf_op jit(solution)/shard_map/ppermute | solution.py:512
  25.8 2.5 %collective-permute-start.3 = (bf16[256,1280]{1,0:T(8,128)(2,1)}, bf16[256,1280]{1,0:T(8,128)(2,1)}, u32[]{:S(2)}, u32[]{:S(2)}) collective-permute-start(bf16[256,1280]{1,0:T(8,128)(2,1)} %copy-done.5), channel_id=1, source_target_pairs={{8,16},{16,8},{9,17},{17,9},{10,18},{18,10},{11,19},{19,11},{12,20... | collective-permute-start | bytes 1966088 | tf_op jit(solution)/shard_map/ppermute | solution.py:509
  28.3 0.3 collective-permute-start.6
  28.6 3.0 %collective-permute-start.8 = (bf16[256,1280]{1,0:T(8,128)(2,1)}, bf16[256,1280]{1,0:T(8,128)(2,1)}, u32[]{:S(2)}, u32[]{:S(2)}) collective-permute-start(bf16[256,1280]{1,0:T(8,128)(2,1)} %copy-done.5), channel_id=1, source_target_pairs={{0,1},{1,0},{2,3},{3,2},{4,5},{5,4},{6,7},{7,6},{8,9},{9,8},{10,11... | collective-permute-start | bytes 1966088 | tf_op jit(solution)/shard_map/ppermute | solution.py:513
  31.6 2.2 %copy-done = bf16[1,256,8192]{2,1,0:T(8,128)(2,1)S(1)} copy-done((bf16[1,256,8192]{2,1,0:T(8,128)(2,1)S(1)}, bf16[1,256,8192]{2,1,0:T(8,128)(2,1)}, u32[]{:S(2)}) %copy-start) | copy-done | bytes 4194328
  33.8 2.0 %prepare.1 = (bf16[256,1280]{1,0:T(8,128)(2,1)S(1)}, f32[256,128]{1,0:T(8,128)S(1)}, f32[1,256]{1,0:T(1,128)S(1)}) custom-call(bf16[256,8192]{1,0:T(8,128)(2,1)S(1)} %bitcast.11), custom_call_target="tpu_custom_call" | custom-call | tf_op jit(solution)/shard_map/prepare/pallas_call | solution.py:224
  36.1 1.2 %collective-permute-start.4 = (f32[1,256]{1,0:T(1,128)S(1)}, f32[1,256]{1,0:T(1,128)S(1)}, u32[]{:S(2)}, u32[]{:S(2)}) collective-permute-start(f32[1,256]{1,0:T(1,128)S(1)} %get-tuple-element.52), channel_id=1, source_target_pairs={{0,4},{4,0},{1,5},{5,1},{2,6},{6,2},{3,7},{7,3},{8,12},{12,8},{9,1... | collective-permute-start | bytes 3080 | tf_op jit(solution)/shard_map/ppermute | solution.py:515
  37.4 1.2 %broadcast_select_fusion.1.refs_5_ = bf16[256,1280]{1,0:T(8,128)(2,1)S(1)} fusion(bf16[256,1280]{1,0:T(8,128)(2,1)} %collective-permute-done.1, bf16[256,1280]{1,0:T(8,128)(2,1)} %collective-permute-done.5, pred[]{:T(512)S(6)} %or.3), kind=kLoop, calls=%fused_computation.1 | loop fusion | flops 327680 | bytes 1966081 | tf_op jit(solution)/shard_map/jit(_where)/select_n | solution.py:516
  38.5 3.2 %collective-permute-done.4.refs_3_ = f32[1,256]{1,0:T(1,128)S(1)} collective-permute-done((f32[1,256]{1,0:T(1,128)S(1)}, f32[1,256]{1,0:T(1,128)S(1)}, u32[]{:S(2)}, u32[]{:S(2)}) %collective-permute-start.4) | collective-permute-done | bytes 1056 | tf_op jit(solution)/shard_map/ppermute | solution.py:515
  41.8 0.4 collective-permute-done.6.refs_9_
  42.2 3.6 %collective-permute-start.13 = (bf16[256,1280]{1,0:T(8,128)(2,1)}, bf16[256,1280]{1,0:T(8,128)(2,1)S(1)}, u32[]{:S(2)}, u32[]{:S(2)}) collective-permute-start(bf16[256,1280]{1,0:T(8,128)(2,1)} %collective-permute-done.6.refs_9_), channel_id=1, source_target_pairs={{0,1},{1,0},{2,3},{3,2},{4,5},{5,4},{6,7},{7,6},{8,9},{9,8},{10,11... | collective-permute-start | bytes 1966088 | tf_op jit(solution)/shard_map/ppermute | solution.py:523
  45.9 1.3 %collective-permute-start.9 = (bf16[256,1280]{1,0:T(8,128)(2,1)}, bf16[256,1280]{1,0:T(8,128)(2,1)S(1)}, u32[]{:S(2)}, u32[]{:S(2)}) collective-permute-start(bf16[256,1280]{1,0:T(8,128)(2,1)} %collective-permute-done.3), channel_id=1, source_target_pairs={{8,0},{16,24},{9,1},{17,25},{10,2},{18,26},{11,3},{19,27},{12,4},{... | collective-permute-start | bytes 1966088 | tf_op jit(solution)/shard_map/ppermute | solution.py:520
  47.8 1.1 %collective-permute-start.11 = (bf16[256,1280]{1,0:T(8,128)(2,1)S(1)}, bf16[256,1280]{1,0:T(8,128)(2,1)S(1)}, u32[]{:S(2)}, u32[]{:S(2)}) collective-permute-start(bf16[256,1280]{1,0:T(8,128)(2,1)S(1)} %get-tuple-element.59), channel_id=1, source_target_pairs={{0,4},{4,0},{1,5},{5,1},{2,6},{6,2},{3,7},{7,3},{8,12},{12,8},{9,1... | collective-permute-start | bytes 1966088 | tf_op jit(solution)/shard_map/ppermute | solution.py:522
  48.9 4.8 %early_slots.2.refs_9_ = f32[512,1280]{1,0:T(8,128)S(1)} custom-call(bf16[256,8192]{1,0:T(8,128)(2,1)S(1)} %bitcast.12, bf16[256,1280]{1,0:T(8,128)(2,1)} %collective-permute-done.2.refs_0_, bf16[256,1536]{1,0:T(8,128)(2,1)S(1)} %collective-permute-done.7.refs_1_.refs_0_, f32[256,128]{1,0:T(8,128)S(1)} %get-tuple-element.62.refs_2_, ...), custom_call_target="tpu_custom_call" | custom-call | flops 2684354560 | bytes 9961472 | tf_op jit(solution)/shard_map/early_slots/pallas_call | solution.py:332
  53.7 8.1 %collective-permute-done.9 = bf16[256,1280]{1,0:T(8,128)(2,1)S(1)} collective-permute-done((bf16[256,1280]{1,0:T(8,128)(2,1)}, bf16[256,1280]{1,0:T(8,128)(2,1)S(1)}, u32[]{:S(2)}, u32[]{:S(2)}) %collective-permute-start.9) | collective-permute-done | bytes 655392 | tf_op jit(solution)/shard_map/ppermute | solution.py:520
  61.8 1.2 %broadcast_select_fusion.refs_0_ = bf16[256,1280]{1,0:T(8,128)(2,1)S(1)} fusion(bf16[256,1280]{1,0:T(8,128)(2,1)} %collective-permute-done.3, bf16[256,1280]{1,0:T(8,128)(2,1)S(1)} %collective-permute-done.9, pred[]{:T(512)S(6)} %or.3), kind=kLoop, calls=%fused_computation | loop fusion | flops 327680 | bytes 1966081 | tf_op jit(solution)/shard_map/jit(_where)/select_n | solution.py:537
  63.0 0.6 collective-permute-done.10.refs_6_
  63.6 0.3 collective-permute-done.11.refs_1_
  63.9 1.0 collective-permute-start.15
  65.0 1.3 %collective-permute-start.14 = (bf16[256,768]{1,0:T(8,128)(2,1)S(1)}, bf16[256,768]{1,0:T(8,128)(2,1)S(1)}, u32[]{:S(2)}, u32[]{:S(2)}) collective-permute-start(bf16[256,768]{1,0:T(8,128)(2,1)S(1)} %slice.6), channel_id=1, source_target_pairs={{0,2},{1,3},{2,0},{3,1},{4,6},{5,7},{6,4},{7,5},{8,10},{9,11},{10,... | collective-permute-start | bytes 1179656 | tf_op jit(solution)/shard_map/ppermute | solution.py:541
  66.3 0.4 collective-permute-done.15.refs_8_
  66.7 3.1 %early_slots.3 = (f32[512,1280]{1,0:T(8,128)S(1)}, bf16[512,1024]{1,0:T(8,128)(2,1)S(1)}) custom-call(bf16[256,8192]{1,0:T(8,128)(2,1)S(1)} %bitcast.13, bf16[256,1536]{1,0:T(8,128)(2,1)S(1)} %collective-permute-done.7.refs_1_.refs_0_, bf16[256,1280]{1,0:T(8,128)(2,1)S(1)} %collective-permute-done.11.refs_1_, f32[256,128]{1,0:T(8,128)S(1)} %get-tuple-element.62.refs_2_, ...), custom_call_target="tpu_custom_call" | custom-call | flops 1342177280 | bytes 7340032 | tf_op jit(solution)/shard_map/early_slots/pallas_call | solution.py:332
  69.8 5.4 %collective-permute-done.14.refs_1_ = bf16[256,768]{1,0:T(8,128)(2,1)S(1)} collective-permute-done((bf16[256,768]{1,0:T(8,128)(2,1)S(1)}, bf16[256,768]{1,0:T(8,128)(2,1)S(1)}, u32[]{:S(2)}, u32[]{:S(2)}) %collective-permute-start.14) | collective-permute-done | bytes 393248 | tf_op jit(solution)/shard_map/ppermute | solution.py:541
  75.2 1.4 %collective-permute-start.17 = (bf16[256,768]{1,0:T(8,128)(2,1)S(1)}, bf16[256,768]{1,0:T(8,128)(2,1)S(1)}, u32[]{:S(2)}, u32[]{:S(2)}) collective-permute-start(bf16[256,768]{1,0:T(8,128)(2,1)S(1)} %collective-permute-done.14.refs_1_), channel_id=1, source_target_pairs={{0,1},{1,0},{2,3},{3,2},{4,5},{5,4},{6,7},{7,6},{8,9},{9,8},{10,11... | collective-permute-start | bytes 1179656 | tf_op jit(solution)/shard_map/ppermute | solution.py:561
  76.6 1.3 %collective-permute-start.19 = (bf16[256,512]{1,0:T(8,128)(2,1)S(1)}, bf16[256,512]{1,0:T(8,128)(2,1)S(1)}, u32[]{:S(2)}, u32[]{:S(2)}) collective-permute-start(bf16[256,512]{1,0:T(8,128)(2,1)S(1)} %slice.7), channel_id=1, source_target_pairs={{0,2},{1,3},{2,0},{3,1},{4,6},{5,7},{6,4},{7,5},{8,10},{9,11},{10,... | collective-permute-start | bytes 786440 | tf_op jit(solution)/shard_map/ppermute | solution.py:560
  77.9 1.5 %late_slot.2 = (f32[256,256]{1,0:T(8,128)S(1)}, f32[256,512]{1,0:T(8,128)S(1)}, bf16[256,256]{1,0:T(8,128)(2,1)S(1)}, bf16[256,512]{1,0:T(8,128)(2,1)S(1)}) custom-call(f32[512,1280]{1,0:T(8,128)S(1)} %get-tuple-element.74.before, bf16[512,1024]{1,0:T(8,128)(2,1)S(1)} %get-tuple-element.75.last_rows, bf16[256,1280]{1,0:T(8,128)(2,1)S(1)} %broadcast_select_fusion.refs_0_, ...), custom_call_target="tpu_custom_call" | custom-call | flops 805306368 | bytes 1572864 | tf_op jit(solution)/shard_map/late_slot/pallas_call | solution.py:375
  79.4 1.1 %collective-permute-start.18 = (bf16[256,256]{1,0:T(8,128)(2,1)S(1)}, bf16[256,256]{1,0:T(8,128)(2,1)S(1)}, u32[]{:S(2)}, u32[]{:S(2)}) collective-permute-start(bf16[256,256]{1,0:T(8,128)(2,1)S(1)} %get-tuple-element.79), channel_id=1, source_target_pairs={{0,4},{4,0},{1,5},{5,1},{2,6},{6,2},{3,7},{7,3},{8,12},{12,8},{9,1... | collective-permute-start | bytes 393224 | tf_op jit(solution)/shard_map/ppermute | solution.py:570
  80.6 4.1 %collective-permute-done.19.refs_1_ = bf16[256,512]{1,0:T(8,128)(2,1)S(1)} collective-permute-done((bf16[256,512]{1,0:T(8,128)(2,1)S(1)}, bf16[256,512]{1,0:T(8,128)(2,1)S(1)}, u32[]{:S(2)}, u32[]{:S(2)}) %collective-permute-start.19) | collective-permute-done | bytes 262176 | tf_op jit(solution)/shard_map/ppermute | solution.py:560
  84.6 0.8 collective-permute-start.20
  85.4 1.1 %collective-permute-start.25 = (bf16[256,512]{1,0:T(8,128)(2,1)S(1)}, bf16[256,512]{1,0:T(8,128)(2,1)S(1)}, u32[]{:S(2)}, u32[]{:S(2)}) collective-permute-start(bf16[256,512]{1,0:T(8,128)(2,1)S(1)} %get-tuple-element.90), channel_id=1, source_target_pairs={{0,4},{4,0},{1,5},{5,1},{2,6},{6,2},{3,7},{7,3},{8,12},{12,8},{9,1... | collective-permute-start | bytes 786440 | tf_op jit(solution)/shard_map/ppermute | solution.py:571
  86.6 1.3 %collective-permute-start.23 = (bf16[256,256]{1,0:T(8,128)(2,1)S(1)}, bf16[256,256]{1,0:T(8,128)(2,1)S(1)}, u32[]{:S(2)}, u32[]{:S(2)}) collective-permute-start(bf16[256,256]{1,0:T(8,128)(2,1)S(1)} %key_value.1.refs_7_.refs_5_), channel_id=1, source_target_pairs={{0,2},{1,3},{4,6},{5,7},{8,10},{9,11},{12,14},{13,15},{16,18},{17,... | collective-permute-start | bytes 393224 | tf_op jit(solution)/shard_map/ppermute | solution.py:592
  87.9 0.8 late_slot.3
  88.8 0.5 collective-permute-start.21
  89.2 0.6 collective-permute-start.22
  89.8 3.5 %collective-permute-done.23.refs_9_.refs_7_ = bf16[256,256]{1,0:T(8,128)(2,1)S(1)} collective-permute-done((bf16[256,256]{1,0:T(8,128)(2,1)S(1)}, bf16[256,256]{1,0:T(8,128)(2,1)S(1)}, u32[]{:S(2)}, u32[]{:S(2)}) %collective-permute-start.23) | collective-permute-done | bytes 131104 | tf_op jit(solution)/shard_map/ppermute | solution.py:592
  93.3 3.2 %collective-permute-start.24 = (bf16[256,256]{1,0:T(8,128)(2,1)S(1)}, bf16[256,256]{1,0:T(8,128)(2,1)S(1)}, u32[]{:S(2)}, u32[]{:S(2)}) collective-permute-start(bf16[256,256]{1,0:T(8,128)(2,1)S(1)} %collective-permute-done.23.refs_9_.refs_7_), channel_id=1, source_target_pairs={{2,3},{3,2},{6,7},{7,6},{10,11},{11,10},{14,15},{15,14},{18,19},{1... | collective-permute-start | bytes 393224 | tf_op jit(solution)/shard_map/ppermute | solution.py:594
  96.5 0.8 collective-permute-done.24.refs_10_.refs_8_
  97.3 2.4 %attention.2.refs_9_ = bf16[256,512]{1,0:T(8,128)(2,1)S(1)} custom-call(f32[256,256]{1,0:T(8,128)S(1)} %get-tuple-element.86.sums.refs_0_, f32[256,512]{1,0:T(8,128)S(1)} %get-tuple-element.89.refs_1_, bf16[256,256]{1,0:T(8,128)(2,1)S(1)} %collective-permute-done.18.back.refs_2_, bf16[256,512]{1,0:T(8,128)(2,1)S(1)} %collective-permute-done.25.refs_3_, ...), custom_call_target="tpu_custom_call" | custom-call | flops 536870912 | bytes 1048576 | tf_op jit(solution)/shard_map/attention/pallas_call | solution.py:454
  99.6 3.2 %attention.3 = bf16[256,1024]{1,0:T(8,128)(2,1)} custom-call(f32[256,512]{1,0:T(8,128)S(1)} %get-tuple-element.81.refs_0_, bf16[256,512]{1,0:T(8,128)(2,1)S(1)} %collective-permute-done.21.refs_1_, f32[1,1024]{1,0:T(1,128)S(1)} %bitcast.15, f32[256,128]{1,0:T(8,128)S(1)} %get-tuple-element.84.cosine.refs_5_.refs_3_, ...), custom_call_target="tpu_custom_call" | custom-call | flops 536870912 | bytes 1048576 | tf_op jit(solution)/shard_map/attention/pallas_call | solution.py:454
  (47 shorter events, 1.6 us)
Async XLA Ops:
  2.4 8.1 %copy-start.7 = (bf16[8192]{0:T(1024)(128)(2,1)S(1)}, bf16[8192]{0:T(1024)(128)(2,1)}, u32[]{:S(2)}) copy-start(bf16[8192]{0:T(1024)(128)(2,1)} %param.9) | copy-start | bytes 49156
  2.4 8.1 %copy-start.8 = (bf16[1024]{0:T(1024)(128)(2,1)S(1)}, bf16[1024]{0:T(1024)(128)(2,1)}, u32[]{:S(2)}) copy-start(bf16[1024]{0:T(1024)(128)(2,1)} %param.13) | copy-start | bytes 6148
  2.4 8.2 %copy-start.9 = (bf16[128]{0:T(256)(128)(2,1)S(1)}, bf16[128]{0:T(256)(128)(2,1)}, u32[]{:S(2)}) copy-start(bf16[128]{0:T(256)(128)(2,1)} %param.15) | copy-start | bytes 772
  2.5 8.2 %copy-start.10 = (bf16[128]{0:T(256)(128)(2,1)S(1)}, bf16[128]{0:T(256)(128)(2,1)}, u32[]{:S(2)}) copy-start(bf16[128]{0:T(256)(128)(2,1)} %param.14) | copy-start | bytes 772
  2.5 16.0 %collective-permute-start = (bf16[256,1280]{1,0:T(8,128)(2,1)}, bf16[256,1280]{1,0:T(8,128)(2,1)S(1)}, u32[]{:S(2)}, u32[]{:S(2)}) collective-permute-start(bf16[256,1280]{1,0:T(8,128)(2,1)} %get-tuple-element.48), channel_id=1, source_target_pairs={{0,8},{8,0},{16,24},{24,16},{1,9},{9,1},{17,25},{25,17},{2,10},{10... | collective-permute-start | bytes 1966088 | tf_op jit(solution)/shard_map/ppermute | solution.py:493
  2.7 18.8 %collective-permute-start.1 = (bf16[256,1280]{1,0:T(8,128)(2,1)}, bf16[256,1280]{1,0:T(8,128)(2,1)}, u32[]{:S(2)}, u32[]{:S(2)}) collective-permute-start(bf16[256,1280]{1,0:T(8,128)(2,1)} %get-tuple-element.48), channel_id=1, source_target_pairs={{8,16},{16,8},{9,17},{17,9},{10,18},{18,10},{11,19},{19,11},{12,20... | collective-permute-start | bytes 1966088 | tf_op jit(solution)/shard_map/ppermute | solution.py:494
  7.0 15.4 %collective-permute-start.2 = (bf16[256,1280]{1,0:T(8,128)(2,1)}, bf16[256,1280]{1,0:T(8,128)(2,1)}, u32[]{:S(2)}, u32[]{:S(2)}) collective-permute-start(bf16[256,1280]{1,0:T(8,128)(2,1)} %get-tuple-element.49), channel_id=1, source_target_pairs={{0,4},{4,0},{1,5},{5,1},{2,6},{6,2},{3,7},{7,3},{8,12},{12,8},{9,1... | collective-permute-start | bytes 1966088 | tf_op jit(solution)/shard_map/ppermute | solution.py:495
  8.3 40.5 %copy-start.2 = (bf16[1024,1024]{1,0:T(8,128)(2,1)S(1)}, bf16[1024,1024]{1,0:T(8,128)(2,1)}, u32[]{:S(2)}) copy-start(bf16[1024,1024]{1,0:T(8,128)(2,1)} %refs_7_.1) | copy-start | bytes 6291460
  18.4 4.0 %copy-start.5 = (bf16[256,1280]{1,0:T(8,128)(2,1)}, bf16[256,1280]{1,0:T(8,128)(2,1)S(1)}, u32[]{:S(2)}) copy-start(bf16[256,1280]{1,0:T(8,128)(2,1)S(1)} %collective-permute-done.refs_8_) | copy-start | bytes 1966084
  22.4 13.7 %collective-permute-start.5 = (bf16[256,1280]{1,0:T(8,128)(2,1)}, bf16[256,1280]{1,0:T(8,128)(2,1)}, u32[]{:S(2)}, u32[]{:S(2)}) collective-permute-start(bf16[256,1280]{1,0:T(8,128)(2,1)} %collective-permute-done.1), channel_id=1, source_target_pairs={{8,0},{16,24},{9,1},{17,25},{10,2},{18,26},{11,3},{19,27},{12,4},{... | collective-permute-start | bytes 1966088 | tf_op jit(solution)/shard_map/ppermute | solution.py:510
  24.6 17.7 %collective-permute-start.7 = (bf16[256,1536]{1,0:T(8,128)(2,1)}, bf16[256,1536]{1,0:T(8,128)(2,1)S(1)}, u32[]{:S(2)}, u32[]{:S(2)}) collective-permute-start(bf16[256,1536]{1,0:T(8,128)(2,1)} %pack.3), channel_id=1, source_target_pairs={{0,4},{4,0},{1,5},{5,1},{2,6},{6,2},{3,7},{7,3},{8,12},{12,8},{9,1... | collective-permute-start | bytes 2359304 | tf_op jit(solution)/shard_map/ppermute | solution.py:512
  25.8 16.0 %collective-permute-start.3 = (bf16[256,1280]{1,0:T(8,128)(2,1)}, bf16[256,1280]{1,0:T(8,128)(2,1)}, u32[]{:S(2)}, u32[]{:S(2)}) collective-permute-start(bf16[256,1280]{1,0:T(8,128)(2,1)} %copy-done.5), channel_id=1, source_target_pairs={{8,16},{16,8},{9,17},{17,9},{10,18},{18,10},{11,19},{19,11},{12,20... | collective-permute-start | bytes 1966088 | tf_op jit(solution)/shard_map/ppermute | solution.py:509
  28.3 13.9 %collective-permute-start.6 = (bf16[256,1280]{1,0:T(8,128)(2,1)}, bf16[256,1280]{1,0:T(8,128)(2,1)}, u32[]{:S(2)}, u32[]{:S(2)}) collective-permute-start(bf16[256,1280]{1,0:T(8,128)(2,1)} %copy-done.5), channel_id=1, source_target_pairs={{0,2},{1,3},{2,0},{3,1},{4,6},{5,7},{6,4},{7,5},{8,10},{9,11},{10,... | collective-permute-start | bytes 1966088 | tf_op jit(solution)/shard_map/ppermute | solution.py:511
  28.6 13.6 %collective-permute-start.8 = (bf16[256,1280]{1,0:T(8,128)(2,1)}, bf16[256,1280]{1,0:T(8,128)(2,1)}, u32[]{:S(2)}, u32[]{:S(2)}) collective-permute-start(bf16[256,1280]{1,0:T(8,128)(2,1)} %copy-done.5), channel_id=1, source_target_pairs={{0,1},{1,0},{2,3},{3,2},{4,5},{5,4},{6,7},{7,6},{8,9},{9,8},{10,11... | collective-permute-start | bytes 1966088 | tf_op jit(solution)/shard_map/ppermute | solution.py:513
  31.6 2.2 %copy-start = (bf16[1,256,8192]{2,1,0:T(8,128)(2,1)S(1)}, bf16[1,256,8192]{2,1,0:T(8,128)(2,1)}, u32[]{:S(2)}) copy-start(bf16[1,256,8192]{2,1,0:T(8,128)(2,1)} %param.8) | copy-start | bytes 12582916
  33.8 15.1 %copy-start.1 = (bf16[1,256,8192]{2,1,0:T(8,128)(2,1)S(1)}, bf16[1,256,8192]{2,1,0:T(8,128)(2,1)}, u32[]{:S(2)}) copy-start(bf16[1,256,8192]{2,1,0:T(8,128)(2,1)} %param.8) | copy-start | bytes 12582916
  33.8 15.1 %copy-start.3 = (bf16[1024,128]{1,0:T(8,128)(2,1)S(1)}, bf16[1024,128]{1,0:T(8,128)(2,1)}, u32[]{:S(2)}) copy-start(bf16[1024,128]{1,0:T(8,128)(2,1)} %refs_5_.1) | copy-start | bytes 786436
  33.8 15.1 %copy-start.4 = (bf16[1024,128]{1,0:T(8,128)(2,1)S(1)}, bf16[1024,128]{1,0:T(8,128)(2,1)}, u32[]{:S(2)}) copy-start(bf16[1024,128]{1,0:T(8,128)(2,1)} %refs_6_.1) | copy-start | bytes 786436
  33.8 15.1 %copy-start.6 = (bf16[256,1280]{1,0:T(8,128)(2,1)S(1)}, bf16[256,1280]{1,0:T(8,128)(2,1)}, u32[]{:S(2)}) copy-start(bf16[256,1280]{1,0:T(8,128)(2,1)} %copy-done.5) | copy-start | bytes 1966084
  36.1 5.6 %collective-permute-start.4 = (f32[1,256]{1,0:T(1,128)S(1)}, f32[1,256]{1,0:T(1,128)S(1)}, u32[]{:S(2)}, u32[]{:S(2)}) collective-permute-start(f32[1,256]{1,0:T(1,128)S(1)} %get-tuple-element.52), channel_id=1, source_target_pairs={{0,4},{4,0},{1,5},{5,1},{2,6},{6,2},{3,7},{7,3},{8,12},{12,8},{9,1... | collective-permute-start | bytes 3080 | tf_op jit(solution)/shard_map/ppermute | solution.py:515
  42.2 6.6 %collective-permute-start.13 = (bf16[256,1280]{1,0:T(8,128)(2,1)}, bf16[256,1280]{1,0:T(8,128)(2,1)S(1)}, u32[]{:S(2)}, u32[]{:S(2)}) collective-permute-start(bf16[256,1280]{1,0:T(8,128)(2,1)} %collective-permute-done.6.refs_9_), channel_id=1, source_target_pairs={{0,1},{1,0},{2,3},{3,2},{4,5},{5,4},{6,7},{7,6},{8,9},{9,8},{10,11... | collective-permute-start | bytes 1966088 | tf_op jit(solution)/shard_map/ppermute | solution.py:523
  45.9 15.9 %collective-permute-start.9 = (bf16[256,1280]{1,0:T(8,128)(2,1)}, bf16[256,1280]{1,0:T(8,128)(2,1)S(1)}, u32[]{:S(2)}, u32[]{:S(2)}) collective-permute-start(bf16[256,1280]{1,0:T(8,128)(2,1)} %collective-permute-done.3), channel_id=1, source_target_pairs={{8,0},{16,24},{9,1},{17,25},{10,2},{18,26},{11,3},{19,27},{12,4},{... | collective-permute-start | bytes 1966088 | tf_op jit(solution)/shard_map/ppermute | solution.py:520
  47.2 16.4 %collective-permute-start.10 = (bf16[256,1280]{1,0:T(8,128)(2,1)S(1)}, bf16[256,1280]{1,0:T(8,128)(2,1)S(1)}, u32[]{:S(2)}, u32[]{:S(2)}) collective-permute-start(bf16[256,1280]{1,0:T(8,128)(2,1)S(1)} %broadcast_select_fusion.1.refs_5_), channel_id=1, source_target_pairs={{0,2},{1,3},{2,0},{3,1},{4,6},{5,7},{6,4},{7,5},{8,10},{9,11},{10,... | collective-permute-start | bytes 1966088 | tf_op jit(solution)/shard_map/ppermute | solution.py:521
  47.5 16.4 %collective-permute-start.12 = (bf16[256,1280]{1,0:T(8,128)(2,1)S(1)}, bf16[256,1280]{1,0:T(8,128)(2,1)S(1)}, u32[]{:S(2)}, u32[]{:S(2)}) collective-permute-start(bf16[256,1280]{1,0:T(8,128)(2,1)S(1)} %broadcast_select_fusion.1.refs_5_), channel_id=1, source_target_pairs={{0,1},{1,0},{2,3},{3,2},{4,5},{5,4},{6,7},{7,6},{8,9},{9,8},{10,11... | collective-permute-start | bytes 1966088 | tf_op jit(solution)/shard_map/ppermute | solution.py:524
  47.8 16.1 %collective-permute-start.11 = (bf16[256,1280]{1,0:T(8,128)(2,1)S(1)}, bf16[256,1280]{1,0:T(8,128)(2,1)S(1)}, u32[]{:S(2)}, u32[]{:S(2)}) collective-permute-start(bf16[256,1280]{1,0:T(8,128)(2,1)S(1)} %get-tuple-element.59), channel_id=1, source_target_pairs={{0,4},{4,0},{1,5},{5,1},{2,6},{6,2},{3,7},{7,3},{8,12},{12,8},{9,1... | collective-permute-start | bytes 1966088 | tf_op jit(solution)/shard_map/ppermute | solution.py:522
  63.9 2.7 %collective-permute-start.15 = (bf16[256,1280]{1,0:T(8,128)(2,1)S(1)}, bf16[256,1280]{1,0:T(8,128)(2,1)S(1)}, u32[]{:S(2)}, u32[]{:S(2)}) collective-permute-start(bf16[256,1280]{1,0:T(8,128)(2,1)S(1)} %collective-permute-done.10.refs_6_), channel_id=1, source_target_pairs={{0,1},{1,0},{2,3},{3,2},{4,5},{5,4},{6,7},{7,6},{8,9},{9,8},{10,11... | collective-permute-start | bytes 1966088 | tf_op jit(solution)/shard_map/ppermute | solution.py:542
  65.0 10.3 %collective-permute-start.16 = (bf16[256,1280]{1,0:T(8,128)(2,1)S(1)}, bf16[256,1280]{1,0:T(8,128)(2,1)S(1)}, u32[]{:S(2)}, u32[]{:S(2)}) collective-permute-start(bf16[256,1280]{1,0:T(8,128)(2,1)S(1)} %broadcast_select_fusion.refs_0_), channel_id=1, source_target_pairs={{0,1},{1,0},{2,3},{3,2},{4,5},{5,4},{6,7},{7,6},{8,9},{9,8},{10,11... | collective-permute-start | bytes 1966088 | tf_op jit(solution)/shard_map/ppermute | solution.py:543
  65.0 10.2 %collective-permute-start.14 = (bf16[256,768]{1,0:T(8,128)(2,1)S(1)}, bf16[256,768]{1,0:T(8,128)(2,1)S(1)}, u32[]{:S(2)}, u32[]{:S(2)}) collective-permute-start(bf16[256,768]{1,0:T(8,128)(2,1)S(1)} %slice.6), channel_id=1, source_target_pairs={{0,2},{1,3},{2,0},{3,1},{4,6},{5,7},{6,4},{7,5},{8,10},{9,11},{10,... | collective-permute-start | bytes 1179656 | tf_op jit(solution)/shard_map/ppermute | solution.py:541
  75.2 2.7 %collective-permute-start.17 = (bf16[256,768]{1,0:T(8,128)(2,1)S(1)}, bf16[256,768]{1,0:T(8,128)(2,1)S(1)}, u32[]{:S(2)}, u32[]{:S(2)}) collective-permute-start(bf16[256,768]{1,0:T(8,128)(2,1)S(1)} %collective-permute-done.14.refs_1_), channel_id=1, source_target_pairs={{0,1},{1,0},{2,3},{3,2},{4,5},{5,4},{6,7},{7,6},{8,9},{9,8},{10,11... | collective-permute-start | bytes 1179656 | tf_op jit(solution)/shard_map/ppermute | solution.py:561
  76.6 8.0 %collective-permute-start.19 = (bf16[256,512]{1,0:T(8,128)(2,1)S(1)}, bf16[256,512]{1,0:T(8,128)(2,1)S(1)}, u32[]{:S(2)}, u32[]{:S(2)}) collective-permute-start(bf16[256,512]{1,0:T(8,128)(2,1)S(1)} %slice.7), channel_id=1, source_target_pairs={{0,2},{1,3},{2,0},{3,1},{4,6},{5,7},{6,4},{7,5},{8,10},{9,11},{10,... | collective-permute-start | bytes 786440 | tf_op jit(solution)/shard_map/ppermute | solution.py:560
  79.4 5.2 %collective-permute-start.18 = (bf16[256,256]{1,0:T(8,128)(2,1)S(1)}, bf16[256,256]{1,0:T(8,128)(2,1)S(1)}, u32[]{:S(2)}, u32[]{:S(2)}) collective-permute-start(bf16[256,256]{1,0:T(8,128)(2,1)S(1)} %get-tuple-element.79), channel_id=1, source_target_pairs={{0,4},{4,0},{1,5},{5,1},{2,6},{6,2},{3,7},{7,3},{8,12},{12,8},{9,1... | collective-permute-start | bytes 393224 | tf_op jit(solution)/shard_map/ppermute | solution.py:570
  84.6 3.3 %collective-permute-start.20 = (bf16[256,512]{1,0:T(8,128)(2,1)S(1)}, bf16[256,512]{1,0:T(8,128)(2,1)S(1)}, u32[]{:S(2)}, u32[]{:S(2)}) collective-permute-start(bf16[256,512]{1,0:T(8,128)(2,1)S(1)} %collective-permute-done.19.refs_1_), channel_id=1, source_target_pairs={{0,1},{1,0},{2,3},{3,2},{4,5},{5,4},{6,7},{7,6},{8,9},{9,8},{10,11... | collective-permute-start | bytes 786440 | tf_op jit(solution)/shard_map/ppermute | solution.py:573
  85.4 11.1 %collective-permute-start.25 = (bf16[256,512]{1,0:T(8,128)(2,1)S(1)}, bf16[256,512]{1,0:T(8,128)(2,1)S(1)}, u32[]{:S(2)}, u32[]{:S(2)}) collective-permute-start(bf16[256,512]{1,0:T(8,128)(2,1)S(1)} %get-tuple-element.90), channel_id=1, source_target_pairs={{0,4},{4,0},{1,5},{5,1},{2,6},{6,2},{3,7},{7,3},{8,12},{12,8},{9,1... | collective-permute-start | bytes 786440 | tf_op jit(solution)/shard_map/ppermute | solution.py:571
  86.6 6.7 %collective-permute-start.23 = (bf16[256,256]{1,0:T(8,128)(2,1)S(1)}, bf16[256,256]{1,0:T(8,128)(2,1)S(1)}, u32[]{:S(2)}, u32[]{:S(2)}) collective-permute-start(bf16[256,256]{1,0:T(8,128)(2,1)S(1)} %key_value.1.refs_7_.refs_5_), channel_id=1, source_target_pairs={{0,2},{1,3},{4,6},{5,7},{8,10},{9,11},{12,14},{13,15},{16,18},{17,... | collective-permute-start | bytes 393224 | tf_op jit(solution)/shard_map/ppermute | solution.py:592
  88.8 10.9 %collective-permute-start.21 = (bf16[256,512]{1,0:T(8,128)(2,1)S(1)}, bf16[256,512]{1,0:T(8,128)(2,1)S(1)}, u32[]{:S(2)}, u32[]{:S(2)}) collective-permute-start(bf16[256,512]{1,0:T(8,128)(2,1)S(1)} %get-tuple-element.82), channel_id=1, source_target_pairs={{0,4},{4,0},{1,5},{5,1},{2,6},{6,2},{3,7},{7,3},{8,12},{12,8},{9,1... | collective-permute-start | bytes 786440 | tf_op jit(solution)/shard_map/ppermute | solution.py:581
  89.2 7.3 %collective-permute-start.22 = (bf16[256,256]{1,0:T(8,128)(2,1)S(1)}, bf16[256,256]{1,0:T(8,128)(2,1)S(1)}, u32[]{:S(2)}, u32[]{:S(2)}) collective-permute-start(bf16[256,256]{1,0:T(8,128)(2,1)S(1)} %key_value.1.refs_7_.refs_5_), channel_id=1, source_target_pairs={{0,1},{1,0},{2,3},{3,2},{4,5},{5,4},{6,7},{7,6},{8,9},{9,8},{10,11... | collective-permute-start | bytes 393224 | tf_op jit(solution)/shard_map/ppermute | solution.py:593
  93.3 4.0 %collective-permute-start.24 = (bf16[256,256]{1,0:T(8,128)(2,1)S(1)}, bf16[256,256]{1,0:T(8,128)(2,1)S(1)}, u32[]{:S(2)}, u32[]{:S(2)}) collective-permute-start(bf16[256,256]{1,0:T(8,128)(2,1)S(1)} %collective-permute-done.23.refs_9_.refs_7_), channel_id=1, source_target_pairs={{2,3},{3,2},{6,7},{7,6},{10,11},{11,10},{14,15},{15,14},{18,19},{1... | collective-permute-start | bytes 393224 | tf_op jit(solution)/shard_map/ppermute | solution.py:594

commit v7 on v6

--- a/solution.py
+++ b/solution.py
@@ -413,32 +413,56 @@
     rows = out.shape[0]
     head = cosine.shape[1]
     slab = lax.axis_index("ctx")
-    for block, flip in zip(blocks, (0, 1, 2, 3)):
-        row = pl.multiple_of(jnp.bitwise_xor(slab, flip) * rows, rows)
+    odd = lax.rem(slab, 2)
+    own_block, beside, across, corner = blocks
+    for block, place in ((own_block, odd), (beside, 1 - odd)):
+        row = pl.multiple_of(place * rows, rows)
         keys[pl.ds(row, rows), :] = block[:, :head]
         values[pl.ds(row, rows), :] = block[:, head:]
-    total_keys = keys.shape[0]
-    row_ids = slab * rows + lax.broadcasted_iota(jnp.int32, (rows, total_keys), 0)
-    visible = lax.broadcasted_iota(jnp.int32, (rows, total_keys), 1) <= row_ids
+    near = (rows, keys.shape[0])
+    row_ids = odd * rows + lax.broadcasted_iota(jnp.int32, near, 0)
+    visible = lax.broadcasted_iota(jnp.int32, near, 1) <= row_ids
+    power = scale * math.log2(math.e)
     if first:
         out[:, :first] = done[...]
-    at = first
-    for own, other, skip in zip(sums, backs, skips):
-        for column in range(skip, own.shape[1], head):
-            cols = slice(column, column + head)
-            query = own[:, cols] + other[:, cols].astype(jnp.float32) + bias[:, at : at + head]
-            query = turned(query, cosine[...], sine_table[...]).astype(jnp.bfloat16)
-            scores = lax.dot_general(
-                query, keys[...], (((1,), (1,)), ((), ())), preferred_element_type=jnp.float32
-            )
-            scores = jnp.where(visible, scores * scale, masked_score)
-            exps = jnp.exp(scores - jnp.max(scores, axis=1, keepdims=True))
-            length = jnp.sum(exps, axis=1, keepdims=True)
-            mixed = jnp.dot(
-                exps.astype(jnp.bfloat16), values[...], preferred_element_type=jnp.float32
-            )
-            out[:, at : at + head] = (mixed / length).astype(jnp.bfloat16)
-            at += head
+
+    def all_heads(far):
+        at = first
+        for own, other, skip in zip(sums, backs, skips):
+            for column in range(skip, own.shape[1], head):
+                cols = slice(column, column + head)
+                query = own[:, cols] + other[:, cols].astype(jnp.float32) + bias[:, at : at + head]
+                query = turned(query, cosine[...], sine_table[...]).astype(jnp.bfloat16)
+                pairs = [(keys[...], values[...])]
+                pairs += [(block[:, :head], block[:, head:]) for block in far]
+                scores = [
+                    lax.dot_general(
+                        query, key, (((1,), (1,)), ((), ())), preferred_element_type=jnp.float32
+                    )
+                    for key, _ in pairs
+                ]
+                scores[0] = jnp.where(visible, scores[0], masked_score)
+                peak = jnp.max(scores[0], axis=1, keepdims=True)
+                for block in scores[1:]:
+                    peak = jnp.maximum(peak, jnp.max(block, axis=1, keepdims=True))
+                length = jnp.zeros((rows, 1), jnp.float32)
+                mixed = jnp.zeros((rows, head), jnp.float32)
+                for block, (_, value) in zip(scores, pairs):
+                    exps = jnp.exp2((block - peak) * power)
+                    length = length + jnp.sum(exps, axis=1, keepdims=True)
+                    mixed = mixed + jnp.dot(
+                        exps.astype(jnp.bfloat16), value, preferred_element_type=jnp.float32
+                    )
+                out[:, at : at + head] = (mixed / length).astype(jnp.bfloat16)
+                at += head
+
+    @pl.when(slab < 2)
+    def _():
+        all_heads(())
+
+    @pl.when(slab >= 2)
+    def _():
+        all_heads((across, corner))
 
 
 def attention(sums, backs, skips, bias, cosine, sine_table, blocks, done=None):
@@ -457,8 +481,8 @@
         in_specs=[inside] * len(args),
         out_specs=inside,
         scratch_shapes=[
-            pltpu.VMEM((4 * rows, head), jnp.bfloat16),
-            pltpu.VMEM((4 * rows, head), jnp.bfloat16),
+            pltpu.VMEM((2 * rows, head), jnp.bfloat16),
+            pltpu.VMEM((2 * rows, head), jnp.bfloat16),
         ],
         cost_estimate=pl.CostEstimate(
             flops=4 * total * head, bytes_accessed=8 * rows * width, transcendentals=total

time: 104 us -> 103 us (level)
  no operation moved by 1% of the time
where the time goes in v7:
time: 103 us
  waiting for transfers between devices  38.5 us (37%)
  starting transfers between devices  36.2 us (35%)
  Pallas kernels  22.4 us (22%)
  other arithmetic  3.07 us (3%)
  local copies, waits for them, and re-layouts  2.3 us (2%)
    ppermute x1, waiting for transfers between devices, planned(): fourth_out = lax.ppermute(fourth_in, 'line', outward)  8.08 us
    pallas_call x2, Pallas kernels, early_slots(): pl.pallas_call(functools.partial(early_body, slots, guests, local, final)...  7.93 us
    ppermute x1, waiting for transfers between devices, planned(): second = lax.ppermute(mine, 'line', ends)  7.11 us
    pallas_call x2, Pallas kernels, attention(): pl.pallas_call(functools.partial(attention_body, head ** (-0.5), first, s...  5.49 us
    ppermute x1, waiting for transfers between devices, planned(): fourth_far_1 = lax.ppermute(fourth[:, :half], 'ctx', across)  5.39 us
    pallas_call x2, Pallas kernels, pack(): pl.pallas_call(functools.partial(pack_body, sent_parts, len(weights), dep...  4.59 us
    ppermute x1, starting transfers between devices, planned(): third_in = lax.ppermute(mine, 'line', middle)  4.32 us
    ppermute x1, waiting for transfers between devices, planned(): fourth_far_2 = lax.ppermute(fourth[:, half:], 'ctx', across)  4.07 us
  transfers between devices with their start and end apart: 26, of which 15 were waited for; matrix products, arithmetic and copies ran while one was open for 3% of the time, Pallas kernels for 16%

profile of v7, /device:TPU:11, one launch (start us, length us, event | category | flops | bytes accessed | tf_op | source)
XLA Modules:
  0.0 102.8 jit_solution(11760163226047337056)
XLA Ops:
  0.0 2.4 %pack.2 = (bf16[256,1280]{1,0:T(8,128)(2,1)}, bf16[256,1280]{1,0:T(8,128)(2,1)}) custom-call(bf16[256,8192]{1,0:T(8,128)(2,1)} %bitcast.9, bf16[1024,128]{1,0:T(8,128)(2,1)} %refs_5_.1, bf16[1024,128]{1,0:T(8,128)(2,1)} %refs_6_.1, bf16[1024,1024]{1,0:T(8,128)(2,1)} %refs_7_.1), custom_call_target="tpu_custom_call" | custom-call | tf_op jit(solution)/shard_map/pack/pallas_call | solution.py:171
  2.7 4.3 %collective-permute-start.1 = (bf16[256,1280]{1,0:T(8,128)(2,1)}, bf16[256,1280]{1,0:T(8,128)(2,1)}, u32[]{:S(2)}, u32[]{:S(2)}) collective-permute-start(bf16[256,1280]{1,0:T(8,128)(2,1)} %get-tuple-element.48), channel_id=1, source_target_pairs={{8,16},{16,8},{9,17},{17,9},{10,18},{18,10},{11,19},{19,11},{12,20... | collective-permute-start | bytes 1966088 | tf_op jit(solution)/shard_map/ppermute | solution.py:518
  7.0 1.3 %collective-permute-start.2 = (bf16[256,1280]{1,0:T(8,128)(2,1)}, bf16[256,1280]{1,0:T(8,128)(2,1)}, u32[]{:S(2)}, u32[]{:S(2)}) collective-permute-start(bf16[256,1280]{1,0:T(8,128)(2,1)} %get-tuple-element.49), channel_id=1, source_target_pairs={{0,4},{4,0},{1,5},{5,1},{2,6},{6,2},{3,7},{7,3},{8,12},{12,8},{9,1... | collective-permute-start | bytes 1966088 | tf_op jit(solution)/shard_map/ppermute | solution.py:519
  8.3 2.2 %pack.3 = bf16[256,1536]{1,0:T(8,128)(2,1)} custom-call(bf16[256,8192]{1,0:T(8,128)(2,1)} %bitcast.10), custom_call_target="tpu_custom_call" | custom-call | tf_op jit(solution)/shard_map/pack/pallas_call | solution.py:171
  10.6 0.5 fusion
  11.3 7.1 %collective-permute-done.refs_8_ = bf16[256,1280]{1,0:T(8,128)(2,1)S(1)} collective-permute-done((bf16[256,1280]{1,0:T(8,128)(2,1)}, bf16[256,1280]{1,0:T(8,128)(2,1)S(1)}, u32[]{:S(2)}, u32[]{:S(2)}) %collective-permute-start) | collective-permute-done | bytes 655392 | tf_op jit(solution)/shard_map/ppermute | solution.py:517
  18.4 3.0 %collective-permute-done.1 = bf16[256,1280]{1,0:T(8,128)(2,1)} collective-permute-done((bf16[256,1280]{1,0:T(8,128)(2,1)}, bf16[256,1280]{1,0:T(8,128)(2,1)}, u32[]{:S(2)}, u32[]{:S(2)}) %collective-permute-start.1) | collective-permute-done | bytes 655392 | tf_op jit(solution)/shard_map/ppermute | solution.py:518
  21.5 0.9 collective-permute-done.2.refs_0_
  22.4 2.2 %collective-permute-start.5 = (bf16[256,1280]{1,0:T(8,128)(2,1)}, bf16[256,1280]{1,0:T(8,128)(2,1)}, u32[]{:S(2)}, u32[]{:S(2)}) collective-permute-start(bf16[256,1280]{1,0:T(8,128)(2,1)} %collective-permute-done.1), channel_id=1, source_target_pairs={{8,0},{16,24},{9,1},{17,25},{10,2},{18,26},{11,3},{19,27},{12,4},{... | collective-permute-start | bytes 1966088 | tf_op jit(solution)/shard_map/ppermute | solution.py:534
  24.6 1.2 %collective-permute-start.7 = (bf16[256,1536]{1,0:T(8,128)(2,1)}, bf16[256,1536]{1,0:T(8,128)(2,1)S(1)}, u32[]{:S(2)}, u32[]{:S(2)}) collective-permute-start(bf16[256,1536]{1,0:T(8,128)(2,1)} %pack.3), channel_id=1, source_target_pairs={{0,4},{4,0},{1,5},{5,1},{2,6},{6,2},{3,7},{7,3},{8,12},{12,8},{9,1... | collective-permute-start | bytes 2359304 | tf_op jit(solution)/shard_map/ppermute | solution.py:536
  25.8 2.5 %collective-permute-start.3 = (bf16[256,1280]{1,0:T(8,128)(2,1)}, bf16[256,1280]{1,0:T(8,128)(2,1)}, u32[]{:S(2)}, u32[]{:S(2)}) collective-permute-start(bf16[256,1280]{1,0:T(8,128)(2,1)} %copy-done.5), channel_id=1, source_target_pairs={{8,16},{16,8},{9,17},{17,9},{10,18},{18,10},{11,19},{19,11},{12,20... | collective-permute-start | bytes 1966088 | tf_op jit(solution)/shard_map/ppermute | solution.py:533
  28.3 0.3 collective-permute-start.6
  28.6 3.0 %collective-permute-start.8 = (bf16[256,1280]{1,0:T(8,128)(2,1)}, bf16[256,1280]{1,0:T(8,128)(2,1)}, u32[]{:S(2)}, u32[]{:S(2)}) collective-permute-start(bf16[256,1280]{1,0:T(8,128)(2,1)} %copy-done.5), channel_id=1, source_target_pairs={{0,1},{1,0},{2,3},{3,2},{4,5},{5,4},{6,7},{7,6},{8,9},{9,8},{10,11... | collective-permute-start | bytes 1966088 | tf_op jit(solution)/shard_map/ppermute | solution.py:537
  31.6 2.2 %copy-done = bf16[1,256,8192]{2,1,0:T(8,128)(2,1)S(1)} copy-done((bf16[1,256,8192]{2,1,0:T(8,128)(2,1)S(1)}, bf16[1,256,8192]{2,1,0:T(8,128)(2,1)}, u32[]{:S(2)}) %copy-start) | copy-done | bytes 4194328
  33.8 2.0 %prepare.1 = (bf16[256,1280]{1,0:T(8,128)(2,1)S(1)}, f32[256,128]{1,0:T(8,128)S(1)}, f32[1,256]{1,0:T(1,128)S(1)}) custom-call(bf16[256,8192]{1,0:T(8,128)(2,1)S(1)} %bitcast.11), custom_call_target="tpu_custom_call" | custom-call | tf_op jit(solution)/shard_map/prepare/pallas_call | solution.py:224
  36.1 1.2 %collective-permute-start.4 = (f32[1,256]{1,0:T(1,128)S(1)}, f32[1,256]{1,0:T(1,128)S(1)}, u32[]{:S(2)}, u32[]{:S(2)}) collective-permute-start(f32[1,256]{1,0:T(1,128)S(1)} %get-tuple-element.52), channel_id=1, source_target_pairs={{0,4},{4,0},{1,5},{5,1},{2,6},{6,2},{3,7},{7,3},{8,12},{12,8},{9,1... | collective-permute-start | bytes 3080 | tf_op jit(solution)/shard_map/ppermute | solution.py:539
  37.4 1.2 %broadcast_select_fusion.1.refs_5_ = bf16[256,1280]{1,0:T(8,128)(2,1)S(1)} fusion(bf16[256,1280]{1,0:T(8,128)(2,1)} %collective-permute-done.1, bf16[256,1280]{1,0:T(8,128)(2,1)} %collective-permute-done.5, pred[]{:T(512)S(6)} %or.3), kind=kLoop, calls=%fused_computation.1 | loop fusion | flops 327680 | bytes 1966081 | tf_op jit(solution)/shard_map/jit(_where)/select_n | solution.py:540
  38.5 3.2 %collective-permute-done.4.refs_3_ = f32[1,256]{1,0:T(1,128)S(1)} collective-permute-done((f32[1,256]{1,0:T(1,128)S(1)}, f32[1,256]{1,0:T(1,128)S(1)}, u32[]{:S(2)}, u32[]{:S(2)}) %collective-permute-start.4) | collective-permute-done | bytes 1056 | tf_op jit(solution)/shard_map/ppermute | solution.py:539
  41.8 0.4 collective-permute-done.6.refs_9_
  42.2 3.6 %collective-permute-start.13 = (bf16[256,1280]{1,0:T(8,128)(2,1)}, bf16[256,1280]{1,0:T(8,128)(2,1)S(1)}, u32[]{:S(2)}, u32[]{:S(2)}) collective-permute-start(bf16[256,1280]{1,0:T(8,128)(2,1)} %collective-permute-done.6.refs_9_), channel_id=1, source_target_pairs={{0,1},{1,0},{2,3},{3,2},{4,5},{5,4},{6,7},{7,6},{8,9},{9,8},{10,11... | collective-permute-start | bytes 1966088 | tf_op jit(solution)/shard_map/ppermute | solution.py:547
  45.9 1.3 %collective-permute-start.9 = (bf16[256,1280]{1,0:T(8,128)(2,1)}, bf16[256,1280]{1,0:T(8,128)(2,1)S(1)}, u32[]{:S(2)}, u32[]{:S(2)}) collective-permute-start(bf16[256,1280]{1,0:T(8,128)(2,1)} %collective-permute-done.3), channel_id=1, source_target_pairs={{8,0},{16,24},{9,1},{17,25},{10,2},{18,26},{11,3},{19,27},{12,4},{... | collective-permute-start | bytes 1966088 | tf_op jit(solution)/shard_map/ppermute | solution.py:544
  47.8 1.1 %collective-permute-start.11 = (bf16[256,1280]{1,0:T(8,128)(2,1)S(1)}, bf16[256,1280]{1,0:T(8,128)(2,1)S(1)}, u32[]{:S(2)}, u32[]{:S(2)}) collective-permute-start(bf16[256,1280]{1,0:T(8,128)(2,1)S(1)} %get-tuple-element.59), channel_id=1, source_target_pairs={{0,4},{4,0},{1,5},{5,1},{2,6},{6,2},{3,7},{7,3},{8,12},{12,8},{9,1... | collective-permute-start | bytes 1966088 | tf_op jit(solution)/shard_map/ppermute | solution.py:546
  48.9 4.8 %early_slots.2.refs_9_ = f32[512,1280]{1,0:T(8,128)S(1)} custom-call(bf16[256,8192]{1,0:T(8,128)(2,1)S(1)} %bitcast.12, bf16[256,1280]{1,0:T(8,128)(2,1)} %collective-permute-done.2.refs_0_, bf16[256,1536]{1,0:T(8,128)(2,1)S(1)} %collective-permute-done.7.refs_1_.refs_0_, f32[256,128]{1,0:T(8,128)S(1)} %get-tuple-element.62.refs_2_, ...), custom_call_target="tpu_custom_call" | custom-call | flops 2684354560 | bytes 9961472 | tf_op jit(solution)/shard_map/early_slots/pallas_call | solution.py:332
  53.7 8.1 %collective-permute-done.9 = bf16[256,1280]{1,0:T(8,128)(2,1)S(1)} collective-permute-done((bf16[256,1280]{1,0:T(8,128)(2,1)}, bf16[256,1280]{1,0:T(8,128)(2,1)S(1)}, u32[]{:S(2)}, u32[]{:S(2)}) %collective-permute-start.9) | collective-permute-done | bytes 655392 | tf_op jit(solution)/shard_map/ppermute | solution.py:544
  61.8 1.2 %broadcast_select_fusion.refs_0_ = bf16[256,1280]{1,0:T(8,128)(2,1)S(1)} fusion(bf16[256,1280]{1,0:T(8,128)(2,1)} %collective-permute-done.3, bf16[256,1280]{1,0:T(8,128)(2,1)S(1)} %collective-permute-done.9, pred[]{:T(512)S(6)} %or.3), kind=kLoop, calls=%fused_computation | loop fusion | flops 327680 | bytes 1966081 | tf_op jit(solution)/shard_map/jit(_where)/select_n | solution.py:561
  63.0 0.6 collective-permute-done.10.refs_6_
  63.6 0.3 collective-permute-done.11.refs_1_
  63.9 1.0 collective-permute-start.15
  65.0 1.3 %collective-permute-start.14 = (bf16[256,768]{1,0:T(8,128)(2,1)S(1)}, bf16[256,768]{1,0:T(8,128)(2,1)S(1)}, u32[]{:S(2)}, u32[]{:S(2)}) collective-permute-start(bf16[256,768]{1,0:T(8,128)(2,1)S(1)} %slice.6), channel_id=1, source_target_pairs={{0,2},{1,3},{2,0},{3,1},{4,6},{5,7},{6,4},{7,5},{8,10},{9,11},{10,... | collective-permute-start | bytes 1179656 | tf_op jit(solution)/shard_map/ppermute | solution.py:565
  66.3 0.4 collective-permute-done.15.refs_8_
  66.7 3.1 %early_slots.3 = (f32[512,1280]{1,0:T(8,128)S(1)}, bf16[512,1024]{1,0:T(8,128)(2,1)S(1)}) custom-call(bf16[256,8192]{1,0:T(8,128)(2,1)S(1)} %bitcast.13, bf16[256,1536]{1,0:T(8,128)(2,1)S(1)} %collective-permute-done.7.refs_1_.refs_0_, bf16[256,1280]{1,0:T(8,128)(2,1)S(1)} %collective-permute-done.11.refs_1_, f32[256,128]{1,0:T(8,128)S(1)} %get-tuple-element.62.refs_2_, ...), custom_call_target="tpu_custom_call" | custom-call | flops 1342177280 | bytes 7340032 | tf_op jit(solution)/shard_map/early_slots/pallas_call | solution.py:332
  69.8 5.4 %collective-permute-done.14.refs_1_ = bf16[256,768]{1,0:T(8,128)(2,1)S(1)} collective-permute-done((bf16[256,768]{1,0:T(8,128)(2,1)S(1)}, bf16[256,768]{1,0:T(8,128)(2,1)S(1)}, u32[]{:S(2)}, u32[]{:S(2)}) %collective-permute-start.14) | collective-permute-done | bytes 393248 | tf_op jit(solution)/shard_map/ppermute | solution.py:565
  75.2 1.4 %collective-permute-start.17 = (bf16[256,768]{1,0:T(8,128)(2,1)S(1)}, bf16[256,768]{1,0:T(8,128)(2,1)S(1)}, u32[]{:S(2)}, u32[]{:S(2)}) collective-permute-start(bf16[256,768]{1,0:T(8,128)(2,1)S(1)} %collective-permute-done.14.refs_1_), channel_id=1, source_target_pairs={{0,1},{1,0},{2,3},{3,2},{4,5},{5,4},{6,7},{7,6},{8,9},{9,8},{10,11... | collective-permute-start | bytes 1179656 | tf_op jit(solution)/shard_map/ppermute | solution.py:585
  76.6 1.3 %collective-permute-start.19 = (bf16[256,512]{1,0:T(8,128)(2,1)S(1)}, bf16[256,512]{1,0:T(8,128)(2,1)S(1)}, u32[]{:S(2)}, u32[]{:S(2)}) collective-permute-start(bf16[256,512]{1,0:T(8,128)(2,1)S(1)} %slice.7), channel_id=1, source_target_pairs={{0,2},{1,3},{2,0},{3,1},{4,6},{5,7},{6,4},{7,5},{8,10},{9,11},{10,... | collective-permute-start | bytes 786440 | tf_op jit(solution)/shard_map/ppermute | solution.py:584
  77.9 1.5 %late_slot.2 = (f32[256,256]{1,0:T(8,128)S(1)}, f32[256,512]{1,0:T(8,128)S(1)}, bf16[256,256]{1,0:T(8,128)(2,1)S(1)}, bf16[256,512]{1,0:T(8,128)(2,1)S(1)}) custom-call(f32[512,1280]{1,0:T(8,128)S(1)} %get-tuple-element.74.before, bf16[512,1024]{1,0:T(8,128)(2,1)S(1)} %get-tuple-element.75.last_rows, bf16[256,1280]{1,0:T(8,128)(2,1)S(1)} %broadcast_select_fusion.refs_0_, ...), custom_call_target="tpu_custom_call" | custom-call | flops 805306368 | bytes 1572864 | tf_op jit(solution)/shard_map/late_slot/pallas_call | solution.py:375
  79.4 1.1 %collective-permute-start.18 = (bf16[256,256]{1,0:T(8,128)(2,1)S(1)}, bf16[256,256]{1,0:T(8,128)(2,1)S(1)}, u32[]{:S(2)}, u32[]{:S(2)}) collective-permute-start(bf16[256,256]{1,0:T(8,128)(2,1)S(1)} %get-tuple-element.79), channel_id=1, source_target_pairs={{0,4},{4,0},{1,5},{5,1},{2,6},{6,2},{3,7},{7,3},{8,12},{12,8},{9,1... | collective-permute-start | bytes 393224 | tf_op jit(solution)/shard_map/ppermute | solution.py:594
  80.6 4.1 %collective-permute-done.19.refs_1_ = bf16[256,512]{1,0:T(8,128)(2,1)S(1)} collective-permute-done((bf16[256,512]{1,0:T(8,128)(2,1)S(1)}, bf16[256,512]{1,0:T(8,128)(2,1)S(1)}, u32[]{:S(2)}, u32[]{:S(2)}) %collective-permute-start.19) | collective-permute-done | bytes 262176 | tf_op jit(solution)/shard_map/ppermute | solution.py:584
  84.6 0.8 collective-permute-start.20
  85.4 1.1 %collective-permute-start.25 = (bf16[256,512]{1,0:T(8,128)(2,1)S(1)}, bf16[256,512]{1,0:T(8,128)(2,1)S(1)}, u32[]{:S(2)}, u32[]{:S(2)}) collective-permute-start(bf16[256,512]{1,0:T(8,128)(2,1)S(1)} %get-tuple-element.90), channel_id=1, source_target_pairs={{0,4},{4,0},{1,5},{5,1},{2,6},{6,2},{3,7},{7,3},{8,12},{12,8},{9,1... | collective-permute-start | bytes 786440 | tf_op jit(solution)/shard_map/ppermute | solution.py:595
  86.6 1.3 %collective-permute-start.23 = (bf16[256,256]{1,0:T(8,128)(2,1)S(1)}, bf16[256,256]{1,0:T(8,128)(2,1)S(1)}, u32[]{:S(2)}, u32[]{:S(2)}) collective-permute-start(bf16[256,256]{1,0:T(8,128)(2,1)S(1)} %key_value.1.refs_7_.refs_5_), channel_id=1, source_target_pairs={{0,2},{1,3},{4,6},{5,7},{8,10},{9,11},{12,14},{13,15},{16,18},{17,... | collective-permute-start | bytes 393224 | tf_op jit(solution)/shard_map/ppermute | solution.py:616
  87.9 0.8 late_slot.3
  88.8 0.5 collective-permute-start.21
  89.2 0.6 collective-permute-start.22
  89.8 3.5 %collective-permute-done.23.refs_9_.refs_7_ = bf16[256,256]{1,0:T(8,128)(2,1)S(1)} collective-permute-done((bf16[256,256]{1,0:T(8,128)(2,1)S(1)}, bf16[256,256]{1,0:T(8,128)(2,1)S(1)}, u32[]{:S(2)}, u32[]{:S(2)}) %collective-permute-start.23) | collective-permute-done | bytes 131104 | tf_op jit(solution)/shard_map/ppermute | solution.py:616
  93.3 3.0 %collective-permute-start.24 = (bf16[256,256]{1,0:T(8,128)(2,1)S(1)}, bf16[256,256]{1,0:T(8,128)(2,1)S(1)}, u32[]{:S(2)}, u32[]{:S(2)}) collective-permute-start(bf16[256,256]{1,0:T(8,128)(2,1)S(1)} %collective-permute-done.23.refs_9_.refs_7_), channel_id=1, source_target_pairs={{2,3},{3,2},{6,7},{7,6},{10,11},{11,10},{14,15},{15,14},{18,19},{1... | collective-permute-start | bytes 393224 | tf_op jit(solution)/shard_map/ppermute | solution.py:618
  96.3 0.9 collective-permute-done.24.refs_10_.refs_8_
  97.3 2.4 %attention.2.refs_9_ = bf16[256,512]{1,0:T(8,128)(2,1)S(1)} custom-call(f32[256,256]{1,0:T(8,128)S(1)} %get-tuple-element.86.sums.refs_0_, f32[256,512]{1,0:T(8,128)S(1)} %get-tuple-element.89.refs_1_, bf16[256,256]{1,0:T(8,128)(2,1)S(1)} %collective-permute-done.18.back.refs_2_, bf16[256,512]{1,0:T(8,128)(2,1)S(1)} %collective-permute-done.25.refs_3_, ...), custom_call_target="tpu_custom_call" | custom-call | flops 536870912 | bytes 1048576 | tf_op jit(solution)/shard_map/attention/pallas_call | solution.py:478
  99.7 3.1 %attention.3 = bf16[256,1024]{1,0:T(8,128)(2,1)} custom-call(f32[256,512]{1,0:T(8,128)S(1)} %get-tuple-element.81.refs_0_, bf16[256,512]{1,0:T(8,128)(2,1)S(1)} %collective-permute-done.21.refs_1_, f32[1,1024]{1,0:T(1,128)S(1)} %bitcast.15, f32[256,128]{1,0:T(8,128)S(1)} %get-tuple-element.84.cosine.refs_5_.refs_3_, ...), custom_call_target="tpu_custom_call" | custom-call | flops 536870912 | bytes 1048576 | tf_op jit(solution)/shard_map/attention/pallas_call | solution.py:478
  (47 shorter events, 1.6 us)
Async XLA Ops:
  2.4 8.1 %copy-start.7 = (bf16[8192]{0:T(1024)(128)(2,1)S(1)}, bf16[8192]{0:T(1024)(128)(2,1)}, u32[]{:S(2)}) copy-start(bf16[8192]{0:T(1024)(128)(2,1)} %param.9) | copy-start | bytes 49156
  2.4 8.1 %copy-start.8 = (bf16[1024]{0:T(1024)(128)(2,1)S(1)}, bf16[1024]{0:T(1024)(128)(2,1)}, u32[]{:S(2)}) copy-start(bf16[1024]{0:T(1024)(128)(2,1)} %param.13) | copy-start | bytes 6148
  2.4 8.2 %copy-start.9 = (bf16[128]{0:T(256)(128)(2,1)S(1)}, bf16[128]{0:T(256)(128)(2,1)}, u32[]{:S(2)}) copy-start(bf16[128]{0:T(256)(128)(2,1)} %param.15) | copy-start | bytes 772
  2.5 8.2 %copy-start.10 = (bf16[128]{0:T(256)(128)(2,1)S(1)}, bf16[128]{0:T(256)(128)(2,1)}, u32[]{:S(2)}) copy-start(bf16[128]{0:T(256)(128)(2,1)} %param.14) | copy-start | bytes 772
  2.5 16.0 %collective-permute-start = (bf16[256,1280]{1,0:T(8,128)(2,1)}, bf16[256,1280]{1,0:T(8,128)(2,1)S(1)}, u32[]{:S(2)}, u32[]{:S(2)}) collective-permute-start(bf16[256,1280]{1,0:T(8,128)(2,1)} %get-tuple-element.48), channel_id=1, source_target_pairs={{0,8},{8,0},{16,24},{24,16},{1,9},{9,1},{17,25},{25,17},{2,10},{10... | collective-permute-start | bytes 1966088 | tf_op jit(solution)/shard_map/ppermute | solution.py:517
  2.7 18.8 %collective-permute-start.1 = (bf16[256,1280]{1,0:T(8,128)(2,1)}, bf16[256,1280]{1,0:T(8,128)(2,1)}, u32[]{:S(2)}, u32[]{:S(2)}) collective-permute-start(bf16[256,1280]{1,0:T(8,128)(2,1)} %get-tuple-element.48), channel_id=1, source_target_pairs={{8,16},{16,8},{9,17},{17,9},{10,18},{18,10},{11,19},{19,11},{12,20... | collective-permute-start | bytes 1966088 | tf_op jit(solution)/shard_map/ppermute | solution.py:518
  7.0 15.4 %collective-permute-start.2 = (bf16[256,1280]{1,0:T(8,128)(2,1)}, bf16[256,1280]{1,0:T(8,128)(2,1)}, u32[]{:S(2)}, u32[]{:S(2)}) collective-permute-start(bf16[256,1280]{1,0:T(8,128)(2,1)} %get-tuple-element.49), channel_id=1, source_target_pairs={{0,4},{4,0},{1,5},{5,1},{2,6},{6,2},{3,7},{7,3},{8,12},{12,8},{9,1... | collective-permute-start | bytes 1966088 | tf_op jit(solution)/shard_map/ppermute | solution.py:519
  8.3 40.5 %copy-start.2 = (bf16[1024,1024]{1,0:T(8,128)(2,1)S(1)}, bf16[1024,1024]{1,0:T(8,128)(2,1)}, u32[]{:S(2)}) copy-start(bf16[1024,1024]{1,0:T(8,128)(2,1)} %refs_7_.1) | copy-start | bytes 6291460
  18.4 4.0 %copy-start.5 = (bf16[256,1280]{1,0:T(8,128)(2,1)}, bf16[256,1280]{1,0:T(8,128)(2,1)S(1)}, u32[]{:S(2)}) copy-start(bf16[256,1280]{1,0:T(8,128)(2,1)S(1)} %collective-permute-done.refs_8_) | copy-start | bytes 1966084
  22.4 13.7 %collective-permute-start.5 = (bf16[256,1280]{1,0:T(8,128)(2,1)}, bf16[256,1280]{1,0:T(8,128)(2,1)}, u32[]{:S(2)}, u32[]{:S(2)}) collective-permute-start(bf16[256,1280]{1,0:T(8,128)(2,1)} %collective-permute-done.1), channel_id=1, source_target_pairs={{8,0},{16,24},{9,1},{17,25},{10,2},{18,26},{11,3},{19,27},{12,4},{... | collective-permute-start | bytes 1966088 | tf_op jit(solution)/shard_map/ppermute | solution.py:534
  24.6 17.7 %collective-permute-start.7 = (bf16[256,1536]{1,0:T(8,128)(2,1)}, bf16[256,1536]{1,0:T(8,128)(2,1)S(1)}, u32[]{:S(2)}, u32[]{:S(2)}) collective-permute-start(bf16[256,1536]{1,0:T(8,128)(2,1)} %pack.3), channel_id=1, source_target_pairs={{0,4},{4,0},{1,5},{5,1},{2,6},{6,2},{3,7},{7,3},{8,12},{12,8},{9,1... | collective-permute-start | bytes 2359304 | tf_op jit(solution)/shard_map/ppermute | solution.py:536
  25.8 16.0 %collective-permute-start.3 = (bf16[256,1280]{1,0:T(8,128)(2,1)}, bf16[256,1280]{1,0:T(8,128)(2,1)}, u32[]{:S(2)}, u32[]{:S(2)}) collective-permute-start(bf16[256,1280]{1,0:T(8,128)(2,1)} %copy-done.5), channel_id=1, source_target_pairs={{8,16},{16,8},{9,17},{17,9},{10,18},{18,10},{11,19},{19,11},{12,20... | collective-permute-start | bytes 1966088 | tf_op jit(solution)/shard_map/ppermute | solution.py:533
  28.3 13.9 %collective-permute-start.6 = (bf16[256,1280]{1,0:T(8,128)(2,1)}, bf16[256,1280]{1,0:T(8,128)(2,1)}, u32[]{:S(2)}, u32[]{:S(2)}) collective-permute-start(bf16[256,1280]{1,0:T(8,128)(2,1)} %copy-done.5), channel_id=1, source_target_pairs={{0,2},{1,3},{2,0},{3,1},{4,6},{5,7},{6,4},{7,5},{8,10},{9,11},{10,... | collective-permute-start | bytes 1966088 | tf_op jit(solution)/shard_map/ppermute | solution.py:535
  28.6 13.6 %collective-permute-start.8 = (bf16[256,1280]{1,0:T(8,128)(2,1)}, bf16[256,1280]{1,0:T(8,128)(2,1)}, u32[]{:S(2)}, u32[]{:S(2)}) collective-permute-start(bf16[256,1280]{1,0:T(8,128)(2,1)} %copy-done.5), channel_id=1, source_target_pairs={{0,1},{1,0},{2,3},{3,2},{4,5},{5,4},{6,7},{7,6},{8,9},{9,8},{10,11... | collective-permute-start | bytes 1966088 | tf_op jit(solution)/shard_map/ppermute | solution.py:537
  31.6 2.2 %copy-start = (bf16[1,256,8192]{2,1,0:T(8,128)(2,1)S(1)}, bf16[1,256,8192]{2,1,0:T(8,128)(2,1)}, u32[]{:S(2)}) copy-start(bf16[1,256,8192]{2,1,0:T(8,128)(2,1)} %param.8) | copy-start | bytes 12582916
  33.8 15.1 %copy-start.1 = (bf16[1,256,8192]{2,1,0:T(8,128)(2,1)S(1)}, bf16[1,256,8192]{2,1,0:T(8,128)(2,1)}, u32[]{:S(2)}) copy-start(bf16[1,256,8192]{2,1,0:T(8,128)(2,1)} %param.8) | copy-start | bytes 12582916
  33.8 15.1 %copy-start.3 = (bf16[1024,128]{1,0:T(8,128)(2,1)S(1)}, bf16[1024,128]{1,0:T(8,128)(2,1)}, u32[]{:S(2)}) copy-start(bf16[1024,128]{1,0:T(8,128)(2,1)} %refs_5_.1) | copy-start | bytes 786436
  33.8 15.1 %copy-start.4 = (bf16[1024,128]{1,0:T(8,128)(2,1)S(1)}, bf16[1024,128]{1,0:T(8,128)(2,1)}, u32[]{:S(2)}) copy-start(bf16[1024,128]{1,0:T(8,128)(2,1)} %refs_6_.1) | copy-start | bytes 786436
  33.8 15.1 %copy-start.6 = (bf16[256,1280]{1,0:T(8,128)(2,1)S(1)}, bf16[256,1280]{1,0:T(8,128)(2,1)}, u32[]{:S(2)}) copy-start(bf16[256,1280]{1,0:T(8,128)(2,1)} %copy-done.5) | copy-start | bytes 1966084
  36.1 5.6 %collective-permute-start.4 = (f32[1,256]{1,0:T(1,128)S(1)}, f32[1,256]{1,0:T(1,128)S(1)}, u32[]{:S(2)}, u32[]{:S(2)}) collective-permute-start(f32[1,256]{1,0:T(1,128)S(1)} %get-tuple-element.52), channel_id=1, source_target_pairs={{0,4},{4,0},{1,5},{5,1},{2,6},{6,2},{3,7},{7,3},{8,12},{12,8},{9,1... | collective-permute-start | bytes 3080 | tf_op jit(solution)/shard_map/ppermute | solution.py:539
  42.2 6.6 %collective-permute-start.13 = (bf16[256,1280]{1,0:T(8,128)(2,1)}, bf16[256,1280]{1,0:T(8,128)(2,1)S(1)}, u32[]{:S(2)}, u32[]{:S(2)}) collective-permute-start(bf16[256,1280]{1,0:T(8,128)(2,1)} %collective-permute-done.6.refs_9_), channel_id=1, source_target_pairs={{0,1},{1,0},{2,3},{3,2},{4,5},{5,4},{6,7},{7,6},{8,9},{9,8},{10,11... | collective-permute-start | bytes 1966088 | tf_op jit(solution)/shard_map/ppermute | solution.py:547
  45.9 15.9 %collective-permute-start.9 = (bf16[256,1280]{1,0:T(8,128)(2,1)}, bf16[256,1280]{1,0:T(8,128)(2,1)S(1)}, u32[]{:S(2)}, u32[]{:S(2)}) collective-permute-start(bf16[256,1280]{1,0:T(8,128)(2,1)} %collective-permute-done.3), channel_id=1, source_target_pairs={{8,0},{16,24},{9,1},{17,25},{10,2},{18,26},{11,3},{19,27},{12,4},{... | collective-permute-start | bytes 1966088 | tf_op jit(solution)/shard_map/ppermute | solution.py:544
  47.2 16.4 %collective-permute-start.10 = (bf16[256,1280]{1,0:T(8,128)(2,1)S(1)}, bf16[256,1280]{1,0:T(8,128)(2,1)S(1)}, u32[]{:S(2)}, u32[]{:S(2)}) collective-permute-start(bf16[256,1280]{1,0:T(8,128)(2,1)S(1)} %broadcast_select_fusion.1.refs_5_), channel_id=1, source_target_pairs={{0,2},{1,3},{2,0},{3,1},{4,6},{5,7},{6,4},{7,5},{8,10},{9,11},{10,... | collective-permute-start | bytes 1966088 | tf_op jit(solution)/shard_map/ppermute | solution.py:545
  47.5 16.4 %collective-permute-start.12 = (bf16[256,1280]{1,0:T(8,128)(2,1)S(1)}, bf16[256,1280]{1,0:T(8,128)(2,1)S(1)}, u32[]{:S(2)}, u32[]{:S(2)}) collective-permute-start(bf16[256,1280]{1,0:T(8,128)(2,1)S(1)} %broadcast_select_fusion.1.refs_5_), channel_id=1, source_target_pairs={{0,1},{1,0},{2,3},{3,2},{4,5},{5,4},{6,7},{7,6},{8,9},{9,8},{10,11... | collective-permute-start | bytes 1966088 | tf_op jit(solution)/shard_map/ppermute | solution.py:548
  47.8 16.1 %collective-permute-start.11 = (bf16[256,1280]{1,0:T(8,128)(2,1)S(1)}, bf16[256,1280]{1,0:T(8,128)(2,1)S(1)}, u32[]{:S(2)}, u32[]{:S(2)}) collective-permute-start(bf16[256,1280]{1,0:T(8,128)(2,1)S(1)} %get-tuple-element.59), channel_id=1, source_target_pairs={{0,4},{4,0},{1,5},{5,1},{2,6},{6,2},{3,7},{7,3},{8,12},{12,8},{9,1... | collective-permute-start | bytes 1966088 | tf_op jit(solution)/shard_map/ppermute | solution.py:546
  63.9 2.7 %collective-permute-start.15 = (bf16[256,1280]{1,0:T(8,128)(2,1)S(1)}, bf16[256,1280]{1,0:T(8,128)(2,1)S(1)}, u32[]{:S(2)}, u32[]{:S(2)}) collective-permute-start(bf16[256,1280]{1,0:T(8,128)(2,1)S(1)} %collective-permute-done.10.refs_6_), channel_id=1, source_target_pairs={{0,1},{1,0},{2,3},{3,2},{4,5},{5,4},{6,7},{7,6},{8,9},{9,8},{10,11... | collective-permute-start | bytes 1966088 | tf_op jit(solution)/shard_map/ppermute | solution.py:566
  65.0 10.3 %collective-permute-start.16 = (bf16[256,1280]{1,0:T(8,128)(2,1)S(1)}, bf16[256,1280]{1,0:T(8,128)(2,1)S(1)}, u32[]{:S(2)}, u32[]{:S(2)}) collective-permute-start(bf16[256,1280]{1,0:T(8,128)(2,1)S(1)} %broadcast_select_fusion.refs_0_), channel_id=1, source_target_pairs={{0,1},{1,0},{2,3},{3,2},{4,5},{5,4},{6,7},{7,6},{8,9},{9,8},{10,11... | collective-permute-start | bytes 1966088 | tf_op jit(solution)/shard_map/ppermute | solution.py:567
  65.0 10.2 %collective-permute-start.14 = (bf16[256,768]{1,0:T(8,128)(2,1)S(1)}, bf16[256,768]{1,0:T(8,128)(2,1)S(1)}, u32[]{:S(2)}, u32[]{:S(2)}) collective-permute-start(bf16[256,768]{1,0:T(8,128)(2,1)S(1)} %slice.6), channel_id=1, source_target_pairs={{0,2},{1,3},{2,0},{3,1},{4,6},{5,7},{6,4},{7,5},{8,10},{9,11},{10,... | collective-permute-start | bytes 1179656 | tf_op jit(solution)/shard_map/ppermute | solution.py:565
  75.2 2.7 %collective-permute-start.17 = (bf16[256,768]{1,0:T(8,128)(2,1)S(1)}, bf16[256,768]{1,0:T(8,128)(2,1)S(1)}, u32[]{:S(2)}, u32[]{:S(2)}) collective-permute-start(bf16[256,768]{1,0:T(8,128)(2,1)S(1)} %collective-permute-done.14.refs_1_), channel_id=1, source_target_pairs={{0,1},{1,0},{2,3},{3,2},{4,5},{5,4},{6,7},{7,6},{8,9},{9,8},{10,11... | collective-permute-start | bytes 1179656 | tf_op jit(solution)/shard_map/ppermute | solution.py:585
  76.6 8.0 %collective-permute-start.19 = (bf16[256,512]{1,0:T(8,128)(2,1)S(1)}, bf16[256,512]{1,0:T(8,128)(2,1)S(1)}, u32[]{:S(2)}, u32[]{:S(2)}) collective-permute-start(bf16[256,512]{1,0:T(8,128)(2,1)S(1)} %slice.7), channel_id=1, source_target_pairs={{0,2},{1,3},{2,0},{3,1},{4,6},{5,7},{6,4},{7,5},{8,10},{9,11},{10,... | collective-permute-start | bytes 786440 | tf_op jit(solution)/shard_map/ppermute | solution.py:584
  79.4 5.2 %collective-permute-start.18 = (bf16[256,256]{1,0:T(8,128)(2,1)S(1)}, bf16[256,256]{1,0:T(8,128)(2,1)S(1)}, u32[]{:S(2)}, u32[]{:S(2)}) collective-permute-start(bf16[256,256]{1,0:T(8,128)(2,1)S(1)} %get-tuple-element.79), channel_id=1, source_target_pairs={{0,4},{4,0},{1,5},{5,1},{2,6},{6,2},{3,7},{7,3},{8,12},{12,8},{9,1... | collective-permute-start | bytes 393224 | tf_op jit(solution)/shard_map/ppermute | solution.py:594
  84.6 3.3 %collective-permute-start.20 = (bf16[256,512]{1,0:T(8,128)(2,1)S(1)}, bf16[256,512]{1,0:T(8,128)(2,1)S(1)}, u32[]{:S(2)}, u32[]{:S(2)}) collective-permute-start(bf16[256,512]{1,0:T(8,128)(2,1)S(1)} %collective-permute-done.19.refs_1_), channel_id=1, source_target_pairs={{0,1},{1,0},{2,3},{3,2},{4,5},{5,4},{6,7},{7,6},{8,9},{9,8},{10,11... | collective-permute-start | bytes 786440 | tf_op jit(solution)/shard_map/ppermute | solution.py:597
  85.4 10.9 %collective-permute-start.25 = (bf16[256,512]{1,0:T(8,128)(2,1)S(1)}, bf16[256,512]{1,0:T(8,128)(2,1)S(1)}, u32[]{:S(2)}, u32[]{:S(2)}) collective-permute-start(bf16[256,512]{1,0:T(8,128)(2,1)S(1)} %get-tuple-element.90), channel_id=1, source_target_pairs={{0,4},{4,0},{1,5},{5,1},{2,6},{6,2},{3,7},{7,3},{8,12},{12,8},{9,1... | collective-permute-start | bytes 786440 | tf_op jit(solution)/shard_map/ppermute | solution.py:595
  86.6 6.7 %collective-permute-start.23 = (bf16[256,256]{1,0:T(8,128)(2,1)S(1)}, bf16[256,256]{1,0:T(8,128)(2,1)S(1)}, u32[]{:S(2)}, u32[]{:S(2)}) collective-permute-start(bf16[256,256]{1,0:T(8,128)(2,1)S(1)} %key_value.1.refs_7_.refs_5_), channel_id=1, source_target_pairs={{0,2},{1,3},{4,6},{5,7},{8,10},{9,11},{12,14},{13,15},{16,18},{17,... | collective-permute-start | bytes 393224 | tf_op jit(solution)/shard_map/ppermute | solution.py:616
  88.8 10.9 %collective-permute-start.21 = (bf16[256,512]{1,0:T(8,128)(2,1)S(1)}, bf16[256,512]{1,0:T(8,128)(2,1)S(1)}, u32[]{:S(2)}, u32[]{:S(2)}) collective-permute-start(bf16[256,512]{1,0:T(8,128)(2,1)S(1)} %get-tuple-element.82), channel_id=1, source_target_pairs={{0,4},{4,0},{1,5},{5,1},{2,6},{6,2},{3,7},{7,3},{8,12},{12,8},{9,1... | collective-permute-start | bytes 786440 | tf_op jit(solution)/shard_map/ppermute | solution.py:605
  89.2 7.1 %collective-permute-start.22 = (bf16[256,256]{1,0:T(8,128)(2,1)S(1)}, bf16[256,256]{1,0:T(8,128)(2,1)S(1)}, u32[]{:S(2)}, u32[]{:S(2)}) collective-permute-start(bf16[256,256]{1,0:T(8,128)(2,1)S(1)} %key_value.1.refs_7_.refs_5_), channel_id=1, source_target_pairs={{0,1},{1,0},{2,3},{3,2},{4,5},{5,4},{6,7},{7,6},{8,9},{9,8},{10,11... | collective-permute-start | bytes 393224 | tf_op jit(solution)/shard_map/ppermute | solution.py:617
  93.3 4.0 %collective-permute-start.24 = (bf16[256,256]{1,0:T(8,128)(2,1)S(1)}, bf16[256,256]{1,0:T(8,128)(2,1)S(1)}, u32[]{:S(2)}, u32[]{:S(2)}) collective-permute-start(bf16[256,256]{1,0:T(8,128)(2,1)S(1)} %collective-permute-done.23.refs_9_.refs_7_), channel_id=1, source_target_pairs={{2,3},{3,2},{6,7},{7,6},{10,11},{11,10},{14,15},{15,14},{18,19},{1... | collective-permute-start | bytes 393224 | tf_op jit(solution)/shard_map/ppermute | solution.py:618

commit v8 on v7

--- a/solution.py
+++ b/solution.py
@@ -409,7 +409,8 @@
     blocks, refs = (refs[:4], refs[4:])
     if first:
         done, *refs = refs
-    out, keys, values = refs
+    out, keys, values, held, sems = refs
+    spare = out.shape[1] // cosine.shape[1]
     rows = out.shape[0]
     head = cosine.shape[1]
     slab = lax.axis_index("ctx")
@@ -423,11 +424,12 @@
     row_ids = odd * rows + lax.broadcasted_iota(jnp.int32, near, 0)
     visible = lax.broadcasted_iota(jnp.int32, near, 1) <= row_ids
     power = scale * math.log2(math.e)
-    if first:
-        out[:, :first] = done[...]
 
     def all_heads(far):
         at = first
+        flights = []
+        if first:
+            flights += started([(done, out.at[:, pl.ds(0, first)])], sems, spare)
         for own, other, skip in zip(sums, backs, skips):
             for column in range(skip, own.shape[1], head):
                 cols = slice(column, column + head)
@@ -453,8 +455,16 @@
                     mixed = mixed + jnp.dot(
                         exps.astype(jnp.bfloat16), value, preferred_element_type=jnp.float32
                     )
-                out[:, at : at + head] = (mixed / length).astype(jnp.bfloat16)
+                result = (mixed / length).astype(jnp.bfloat16)
+                if first:
+                    part = held.at[:, pl.ds(at - first, head)]
+                    part[...] = result
+                    flights += started([(part, out.at[:, pl.ds(at, head)])], sems, at // head)
+                else:
+                    out[:, at : at + head] = result
                 at += head
+        for flight in flights:
+            flight.wait()
 
     @pl.when(slab < 2)
     def _():
@@ -465,24 +475,27 @@
         all_heads((across, corner))
 
 
-def attention(sums, backs, skips, bias, cosine, sine_table, blocks, done=None):
+def attention(first, sums, backs, skips, bias, cosine, sine_table, blocks, done=None):
     rows = sums[0].shape[0]
     width = sum(own.shape[1] - skip for own, skip in zip(sums, skips))
     head = cosine.shape[1]
-    first = 0 if done is None else done.shape[1]
     inside = pl.BlockSpec(memory_space=pltpu.VMEM)
     args = [*sums, *backs, bias, cosine, sine_table, *blocks]
+    in_specs = [inside] * len(args)
     if first:
         args.append(done)
+        in_specs.append(inside)
     total = 4 * rows * rows * (width // head)
     return pl.pallas_call(
         functools.partial(attention_body, head ** (-0.5), first, skips),
         out_shape=jax.ShapeDtypeStruct((rows, first + width), jnp.bfloat16),
-        in_specs=[inside] * len(args),
-        out_specs=inside,
+        in_specs=in_specs,
+        out_specs=pl.BlockSpec(memory_space=pl.ANY) if first else inside,
         scratch_shapes=[
             pltpu.VMEM((2 * rows, head), jnp.bfloat16),
             pltpu.VMEM((2 * rows, head), jnp.bfloat16),
+            pltpu.VMEM((rows, width), jnp.bfloat16),
+            pltpu.SemaphoreType.DMA(((first + width) // head + 1,)),
         ],
         cost_estimate=pl.CostEstimate(
             flops=4 * total * head, bytes_accessed=8 * rows * width, transcendentals=total
@@ -618,8 +631,8 @@
     kv_corner = lax.ppermute(kv_across, "ctx", [(2, 3), (3, 2)])
     blocks = (key_value, kv_beside, kv_across, kv_corner)
     tables = (bias_q, cosine, sine_table, blocks)
-    attended = attention((sums_0, sums_1), (back_0, back_1), (kv_width, 0), *tables)
-    attended = attention((sums_2,), (back_2,), (0,), *tables, attended)
+    attended = attention(0, (sums_0, sums_1), (back_0, back_1), (kv_width, 0), *tables)
+    attended = attention(half - kv_width, (sums_2,), (back_2,), (0,), *tables, attended)
     return attended[None]
 
 

time: 103 us -> 103 us (level)
  transfers between devices with their start and end apart: 26 -> 26, of which waited for: 15 -> 15; matrix products, arithmetic and copies ran while one was open for 3% -> 3% of each run, Pallas kernels for 16% -> 17%
where the time goes in v8:
time: 103 us
  waiting for transfers between devices  38.5 us (37%)
  starting transfers between devices  36.2 us (35%)
  Pallas kernels  22.4 us (22%)
  other arithmetic  3.07 us (3%)
  local copies, waits for them, and re-layouts  2.3 us (2%)
    ppermute x1, waiting for transfers between devices, planned(): fourth_out = lax.ppermute(fourth_in, 'line', outward)  8.08 us
    pallas_call x2, Pallas kernels, early_slots(): pl.pallas_call(functools.partial(early_body, slots, guests, local, final)...  7.93 us
    ppermute x1, waiting for transfers between devices, planned(): second = lax.ppermute(mine, 'line', ends)  7.11 us
    pallas_call x2, Pallas kernels, attention(): pl.pallas_call(functools.partial(attention_body, head ** (-0.5), first, s...  5.43 us
    ppermute x1, waiting for transfers between devices, planned(): fourth_far_1 = lax.ppermute(fourth[:, :half], 'ctx', across)  5.39 us
    pallas_call x2, Pallas kernels, pack(): pl.pallas_call(functools.partial(pack_body, sent_parts, len(weights), dep...  4.59 us
    ppermute x1, starting transfers between devices, planned(): third_in = lax.ppermute(mine, 'line', middle)  4.32 us
    ppermute x1, waiting for transfers between devices, planned(): fourth_far_2 = lax.ppermute(fourth[:, half:], 'ctx', across)  4.07 us
  transfers between devices with their start and end apart: 26, of which 15 were waited for; matrix products, arithmetic and copies ran while one was open for 3% of the time, Pallas kernels for 17%

profile of v8, /device:TPU:11, one launch (start us, length us, event | category | flops | bytes accessed | tf_op | source)
XLA Modules:
  0.0 102.9 jit_solution(1161712735919105614)
XLA Ops:
  0.0 2.4 %pack.2 = (bf16[256,1280]{1,0:T(8,128)(2,1)}, bf16[256,1280]{1,0:T(8,128)(2,1)}) custom-call(bf16[256,8192]{1,0:T(8,128)(2,1)} %bitcast.9, bf16[1024,128]{1,0:T(8,128)(2,1)} %refs_5_.1, bf16[1024,128]{1,0:T(8,128)(2,1)} %refs_6_.1, bf16[1024,1024]{1,0:T(8,128)(2,1)} %refs_7_.1), custom_call_target="tpu_custom_call" | custom-call | tf_op jit(solution)/shard_map/pack/pallas_call | solution.py:171
  2.7 4.3 %collective-permute-start.1 = (bf16[256,1280]{1,0:T(8,128)(2,1)}, bf16[256,1280]{1,0:T(8,128)(2,1)}, u32[]{:S(2)}, u32[]{:S(2)}) collective-permute-start(bf16[256,1280]{1,0:T(8,128)(2,1)} %get-tuple-element.48), channel_id=1, source_target_pairs={{8,16},{16,8},{9,17},{17,9},{10,18},{18,10},{11,19},{19,11},{12,20... | collective-permute-start | bytes 1966088 | tf_op jit(solution)/shard_map/ppermute | solution.py:531
  7.0 1.3 %collective-permute-start.2 = (bf16[256,1280]{1,0:T(8,128)(2,1)}, bf16[256,1280]{1,0:T(8,128)(2,1)}, u32[]{:S(2)}, u32[]{:S(2)}) collective-permute-start(bf16[256,1280]{1,0:T(8,128)(2,1)} %get-tuple-element.49), channel_id=1, source_target_pairs={{0,4},{4,0},{1,5},{5,1},{2,6},{6,2},{3,7},{7,3},{8,12},{12,8},{9,1... | collective-permute-start | bytes 1966088 | tf_op jit(solution)/shard_map/ppermute | solution.py:532
  8.3 2.2 %pack.3 = bf16[256,1536]{1,0:T(8,128)(2,1)} custom-call(bf16[256,8192]{1,0:T(8,128)(2,1)} %bitcast.10), custom_call_target="tpu_custom_call" | custom-call | tf_op jit(solution)/shard_map/pack/pallas_call | solution.py:171
  10.6 0.5 fusion
  11.3 7.1 %collective-permute-done.refs_8_ = bf16[256,1280]{1,0:T(8,128)(2,1)S(1)} collective-permute-done((bf16[256,1280]{1,0:T(8,128)(2,1)}, bf16[256,1280]{1,0:T(8,128)(2,1)S(1)}, u32[]{:S(2)}, u32[]{:S(2)}) %collective-permute-start) | collective-permute-done | bytes 655392 | tf_op jit(solution)/shard_map/ppermute | solution.py:530
  18.4 3.0 %collective-permute-done.1 = bf16[256,1280]{1,0:T(8,128)(2,1)} collective-permute-done((bf16[256,1280]{1,0:T(8,128)(2,1)}, bf16[256,1280]{1,0:T(8,128)(2,1)}, u32[]{:S(2)}, u32[]{:S(2)}) %collective-permute-start.1) | collective-permute-done | bytes 655392 | tf_op jit(solution)/shard_map/ppermute | solution.py:531
  21.5 0.9 collective-permute-done.2.refs_0_
  22.4 2.2 %collective-permute-start.5 = (bf16[256,1280]{1,0:T(8,128)(2,1)}, bf16[256,1280]{1,0:T(8,128)(2,1)}, u32[]{:S(2)}, u32[]{:S(2)}) collective-permute-start(bf16[256,1280]{1,0:T(8,128)(2,1)} %collective-permute-done.1), channel_id=1, source_target_pairs={{8,0},{16,24},{9,1},{17,25},{10,2},{18,26},{11,3},{19,27},{12,4},{... | collective-permute-start | bytes 1966088 | tf_op jit(solution)/shard_map/ppermute | solution.py:547
  24.6 1.2 %collective-permute-start.7 = (bf16[256,1536]{1,0:T(8,128)(2,1)}, bf16[256,1536]{1,0:T(8,128)(2,1)S(1)}, u32[]{:S(2)}, u32[]{:S(2)}) collective-permute-start(bf16[256,1536]{1,0:T(8,128)(2,1)} %pack.3), channel_id=1, source_target_pairs={{0,4},{4,0},{1,5},{5,1},{2,6},{6,2},{3,7},{7,3},{8,12},{12,8},{9,1... | collective-permute-start | bytes 2359304 | tf_op jit(solution)/shard_map/ppermute | solution.py:549
  25.8 2.5 %collective-permute-start.3 = (bf16[256,1280]{1,0:T(8,128)(2,1)}, bf16[256,1280]{1,0:T(8,128)(2,1)}, u32[]{:S(2)}, u32[]{:S(2)}) collective-permute-start(bf16[256,1280]{1,0:T(8,128)(2,1)} %copy-done.5), channel_id=1, source_target_pairs={{8,16},{16,8},{9,17},{17,9},{10,18},{18,10},{11,19},{19,11},{12,20... | collective-permute-start | bytes 1966088 | tf_op jit(solution)/shard_map/ppermute | solution.py:546
  28.3 0.3 collective-permute-start.6
  28.6 3.0 %collective-permute-start.8 = (bf16[256,1280]{1,0:T(8,128)(2,1)}, bf16[256,1280]{1,0:T(8,128)(2,1)}, u32[]{:S(2)}, u32[]{:S(2)}) collective-permute-start(bf16[256,1280]{1,0:T(8,128)(2,1)} %copy-done.5), channel_id=1, source_target_pairs={{0,1},{1,0},{2,3},{3,2},{4,5},{5,4},{6,7},{7,6},{8,9},{9,8},{10,11... | collective-permute-start | bytes 1966088 | tf_op jit(solution)/shard_map/ppermute | solution.py:550
  31.6 2.2 %copy-done = bf16[1,256,8192]{2,1,0:T(8,128)(2,1)S(1)} copy-done((bf16[1,256,8192]{2,1,0:T(8,128)(2,1)S(1)}, bf16[1,256,8192]{2,1,0:T(8,128)(2,1)}, u32[]{:S(2)}) %copy-start) | copy-done | bytes 4194328
  33.8 2.0 %prepare.1 = (bf16[256,1280]{1,0:T(8,128)(2,1)S(1)}, f32[256,128]{1,0:T(8,128)S(1)}, f32[1,256]{1,0:T(1,128)S(1)}) custom-call(bf16[256,8192]{1,0:T(8,128)(2,1)S(1)} %bitcast.11), custom_call_target="tpu_custom_call" | custom-call | tf_op jit(solution)/shard_map/prepare/pallas_call | solution.py:224
  36.1 1.2 %collective-permute-start.4 = (f32[1,256]{1,0:T(1,128)S(1)}, f32[1,256]{1,0:T(1,128)S(1)}, u32[]{:S(2)}, u32[]{:S(2)}) collective-permute-start(f32[1,256]{1,0:T(1,128)S(1)} %get-tuple-element.52), channel_id=1, source_target_pairs={{0,4},{4,0},{1,5},{5,1},{2,6},{6,2},{3,7},{7,3},{8,12},{12,8},{9,1... | collective-permute-start | bytes 3080 | tf_op jit(solution)/shard_map/ppermute | solution.py:552
  37.4 1.2 %broadcast_select_fusion.1.refs_5_ = bf16[256,1280]{1,0:T(8,128)(2,1)S(1)} fusion(bf16[256,1280]{1,0:T(8,128)(2,1)} %collective-permute-done.1, bf16[256,1280]{1,0:T(8,128)(2,1)} %collective-permute-done.5, pred[]{:T(512)S(6)} %or.3), kind=kLoop, calls=%fused_computation.1 | loop fusion | flops 327680 | bytes 1966081 | tf_op jit(solution)/shard_map/jit(_where)/select_n | solution.py:553
  38.5 3.2 %collective-permute-done.4.refs_3_ = f32[1,256]{1,0:T(1,128)S(1)} collective-permute-done((f32[1,256]{1,0:T(1,128)S(1)}, f32[1,256]{1,0:T(1,128)S(1)}, u32[]{:S(2)}, u32[]{:S(2)}) %collective-permute-start.4) | collective-permute-done | bytes 1056 | tf_op jit(solution)/shard_map/ppermute | solution.py:552
  41.8 0.4 collective-permute-done.6.refs_9_
  42.2 3.6 %collective-permute-start.13 = (bf16[256,1280]{1,0:T(8,128)(2,1)}, bf16[256,1280]{1,0:T(8,128)(2,1)S(1)}, u32[]{:S(2)}, u32[]{:S(2)}) collective-permute-start(bf16[256,1280]{1,0:T(8,128)(2,1)} %collective-permute-done.6.refs_9_), channel_id=1, source_target_pairs={{0,1},{1,0},{2,3},{3,2},{4,5},{5,4},{6,7},{7,6},{8,9},{9,8},{10,11... | collective-permute-start | bytes 1966088 | tf_op jit(solution)/shard_map/ppermute | solution.py:560
  45.9 1.3 %collective-permute-start.9 = (bf16[256,1280]{1,0:T(8,128)(2,1)}, bf16[256,1280]{1,0:T(8,128)(2,1)S(1)}, u32[]{:S(2)}, u32[]{:S(2)}) collective-permute-start(bf16[256,1280]{1,0:T(8,128)(2,1)} %collective-permute-done.3), channel_id=1, source_target_pairs={{8,0},{16,24},{9,1},{17,25},{10,2},{18,26},{11,3},{19,27},{12,4},{... | collective-permute-start | bytes 1966088 | tf_op jit(solution)/shard_map/ppermute | solution.py:557
  47.8 1.1 %collective-permute-start.11 = (bf16[256,1280]{1,0:T(8,128)(2,1)S(1)}, bf16[256,1280]{1,0:T(8,128)(2,1)S(1)}, u32[]{:S(2)}, u32[]{:S(2)}) collective-permute-start(bf16[256,1280]{1,0:T(8,128)(2,1)S(1)} %get-tuple-element.59), channel_id=1, source_target_pairs={{0,4},{4,0},{1,5},{5,1},{2,6},{6,2},{3,7},{7,3},{8,12},{12,8},{9,1... | collective-permute-start | bytes 1966088 | tf_op jit(solution)/shard_map/ppermute | solution.py:559
  48.9 4.8 %early_slots.2.refs_9_ = f32[512,1280]{1,0:T(8,128)S(1)} custom-call(bf16[256,8192]{1,0:T(8,128)(2,1)S(1)} %bitcast.12, bf16[256,1280]{1,0:T(8,128)(2,1)} %collective-permute-done.2.refs_0_, bf16[256,1536]{1,0:T(8,128)(2,1)S(1)} %collective-permute-done.7.refs_1_.refs_0_, f32[256,128]{1,0:T(8,128)S(1)} %get-tuple-element.62.refs_2_, ...), custom_call_target="tpu_custom_call" | custom-call | flops 2684354560 | bytes 9961472 | tf_op jit(solution)/shard_map/early_slots/pallas_call | solution.py:332
  53.7 8.1 %collective-permute-done.9 = bf16[256,1280]{1,0:T(8,128)(2,1)S(1)} collective-permute-done((bf16[256,1280]{1,0:T(8,128)(2,1)}, bf16[256,1280]{1,0:T(8,128)(2,1)S(1)}, u32[]{:S(2)}, u32[]{:S(2)}) %collective-permute-start.9) | collective-permute-done | bytes 655392 | tf_op jit(solution)/shard_map/ppermute | solution.py:557
  61.8 1.2 %broadcast_select_fusion.refs_0_ = bf16[256,1280]{1,0:T(8,128)(2,1)S(1)} fusion(bf16[256,1280]{1,0:T(8,128)(2,1)} %collective-permute-done.3, bf16[256,1280]{1,0:T(8,128)(2,1)S(1)} %collective-permute-done.9, pred[]{:T(512)S(6)} %or.3), kind=kLoop, calls=%fused_computation | loop fusion | flops 327680 | bytes 1966081 | tf_op jit(solution)/shard_map/jit(_where)/select_n | solution.py:574
  63.0 0.6 collective-permute-done.10.refs_6_
  63.6 0.3 collective-permute-done.11.refs_1_
  63.9 1.0 collective-permute-start.15
  65.0 1.3 %collective-permute-start.14 = (bf16[256,768]{1,0:T(8,128)(2,1)S(1)}, bf16[256,768]{1,0:T(8,128)(2,1)S(1)}, u32[]{:S(2)}, u32[]{:S(2)}) collective-permute-start(bf16[256,768]{1,0:T(8,128)(2,1)S(1)} %slice.6), channel_id=1, source_target_pairs={{0,2},{1,3},{2,0},{3,1},{4,6},{5,7},{6,4},{7,5},{8,10},{9,11},{10,... | collective-permute-start | bytes 1179656 | tf_op jit(solution)/shard_map/ppermute | solution.py:578
  66.3 0.4 collective-permute-done.15.refs_8_
  66.7 3.1 %early_slots.3 = (f32[512,1280]{1,0:T(8,128)S(1)}, bf16[512,1024]{1,0:T(8,128)(2,1)S(1)}) custom-call(bf16[256,8192]{1,0:T(8,128)(2,1)S(1)} %bitcast.13, bf16[256,1536]{1,0:T(8,128)(2,1)S(1)} %collective-permute-done.7.refs_1_.refs_0_, bf16[256,1280]{1,0:T(8,128)(2,1)S(1)} %collective-permute-done.11.refs_1_, f32[256,128]{1,0:T(8,128)S(1)} %get-tuple-element.62.refs_2_, ...), custom_call_target="tpu_custom_call" | custom-call | flops 1342177280 | bytes 7340032 | tf_op jit(solution)/shard_map/early_slots/pallas_call | solution.py:332
  69.8 5.4 %collective-permute-done.14.refs_1_ = bf16[256,768]{1,0:T(8,128)(2,1)S(1)} collective-permute-done((bf16[256,768]{1,0:T(8,128)(2,1)S(1)}, bf16[256,768]{1,0:T(8,128)(2,1)S(1)}, u32[]{:S(2)}, u32[]{:S(2)}) %collective-permute-start.14) | collective-permute-done | bytes 393248 | tf_op jit(solution)/shard_map/ppermute | solution.py:578
  75.2 1.4 %collective-permute-start.17 = (bf16[256,768]{1,0:T(8,128)(2,1)S(1)}, bf16[256,768]{1,0:T(8,128)(2,1)S(1)}, u32[]{:S(2)}, u32[]{:S(2)}) collective-permute-start(bf16[256,768]{1,0:T(8,128)(2,1)S(1)} %collective-permute-done.14.refs_1_), channel_id=1, source_target_pairs={{0,1},{1,0},{2,3},{3,2},{4,5},{5,4},{6,7},{7,6},{8,9},{9,8},{10,11... | collective-permute-start | bytes 1179656 | tf_op jit(solution)/shard_map/ppermute | solution.py:598
  76.6 1.3 %collective-permute-start.19 = (bf16[256,512]{1,0:T(8,128)(2,1)S(1)}, bf16[256,512]{1,0:T(8,128)(2,1)S(1)}, u32[]{:S(2)}, u32[]{:S(2)}) collective-permute-start(bf16[256,512]{1,0:T(8,128)(2,1)S(1)} %slice.7), channel_id=1, source_target_pairs={{0,2},{1,3},{2,0},{3,1},{4,6},{5,7},{6,4},{7,5},{8,10},{9,11},{10,... | collective-permute-start | bytes 786440 | tf_op jit(solution)/shard_map/ppermute | solution.py:597
  77.9 1.5 %late_slot.2 = (f32[256,256]{1,0:T(8,128)S(1)}, f32[256,512]{1,0:T(8,128)S(1)}, bf16[256,256]{1,0:T(8,128)(2,1)S(1)}, bf16[256,512]{1,0:T(8,128)(2,1)S(1)}) custom-call(f32[512,1280]{1,0:T(8,128)S(1)} %get-tuple-element.74.before, bf16[512,1024]{1,0:T(8,128)(2,1)S(1)} %get-tuple-element.75.last_rows, bf16[256,1280]{1,0:T(8,128)(2,1)S(1)} %broadcast_select_fusion.refs_0_, ...), custom_call_target="tpu_custom_call" | custom-call | flops 805306368 | bytes 1572864 | tf_op jit(solution)/shard_map/late_slot/pallas_call | solution.py:375
  79.4 1.1 %collective-permute-start.18 = (bf16[256,256]{1,0:T(8,128)(2,1)S(1)}, bf16[256,256]{1,0:T(8,128)(2,1)S(1)}, u32[]{:S(2)}, u32[]{:S(2)}) collective-permute-start(bf16[256,256]{1,0:T(8,128)(2,1)S(1)} %get-tuple-element.79), channel_id=1, source_target_pairs={{0,4},{4,0},{1,5},{5,1},{2,6},{6,2},{3,7},{7,3},{8,12},{12,8},{9,1... | collective-permute-start | bytes 393224 | tf_op jit(solution)/shard_map/ppermute | solution.py:607
  80.6 4.1 %collective-permute-done.19.refs_1_ = bf16[256,512]{1,0:T(8,128)(2,1)S(1)} collective-permute-done((bf16[256,512]{1,0:T(8,128)(2,1)S(1)}, bf16[256,512]{1,0:T(8,128)(2,1)S(1)}, u32[]{:S(2)}, u32[]{:S(2)}) %collective-permute-start.19) | collective-permute-done | bytes 262176 | tf_op jit(solution)/shard_map/ppermute | solution.py:597
  84.6 0.8 collective-permute-start.20
  85.4 1.1 %collective-permute-start.25 = (bf16[256,512]{1,0:T(8,128)(2,1)S(1)}, bf16[256,512]{1,0:T(8,128)(2,1)S(1)}, u32[]{:S(2)}, u32[]{:S(2)}) collective-permute-start(bf16[256,512]{1,0:T(8,128)(2,1)S(1)} %get-tuple-element.90), channel_id=1, source_target_pairs={{0,4},{4,0},{1,5},{5,1},{2,6},{6,2},{3,7},{7,3},{8,12},{12,8},{9,1... | collective-permute-start | bytes 786440 | tf_op jit(solution)/shard_map/ppermute | solution.py:608
  86.6 1.3 %collective-permute-start.23 = (bf16[256,256]{1,0:T(8,128)(2,1)S(1)}, bf16[256,256]{1,0:T(8,128)(2,1)S(1)}, u32[]{:S(2)}, u32[]{:S(2)}) collective-permute-start(bf16[256,256]{1,0:T(8,128)(2,1)S(1)} %key_value.1.refs_7_.refs_5_), channel_id=1, source_target_pairs={{0,2},{1,3},{4,6},{5,7},{8,10},{9,11},{12,14},{13,15},{16,18},{17,... | collective-permute-start | bytes 393224 | tf_op jit(solution)/shard_map/ppermute | solution.py:629
  87.9 0.8 late_slot.3
  88.8 0.5 collective-permute-start.21
  89.2 0.6 collective-permute-start.22
  89.8 3.5 %collective-permute-done.23.refs_9_.refs_7_ = bf16[256,256]{1,0:T(8,128)(2,1)S(1)} collective-permute-done((bf16[256,256]{1,0:T(8,128)(2,1)S(1)}, bf16[256,256]{1,0:T(8,128)(2,1)S(1)}, u32[]{:S(2)}, u32[]{:S(2)}) %collective-permute-start.23) | collective-permute-done | bytes 131104 | tf_op jit(solution)/shard_map/ppermute | solution.py:629
  93.3 3.0 %collective-permute-start.24 = (bf16[256,256]{1,0:T(8,128)(2,1)S(1)}, bf16[256,256]{1,0:T(8,128)(2,1)S(1)}, u32[]{:S(2)}, u32[]{:S(2)}) collective-permute-start(bf16[256,256]{1,0:T(8,128)(2,1)S(1)} %collective-permute-done.23.refs_9_.refs_7_), channel_id=1, source_target_pairs={{2,3},{3,2},{6,7},{7,6},{10,11},{11,10},{14,15},{15,14},{18,19},{1... | collective-permute-start | bytes 393224 | tf_op jit(solution)/shard_map/ppermute | solution.py:631
  96.3 0.9 collective-permute-done.24.refs_10_.refs_8_
  97.3 2.5 %attention.2.refs_9_ = bf16[256,512]{1,0:T(8,128)(2,1)S(1)} custom-call(f32[256,256]{1,0:T(8,128)S(1)} %get-tuple-element.86.sums.refs_0_, f32[256,512]{1,0:T(8,128)S(1)} %get-tuple-element.89.refs_1_, bf16[256,256]{1,0:T(8,128)(2,1)S(1)} %collective-permute-done.18.back.refs_2_, bf16[256,512]{1,0:T(8,128)(2,1)S(1)} %collective-permute-done.25.refs_3_, ...), custom_call_target="tpu_custom_call" | custom-call | flops 536870912 | bytes 1048576 | tf_op jit(solution)/shard_map/attention/pallas_call | solution.py:489
  99.8 3.0 %attention.3 = bf16[256,1024]{1,0:T(8,128)(2,1)} custom-call(f32[256,512]{1,0:T(8,128)S(1)} %get-tuple-element.81.refs_0_, bf16[256,512]{1,0:T(8,128)(2,1)S(1)} %collective-permute-done.21.refs_1_, f32[1,1024]{1,0:T(1,128)S(1)} %bitcast.15, f32[256,128]{1,0:T(8,128)S(1)} %get-tuple-element.84.cosine.refs_5_.refs_3_, ...), custom_call_target="tpu_custom_call" | custom-call | flops 536870912 | bytes 1048576 | tf_op jit(solution)/shard_map/attention/pallas_call | solution.py:489
  (47 shorter events, 1.6 us)
Async XLA Ops:
  2.4 8.1 %copy-start.7 = (bf16[8192]{0:T(1024)(128)(2,1)S(1)}, bf16[8192]{0:T(1024)(128)(2,1)}, u32[]{:S(2)}) copy-start(bf16[8192]{0:T(1024)(128)(2,1)} %param.9) | copy-start | bytes 49156
  2.4 8.1 %copy-start.8 = (bf16[1024]{0:T(1024)(128)(2,1)S(1)}, bf16[1024]{0:T(1024)(128)(2,1)}, u32[]{:S(2)}) copy-start(bf16[1024]{0:T(1024)(128)(2,1)} %param.13) | copy-start | bytes 6148
  2.4 8.2 %copy-start.9 = (bf16[128]{0:T(256)(128)(2,1)S(1)}, bf16[128]{0:T(256)(128)(2,1)}, u32[]{:S(2)}) copy-start(bf16[128]{0:T(256)(128)(2,1)} %param.15) | copy-start | bytes 772
  2.5 8.2 %copy-start.10 = (bf16[128]{0:T(256)(128)(2,1)S(1)}, bf16[128]{0:T(256)(128)(2,1)}, u32[]{:S(2)}) copy-start(bf16[128]{0:T(256)(128)(2,1)} %param.14) | copy-start | bytes 772
  2.5 16.0 %collective-permute-start = (bf16[256,1280]{1,0:T(8,128)(2,1)}, bf16[256,1280]{1,0:T(8,128)(2,1)S(1)}, u32[]{:S(2)}, u32[]{:S(2)}) collective-permute-start(bf16[256,1280]{1,0:T(8,128)(2,1)} %get-tuple-element.48), channel_id=1, source_target_pairs={{0,8},{8,0},{16,24},{24,16},{1,9},{9,1},{17,25},{25,17},{2,10},{10... | collective-permute-start | bytes 1966088 | tf_op jit(solution)/shard_map/ppermute | solution.py:530
  2.7 18.8 %collective-permute-start.1 = (bf16[256,1280]{1,0:T(8,128)(2,1)}, bf16[256,1280]{1,0:T(8,128)(2,1)}, u32[]{:S(2)}, u32[]{:S(2)}) collective-permute-start(bf16[256,1280]{1,0:T(8,128)(2,1)} %get-tuple-element.48), channel_id=1, source_target_pairs={{8,16},{16,8},{9,17},{17,9},{10,18},{18,10},{11,19},{19,11},{12,20... | collective-permute-start | bytes 1966088 | tf_op jit(solution)/shard_map/ppermute | solution.py:531
  7.0 15.4 %collective-permute-start.2 = (bf16[256,1280]{1,0:T(8,128)(2,1)}, bf16[256,1280]{1,0:T(8,128)(2,1)}, u32[]{:S(2)}, u32[]{:S(2)}) collective-permute-start(bf16[256,1280]{1,0:T(8,128)(2,1)} %get-tuple-element.49), channel_id=1, source_target_pairs={{0,4},{4,0},{1,5},{5,1},{2,6},{6,2},{3,7},{7,3},{8,12},{12,8},{9,1... | collective-permute-start | bytes 1966088 | tf_op jit(solution)/shard_map/ppermute | solution.py:532
  8.3 40.5 %copy-start.2 = (bf16[1024,1024]{1,0:T(8,128)(2,1)S(1)}, bf16[1024,1024]{1,0:T(8,128)(2,1)}, u32[]{:S(2)}) copy-start(bf16[1024,1024]{1,0:T(8,128)(2,1)} %refs_7_.1) | copy-start | bytes 6291460
  18.4 4.0 %copy-start.5 = (bf16[256,1280]{1,0:T(8,128)(2,1)}, bf16[256,1280]{1,0:T(8,128)(2,1)S(1)}, u32[]{:S(2)}) copy-start(bf16[256,1280]{1,0:T(8,128)(2,1)S(1)} %collective-permute-done.refs_8_) | copy-start | bytes 1966084
  22.4 13.7 %collective-permute-start.5 = (bf16[256,1280]{1,0:T(8,128)(2,1)}, bf16[256,1280]{1,0:T(8,128)(2,1)}, u32[]{:S(2)}, u32[]{:S(2)}) collective-permute-start(bf16[256,1280]{1,0:T(8,128)(2,1)} %collective-permute-done.1), channel_id=1, source_target_pairs={{8,0},{16,24},{9,1},{17,25},{10,2},{18,26},{11,3},{19,27},{12,4},{... | collective-permute-start | bytes 1966088 | tf_op jit(solution)/shard_map/ppermute | solution.py:547
  24.6 17.7 %collective-permute-start.7 = (bf16[256,1536]{1,0:T(8,128)(2,1)}, bf16[256,1536]{1,0:T(8,128)(2,1)S(1)}, u32[]{:S(2)}, u32[]{:S(2)}) collective-permute-start(bf16[256,1536]{1,0:T(8,128)(2,1)} %pack.3), channel_id=1, source_target_pairs={{0,4},{4,0},{1,5},{5,1},{2,6},{6,2},{3,7},{7,3},{8,12},{12,8},{9,1... | collective-permute-start | bytes 2359304 | tf_op jit(solution)/shard_map/ppermute | solution.py:549
  25.8 16.0 %collective-permute-start.3 = (bf16[256,1280]{1,0:T(8,128)(2,1)}, bf16[256,1280]{1,0:T(8,128)(2,1)}, u32[]{:S(2)}, u32[]{:S(2)}) collective-permute-start(bf16[256,1280]{1,0:T(8,128)(2,1)} %copy-done.5), channel_id=1, source_target_pairs={{8,16},{16,8},{9,17},{17,9},{10,18},{18,10},{11,19},{19,11},{12,20... | collective-permute-start | bytes 1966088 | tf_op jit(solution)/shard_map/ppermute | solution.py:546
  28.3 13.9 %collective-permute-start.6 = (bf16[256,1280]{1,0:T(8,128)(2,1)}, bf16[256,1280]{1,0:T(8,128)(2,1)}, u32[]{:S(2)}, u32[]{:S(2)}) collective-permute-start(bf16[256,1280]{1,0:T(8,128)(2,1)} %copy-done.5), channel_id=1, source_target_pairs={{0,2},{1,3},{2,0},{3,1},{4,6},{5,7},{6,4},{7,5},{8,10},{9,11},{10,... | collective-permute-start | bytes 1966088 | tf_op jit(solution)/shard_map/ppermute | solution.py:548
  28.6 13.6 %collective-permute-start.8 = (bf16[256,1280]{1,0:T(8,128)(2,1)}, bf16[256,1280]{1,0:T(8,128)(2,1)}, u32[]{:S(2)}, u32[]{:S(2)}) collective-permute-start(bf16[256,1280]{1,0:T(8,128)(2,1)} %copy-done.5), channel_id=1, source_target_pairs={{0,1},{1,0},{2,3},{3,2},{4,5},{5,4},{6,7},{7,6},{8,9},{9,8},{10,11... | collective-permute-start | bytes 1966088 | tf_op jit(solution)/shard_map/ppermute | solution.py:550
  31.6 2.2 %copy-start = (bf16[1,256,8192]{2,1,0:T(8,128)(2,1)S(1)}, bf16[1,256,8192]{2,1,0:T(8,128)(2,1)}, u32[]{:S(2)}) copy-start(bf16[1,256,8192]{2,1,0:T(8,128)(2,1)} %param.8) | copy-start | bytes 12582916
  33.8 15.1 %copy-start.1 = (bf16[1,256,8192]{2,1,0:T(8,128)(2,1)S(1)}, bf16[1,256,8192]{2,1,0:T(8,128)(2,1)}, u32[]{:S(2)}) copy-start(bf16[1,256,8192]{2,1,0:T(8,128)(2,1)} %param.8) | copy-start | bytes 12582916
  33.8 15.1 %copy-start.3 = (bf16[1024,128]{1,0:T(8,128)(2,1)S(1)}, bf16[1024,128]{1,0:T(8,128)(2,1)}, u32[]{:S(2)}) copy-start(bf16[1024,128]{1,0:T(8,128)(2,1)} %refs_5_.1) | copy-start | bytes 786436
  33.8 15.1 %copy-start.4 = (bf16[1024,128]{1,0:T(8,128)(2,1)S(1)}, bf16[1024,128]{1,0:T(8,128)(2,1)}, u32[]{:S(2)}) copy-start(bf16[1024,128]{1,0:T(8,128)(2,1)} %refs_6_.1) | copy-start | bytes 786436
  33.8 15.1 %copy-start.6 = (bf16[256,1280]{1,0:T(8,128)(2,1)S(1)}, bf16[256,1280]{1,0:T(8,128)(2,1)}, u32[]{:S(2)}) copy-start(bf16[256,1280]{1,0:T(8,128)(2,1)} %copy-done.5) | copy-start | bytes 1966084
  36.1 5.6 %collective-permute-start.4 = (f32[1,256]{1,0:T(1,128)S(1)}, f32[1,256]{1,0:T(1,128)S(1)}, u32[]{:S(2)}, u32[]{:S(2)}) collective-permute-start(f32[1,256]{1,0:T(1,128)S(1)} %get-tuple-element.52), channel_id=1, source_target_pairs={{0,4},{4,0},{1,5},{5,1},{2,6},{6,2},{3,7},{7,3},{8,12},{12,8},{9,1... | collective-permute-start | bytes 3080 | tf_op jit(solution)/shard_map/ppermute | solution.py:552
  42.2 6.6 %collective-permute-start.13 = (bf16[256,1280]{1,0:T(8,128)(2,1)}, bf16[256,1280]{1,0:T(8,128)(2,1)S(1)}, u32[]{:S(2)}, u32[]{:S(2)}) collective-permute-start(bf16[256,1280]{1,0:T(8,128)(2,1)} %collective-permute-done.6.refs_9_), channel_id=1, source_target_pairs={{0,1},{1,0},{2,3},{3,2},{4,5},{5,4},{6,7},{7,6},{8,9},{9,8},{10,11... | collective-permute-start | bytes 1966088 | tf_op jit(solution)/shard_map/ppermute | solution.py:560
  45.9 15.9 %collective-permute-start.9 = (bf16[256,1280]{1,0:T(8,128)(2,1)}, bf16[256,1280]{1,0:T(8,128)(2,1)S(1)}, u32[]{:S(2)}, u32[]{:S(2)}) collective-permute-start(bf16[256,1280]{1,0:T(8,128)(2,1)} %collective-permute-done.3), channel_id=1, source_target_pairs={{8,0},{16,24},{9,1},{17,25},{10,2},{18,26},{11,3},{19,27},{12,4},{... | collective-permute-start | bytes 1966088 | tf_op jit(solution)/shard_map/ppermute | solution.py:557
  47.2 16.4 %collective-permute-start.10 = (bf16[256,1280]{1,0:T(8,128)(2,1)S(1)}, bf16[256,1280]{1,0:T(8,128)(2,1)S(1)}, u32[]{:S(2)}, u32[]{:S(2)}) collective-permute-start(bf16[256,1280]{1,0:T(8,128)(2,1)S(1)} %broadcast_select_fusion.1.refs_5_), channel_id=1, source_target_pairs={{0,2},{1,3},{2,0},{3,1},{4,6},{5,7},{6,4},{7,5},{8,10},{9,11},{10,... | collective-permute-start | bytes 1966088 | tf_op jit(solution)/shard_map/ppermute | solution.py:558
  47.5 16.4 %collective-permute-start.12 = (bf16[256,1280]{1,0:T(8,128)(2,1)S(1)}, bf16[256,1280]{1,0:T(8,128)(2,1)S(1)}, u32[]{:S(2)}, u32[]{:S(2)}) collective-permute-start(bf16[256,1280]{1,0:T(8,128)(2,1)S(1)} %broadcast_select_fusion.1.refs_5_), channel_id=1, source_target_pairs={{0,1},{1,0},{2,3},{3,2},{4,5},{5,4},{6,7},{7,6},{8,9},{9,8},{10,11... | collective-permute-start | bytes 1966088 | tf_op jit(solution)/shard_map/ppermute | solution.py:561
  47.8 16.1 %collective-permute-start.11 = (bf16[256,1280]{1,0:T(8,128)(2,1)S(1)}, bf16[256,1280]{1,0:T(8,128)(2,1)S(1)}, u32[]{:S(2)}, u32[]{:S(2)}) collective-permute-start(bf16[256,1280]{1,0:T(8,128)(2,1)S(1)} %get-tuple-element.59), channel_id=1, source_target_pairs={{0,4},{4,0},{1,5},{5,1},{2,6},{6,2},{3,7},{7,3},{8,12},{12,8},{9,1... | collective-permute-start | bytes 1966088 | tf_op jit(solution)/shard_map/ppermute | solution.py:559
  63.9 2.7 %collective-permute-start.15 = (bf16[256,1280]{1,0:T(8,128)(2,1)S(1)}, bf16[256,1280]{1,0:T(8,128)(2,1)S(1)}, u32[]{:S(2)}, u32[]{:S(2)}) collective-permute-start(bf16[256,1280]{1,0:T(8,128)(2,1)S(1)} %collective-permute-done.10.refs_6_), channel_id=1, source_target_pairs={{0,1},{1,0},{2,3},{3,2},{4,5},{5,4},{6,7},{7,6},{8,9},{9,8},{10,11... | collective-permute-start | bytes 1966088 | tf_op jit(solution)/shard_map/ppermute | solution.py:579
  65.0 10.3 %collective-permute-start.16 = (bf16[256,1280]{1,0:T(8,128)(2,1)S(1)}, bf16[256,1280]{1,0:T(8,128)(2,1)S(1)}, u32[]{:S(2)}, u32[]{:S(2)}) collective-permute-start(bf16[256,1280]{1,0:T(8,128)(2,1)S(1)} %broadcast_select_fusion.refs_0_), channel_id=1, source_target_pairs={{0,1},{1,0},{2,3},{3,2},{4,5},{5,4},{6,7},{7,6},{8,9},{9,8},{10,11... | collective-permute-start | bytes 1966088 | tf_op jit(solution)/shard_map/ppermute | solution.py:580
  65.0 10.2 %collective-permute-start.14 = (bf16[256,768]{1,0:T(8,128)(2,1)S(1)}, bf16[256,768]{1,0:T(8,128)(2,1)S(1)}, u32[]{:S(2)}, u32[]{:S(2)}) collective-permute-start(bf16[256,768]{1,0:T(8,128)(2,1)S(1)} %slice.6), channel_id=1, source_target_pairs={{0,2},{1,3},{2,0},{3,1},{4,6},{5,7},{6,4},{7,5},{8,10},{9,11},{10,... | collective-permute-start | bytes 1179656 | tf_op jit(solution)/shard_map/ppermute | solution.py:578
  75.2 2.7 %collective-permute-start.17 = (bf16[256,768]{1,0:T(8,128)(2,1)S(1)}, bf16[256,768]{1,0:T(8,128)(2,1)S(1)}, u32[]{:S(2)}, u32[]{:S(2)}) collective-permute-start(bf16[256,768]{1,0:T(8,128)(2,1)S(1)} %collective-permute-done.14.refs_1_), channel_id=1, source_target_pairs={{0,1},{1,0},{2,3},{3,2},{4,5},{5,4},{6,7},{7,6},{8,9},{9,8},{10,11... | collective-permute-start | bytes 1179656 | tf_op jit(solution)/shard_map/ppermute | solution.py:598
  76.6 8.0 %collective-permute-start.19 = (bf16[256,512]{1,0:T(8,128)(2,1)S(1)}, bf16[256,512]{1,0:T(8,128)(2,1)S(1)}, u32[]{:S(2)}, u32[]{:S(2)}) collective-permute-start(bf16[256,512]{1,0:T(8,128)(2,1)S(1)} %slice.7), channel_id=1, source_target_pairs={{0,2},{1,3},{2,0},{3,1},{4,6},{5,7},{6,4},{7,5},{8,10},{9,11},{10,... | collective-permute-start | bytes 786440 | tf_op jit(solution)/shard_map/ppermute | solution.py:597
  79.4 5.2 %collective-permute-start.18 = (bf16[256,256]{1,0:T(8,128)(2,1)S(1)}, bf16[256,256]{1,0:T(8,128)(2,1)S(1)}, u32[]{:S(2)}, u32[]{:S(2)}) collective-permute-start(bf16[256,256]{1,0:T(8,128)(2,1)S(1)} %get-tuple-element.79), channel_id=1, source_target_pairs={{0,4},{4,0},{1,5},{5,1},{2,6},{6,2},{3,7},{7,3},{8,12},{12,8},{9,1... | collective-permute-start | bytes 393224 | tf_op jit(solution)/shard_map/ppermute | solution.py:607
  84.6 3.3 %collective-permute-start.20 = (bf16[256,512]{1,0:T(8,128)(2,1)S(1)}, bf16[256,512]{1,0:T(8,128)(2,1)S(1)}, u32[]{:S(2)}, u32[]{:S(2)}) collective-permute-start(bf16[256,512]{1,0:T(8,128)(2,1)S(1)} %collective-permute-done.19.refs_1_), channel_id=1, source_target_pairs={{0,1},{1,0},{2,3},{3,2},{4,5},{5,4},{6,7},{7,6},{8,9},{9,8},{10,11... | collective-permute-start | bytes 786440 | tf_op jit(solution)/shard_map/ppermute | solution.py:610
  85.4 10.9 %collective-permute-start.25 = (bf16[256,512]{1,0:T(8,128)(2,1)S(1)}, bf16[256,512]{1,0:T(8,128)(2,1)S(1)}, u32[]{:S(2)}, u32[]{:S(2)}) collective-permute-start(bf16[256,512]{1,0:T(8,128)(2,1)S(1)} %get-tuple-element.90), channel_id=1, source_target_pairs={{0,4},{4,0},{1,5},{5,1},{2,6},{6,2},{3,7},{7,3},{8,12},{12,8},{9,1... | collective-permute-start | bytes 786440 | tf_op jit(solution)/shard_map/ppermute | solution.py:608
  86.6 6.7 %collective-permute-start.23 = (bf16[256,256]{1,0:T(8,128)(2,1)S(1)}, bf16[256,256]{1,0:T(8,128)(2,1)S(1)}, u32[]{:S(2)}, u32[]{:S(2)}) collective-permute-start(bf16[256,256]{1,0:T(8,128)(2,1)S(1)} %key_value.1.refs_7_.refs_5_), channel_id=1, source_target_pairs={{0,2},{1,3},{4,6},{5,7},{8,10},{9,11},{12,14},{13,15},{16,18},{17,... | collective-permute-start | bytes 393224 | tf_op jit(solution)/shard_map/ppermute | solution.py:629
  88.8 11.0 %collective-permute-start.21 = (bf16[256,512]{1,0:T(8,128)(2,1)S(1)}, bf16[256,512]{1,0:T(8,128)(2,1)S(1)}, u32[]{:S(2)}, u32[]{:S(2)}) collective-permute-start(bf16[256,512]{1,0:T(8,128)(2,1)S(1)} %get-tuple-element.82), channel_id=1, source_target_pairs={{0,4},{4,0},{1,5},{5,1},{2,6},{6,2},{3,7},{7,3},{8,12},{12,8},{9,1... | collective-permute-start | bytes 786440 | tf_op jit(solution)/shard_map/ppermute | solution.py:618
  89.2 7.1 %collective-permute-start.22 = (bf16[256,256]{1,0:T(8,128)(2,1)S(1)}, bf16[256,256]{1,0:T(8,128)(2,1)S(1)}, u32[]{:S(2)}, u32[]{:S(2)}) collective-permute-start(bf16[256,256]{1,0:T(8,128)(2,1)S(1)} %key_value.1.refs_7_.refs_5_), channel_id=1, source_target_pairs={{0,1},{1,0},{2,3},{3,2},{4,5},{5,4},{6,7},{7,6},{8,9},{9,8},{10,11... | collective-permute-start | bytes 393224 | tf_op jit(solution)/shard_map/ppermute | solution.py:630
  93.3 4.0 %collective-permute-start.24 = (bf16[256,256]{1,0:T(8,128)(2,1)S(1)}, bf16[256,256]{1,0:T(8,128)(2,1)S(1)}, u32[]{:S(2)}, u32[]{:S(2)}) collective-permute-start(bf16[256,256]{1,0:T(8,128)(2,1)S(1)} %collective-permute-done.23.refs_9_.refs_7_), channel_id=1, source_target_pairs={{2,3},{3,2},{6,7},{7,6},{10,11},{11,10},{14,15},{15,14},{18,19},{1... | collective-permute-start | bytes 393224 | tf_op jit(solution)/shard_map/ppermute | solution.py:631
